TPU v7x, 512 devices: a whole 4x4x16 slice. The times are simulated.
512 devices in a mesh: gx: 4 (over x), gy: 8 (over z_hi, core), gz: 16 (over y, z_lo).
Axes of the slice: x: 4, y: 4, z: 16 (z_hi: 4, z_lo: 4; z = z_hi * 4 + z_lo), core: 2. Of those that a mesh axis runs over, the one named last changes fastest.
Arguments:
- positions: float32 [3, 8, 64, 32, 128], P(None, 'gx', 'gy', 'gz'), may hold values from 0 to 11
- velocities: float32 [3, 8, 64, 32, 128], P(None, 'gx', 'gy', 'gz'), may hold values from -6 to 6
- counts: int32 [8, 64, 32], P('gx', 'gy', 'gz'), may hold values from 64 to 128
- grid_cells: int32 [8, 64, 32, 128], P('gx', 'gy', 'gz'), may hold values from 0 to 7
- electron_temp: float32 [16, 128, 64], P('gx', ('gy', 'gz')), may hold values from 0.5 to 8
Outputs:
- velocity_out: float32 [3, 8, 64, 32, 128], P(None, 'gx', 'gy', 'gz')
- electron_out: float32 [16, 128, 64], P('gx', ('gy', 'gz'))
Inputs may be any that keep to these rules, and one draw needn't show every extreme that they name: `counts`: slot k of a cell holds an atom exactly when k is below the cell's count; other slots' positions, velocities and grid cells are ignored. `grid_cells`: grid cells are numbered within the atom cell's block of 2 x 2 x 2 with z fastest.
All inputs are finite; a program needn't handle non-finite values.
Results may differ from a plain program's by a relative error of at most 0.0003.
Values sent between devices are 32-bit elements; how exact they have to be, the bound alone decides.
No kernel may reach another device: no remote copies, remote signals or barrier semaphores. Data moves between devices by JAX's collectives and lax.ppermute only.
A program may use at most 64 MiB of HBM per device.

v0:
```python
import jax
import jax.numpy as jnp
from jax import lax
from jax.sharding import PartitionSpec as P

SUBX = 2
SUBY = 2
SUBZ = 2
SUBSTEPS = 4


CELL_EDGE = 11.0
CUT_SQUARED = 30.25
EMBED_SCALE = 1.0
PAIR_SCALE = 0.5
TIME_STEP = 0.2
ATOM_MASS = 1.0
COUPLING = 0.02
LATTICE_SCALE = 1.0
SPREAD = 0.15
PHONON_RATE = 0.05
FAR_AWAY = 1000.0
FAR_STEP = 100.0
NEIGHBOUR_SHIFTS = [
    (shift_x, shift_y, shift_z)
    for shift_x in (-1, 0, 1)
    for shift_y in (-1, 0, 1)
    for shift_z in (-1, 0, 1)
]


def extended_2(value, sides, width):
    for axis, dim in sides:
        devices, length = (lax.axis_size(axis), value.shape[dim])
        up = [(i, (i + 1) % devices) for i in range(devices)]
        down = [(j, i) for i, j in up]
        last = lax.slice_in_dim(value, length - width, length, axis=dim)
        first = lax.slice_in_dim(value, 0, width, axis=dim)
        before = lax.ppermute(last, axis, up)
        after = lax.ppermute(first, axis, down)
        value = jnp.concatenate([before, value, after], axis=dim)
    return value


def park_atoms(positions, counts):
    capacity = positions.shape[-1]
    slot_index = lax.broadcasted_iota(jnp.int32, counts.shape + (capacity,), counts.ndim)
    occupied = slot_index < counts[..., None]
    parked = FAR_AWAY + FAR_STEP * slot_index.astype(jnp.float32)
    return (jnp.where(occupied[None], positions, parked[None]), occupied)


def separation(centre_atoms, neighbours, shift):
    deltas = [
        neighbours[axis_no][:, None, :]
        - centre_atoms[axis_no][:, :, None]
        + shift[axis_no] * CELL_EDGE
        for axis_no in range(3)
    ]
    squared = deltas[0] * deltas[0] + deltas[1] * deltas[1] + deltas[2] * deltas[2]
    reach = jnp.maximum(1.0 - squared / CUT_SQUARED, 0.0)
    return (deltas, reach)


def densities(source):
    width_x = source.shape[1] - 2
    width_y = source.shape[2] - 2
    height = source.shape[3] - 2
    capacity = source.shape[4]
    diagonal_mask = jnp.eye(capacity, dtype=bool)
    zero = jnp.zeros((), jnp.int32)

    def densities_column(carry, index):
        index_x = index // width_y
        index_y = index % width_y
        window = lax.dynamic_slice(
            source, (zero, index_x, index_y, zero, zero), (3, 3, 3, height + 2, capacity)
        )
        centre_atoms = window[:, 1, 1, 1 : height + 1]
        summed = jnp.zeros((height, capacity), jnp.float32)
        for shift in NEIGHBOUR_SHIFTS:
            neighbours = window[:, shift[0] + 1, shift[1] + 1, shift[2] + 1 : shift[2] + 1 + height]
            deltas, reach = separation(centre_atoms, neighbours, shift)
            weight = reach * reach * reach
            if shift == (0, 0, 0):
                weight = jnp.where(diagonal_mask, 0.0, weight)
            summed = summed + jnp.sum(weight, axis=-1)
        return (carry, summed)

    carry, stacked = lax.scan(
        densities_column, zero, jnp.arange(width_x * width_y, dtype=jnp.int32)
    )
    return stacked.reshape(width_x, width_y, height, capacity)


def forces(source, slopes):
    width_x = source.shape[1] - 2
    width_y = source.shape[2] - 2
    height = source.shape[3] - 2
    capacity = source.shape[4]
    diagonal_mask = jnp.eye(capacity, dtype=bool)
    zero = jnp.zeros((), jnp.int32)

    def forces_column(carry, index):
        index_x = index // width_y
        index_y = index % width_y
        window = lax.dynamic_slice(
            source, (zero, index_x, index_y, zero, zero), (3, 3, 3, height + 2, capacity)
        )
        slope_window = lax.dynamic_slice(
            slopes, (index_x, index_y, zero, zero), (3, 3, height + 2, capacity)
        )
        centre_atoms = window[:, 1, 1, 1 : height + 1]
        centre_slope = slope_window[1, 1, 1 : height + 1]
        sums = [jnp.zeros((height, capacity), jnp.float32) for axis_no in range(3)]
        for shift in NEIGHBOUR_SHIFTS:
            neighbours = window[:, shift[0] + 1, shift[1] + 1, shift[2] + 1 : shift[2] + 1 + height]
            neighbour_slope = slope_window[
                shift[0] + 1, shift[1] + 1, shift[2] + 1 : shift[2] + 1 + height
            ]
            deltas, reach = separation(centre_atoms, neighbours, shift)
            coefficient = (
                2.0
                * reach
                * reach
                * (
                    (centre_slope[:, :, None] + neighbour_slope[:, None, :]) * (-3.0 / CUT_SQUARED)
                    - 3.0 * PAIR_SCALE / CUT_SQUARED
                )
            )
            if shift == (0, 0, 0):
                coefficient = jnp.where(diagonal_mask, 0.0, coefficient)
            sums = [
                sums[axis_no] + jnp.sum(coefficient * deltas[axis_no], axis=-1)
                for axis_no in range(3)
            ]
        return (carry, jnp.stack(sums))

    carry, stacked = lax.scan(forces_column, zero, jnp.arange(width_x * width_y, dtype=jnp.int32))
    return jnp.moveaxis(stacked.reshape(width_x, width_y, 3, height, capacity), 2, 0)


def embed_slope(density):
    return -0.5 * EMBED_SCALE / jnp.sqrt(density + 1.0)


def grid_index(grid_cells, span_y, span_z):
    cell_x = lax.broadcasted_iota(jnp.int32, grid_cells.shape, 0)
    cell_y = lax.broadcasted_iota(jnp.int32, grid_cells.shape, 1)
    cell_z = lax.broadcasted_iota(jnp.int32, grid_cells.shape, 2)
    fine_x = cell_x * SUBX + grid_cells // (SUBY * SUBZ)
    fine_y = cell_y * SUBY + grid_cells // SUBZ % SUBY
    fine_z = cell_z * SUBZ + grid_cells % SUBZ
    return (fine_x * span_y + fine_y) * span_z + fine_z


def diffuse(extended, lattice):
    centre = extended[1:-1, 1:-1]
    beside = extended[2:, 1:-1] + extended[:-2, 1:-1] + extended[1:-1, 2:] + extended[1:-1, :-2]
    beside = beside + jnp.roll(centre, 1, 2) + jnp.roll(centre, -1, 2)
    return centre + SPREAD * (beside - 6.0 * centre) - PHONON_RATE * (centre - lattice)


def per_device(positions, velocities, counts, grid_cells, electron_temp):
    parked, occupied = park_atoms(positions, counts)
    source = extended_2(parked, (("gx", 1), ("gy", 2), ("gz", 3)), 1)
    density = densities(source)
    slopes = extended_2(embed_slope(density), (("gx", 0), ("gy", 1), ("gz", 2)), 1)
    force_field = forces(source, slopes)
    kinetic = jnp.where(occupied, 0.5 * ATOM_MASS * jnp.sum(velocities * velocities, axis=0), 0.0)
    cells_x, cells_y, cells_z = counts.shape
    span_x = SUBX * cells_x
    span_y = SUBY * cells_y
    span_z = SUBZ * cells_z
    flat_index = grid_index(grid_cells, span_y, span_z)
    block = jax.ops.segment_sum(
        kinetic.reshape(-1), flat_index.reshape(-1), num_segments=span_x * span_y * span_z
    )
    block = block.reshape(span_x, span_y, span_z)
    zero = jnp.zeros((), jnp.int32)
    layers = lax.axis_size("gz")
    column_sum = jnp.zeros((span_x, span_y, span_z * layers), jnp.float32)
    column_sum = lax.dynamic_update_slice(
        column_sum, block, (zero, zero, lax.axis_index("gz") * span_z)
    )
    energy = lax.psum_scatter(column_sum, "gz", scatter_dimension=1, tiled=True)
    lattice = LATTICE_SCALE * energy
    heat_field = electron_temp
    for substep in range(SUBSTEPS):
        extended = extended_2(heat_field, (("gx", 0), (("gy", "gz"), 1)), 1)
        heat_field = diffuse(extended, lattice)
    returned = lax.all_to_all(heat_field, "gz", split_axis=2, concat_axis=1, tiled=True)
    electron_here = jnp.take(returned.reshape(-1), flat_index)
    lattice_here = jnp.take((LATTICE_SCALE * block).reshape(-1), flat_index)
    moved = (
        velocities
        + TIME_STEP / ATOM_MASS * force_field
        + COUPLING * (electron_here - lattice_here)[None] * velocities
    )
    velocity_out = jnp.where(occupied[None], moved, 0.0)
    return (velocity_out, heat_field)


def solution(mesh):
    return jax.shard_map(
        per_device,
        mesh=mesh,
        in_specs=(
            P(None, "gx", "gy", "gz", None),
            P(None, "gx", "gy", "gz", None),
            P("gx", "gy", "gz"),
            P("gx", "gy", "gz", None),
            P("gx", ("gy", "gz"), None),
        ),
        out_specs=(P(None, "gx", "gy", "gz", None), P("gx", ("gy", "gz"), None)),
        check_vma=False,
    )
```

profile of v0, /device:TPU:1, one launch (start us, length us, event | category | flops | bytes accessed | tf_op | source)
XLA Modules:
  0.0 580.9 jit_solution(5095545565239913594)
XLA Ops:
  1.4 5.3 collective-permute-start.12
  6.7 1.9 collective-permute-start.13
  9.7 2.1 collective-permute-start
  11.8 4.4 collective-permute-start.1
  18.0 28.8 %scatter_custom_fusion = f32[256]{0:T(256)S(1)} fusion(s32[4096]{0:T(1024)S(1)} %bitcast.675, f32[4096]{0:T(1024)S(1)} %bitcast.678, f32[]{:T(128)} %constant.407.clone.1), kind=kCustom, calls=%fused_computation.896 | custom fusion | flops 4096 | bytes 1028 | tf_op jit(solution)/shard_map/scatter-add | solution.py:176
  47.2 69.6 %all-reduce = f32[4,16,64]{2,0,1:T(4,128)S(1)} all-reduce(f32[4,16,64]{2,0,1:T(4,128)S(1)} %dynamic_update_slice.18), channel_id=2, replica_groups=mesh['gx'=4,'gy'=8,'gz'=16] {'gz'}, use_global_device_ids=true, to_apply=%region_114.115.clone | all-reduce | flops 4096 | bytes 32768
  118.1 16.9 %collective-permute-start.14 = (f32[6,1,64]{2,0,1:T(8,128)S(1)}, f32[6,1,64]{2,0,1:T(8,128)S(1)}, u32[]{:S(2)}, u32[]{:S(2)}) collective-permute-start(f32[6,1,64]{2,0,1:T(8,128)S(1)} %pad_maximum_fusion.12), channel_id=1, source_target_pairs={{1,0},{2,1},{3,2},{4,3},{5,4},{6,5},{7,6},{8,7},{9,8},{10,9},{11,1... | collective-permute-start | bytes 4616 | tf_op jit(solution)/shard_map/ppermute | solution.py:40
  136.9 6.9 %collective-permute-done.15 = f32[6,1,64]{2,0,1:T(8,128)S(1)} collective-permute-done((f32[6,1,64]{2,0,1:T(8,128)S(1)}, f32[6,1,64]{2,0,1:T(8,128)S(1)}, u32[]{:S(2)}, u32[]{:S(2)}) %collective-permute-start.15) | collective-permute-done | bytes 1568 | tf_op jit(solution)/shard_map/ppermute | solution.py:39
  144.6 3.7 collective-permute-start.16
  150.3 3.5 collective-permute-done.17
  153.8 3.4 collective-permute-start.18
  159.1 6.9 %collective-permute-done.19 = f32[6,1,64]{2,0,1:T(8,128)S(1)} collective-permute-done((f32[6,1,64]{2,0,1:T(8,128)S(1)}, f32[6,1,64]{2,0,1:T(8,128)S(1)}, u32[]{:S(2)}, u32[]{:S(2)}) %collective-permute-start.19) | collective-permute-done | bytes 1568 | tf_op jit(solution)/shard_map/ppermute | solution.py:39
  168.7 3.4 collective-permute-start.21
  172.2 2.0 collective-permute-done.21
  174.2 3.1 collective-permute-start.22
  177.4 2.2 collective-permute-start.23
  179.6 6.6 %collective-permute-done.23 = f32[6,1,64]{2,0,1:T(8,128)S(1)} collective-permute-done((f32[6,1,64]{2,0,1:T(8,128)S(1)}, f32[6,1,64]{2,0,1:T(8,128)S(1)}, u32[]{:S(2)}, u32[]{:S(2)}) %collective-permute-start.23) | collective-permute-done | bytes 1568 | tf_op jit(solution)/shard_map/ppermute | solution.py:39
  189.0 3.4 collective-permute-start.25
  192.4 8.1 %collective-permute-start.2 = (f32[3,4,1,2,128]{4,3,2,1,0:T(2,128)S(1)}, f32[3,4,1,2,128]{4,3,2,1,0:T(2,128)S(1)}, u32[]{:S(2)}, u32[]{:S(2)}) collective-permute-start(f32[3,4,1,2,128]{4,3,2,1,0:T(2,128)S(1)} %get-tuple-element.607), channel_id=1, source_target_pairs={{0,16},{16,32},{32,48},{48,64},{64,80},{80,96},{96,112},{112,0},{1... | collective-permute-start | bytes 36872 | tf_op jit(solution)/shard_map/ppermute | solution.py:39
  202.5 2.0 collective-permute-start.26
  204.4 3.3 collective-permute-start.27
  211.5 7.3 %collective-permute-start.5 = (f32[3,4,10,1,128]{4,3,2,1,0:T(1,128)S(1)}, f32[3,4,10,1,128]{4,3,2,1,0:T(1,128)S(1)}, u32[]{:S(2)}, u32[]{:S(2)}) collective-permute-start(f32[3,4,10,1,128]{4,3,2,1,0:T(1,128)S(1)} %get-tuple-element.606), channel_id=1, source_target_pairs={{1,0},{2,1},{3,2},{4,3},{5,4},{6,5},{7,6},{8,7},{9,8},{10,9},{11,1... | collective-permute-start | bytes 184328 | tf_op jit(solution)/shard_map/ppermute | solution.py:40
  220.3 110.7 %while.27 = (s32[]{:T(128)}, f32[16,2,128]{2,1,0:T(2,128)S(1)}, s32[16]{0:T(128)S(1)}, f32[3,4,10,4,128]{4,3,2,1,0:T(4,128)S(1)}, s32[]{:T(128)}, /*index=5*/s32...) while((s32[]{:T(128)}, f32[16,2,128]{2,1,0:T(2,128)S(1)}, ...), condition=%wide.region_28.29_spmd.clone, body=%wide.region_0.28_spmd.clone.sunk | while | flops 14204705 | bytes 353788 | solution.py:90
  331.0 2.4 collective-permute-start.6
  333.4 4.1 collective-permute-start.7
  339.0 7.1 %all-to-all-start = ((f32[4,1,64]{0,1,2:T(1,128)}), f32[4,1,64]{0,1,2:T(1,128)S(1)}, u32[]{:S(2)}, u32[]{:S(2)}) async-start(f32[4,1,64]{0,1,2:T(1,128)} %copy.79), calls=%async_computation | async-start | bytes 65536 | tf_op jit(solution)/shard_map/all_to_all | solution.py:192
  346.1 8.7 %collective-permute-start.8 = (f32[4,1,2,128]{3,2,1,0:T(2,128)S(1)}, f32[4,1,2,128]{3,2,1,0:T(2,128)S(1)}, u32[]{:S(2)}, u32[]{:S(2)}) collective-permute-start(f32[4,1,2,128]{3,2,1,0:T(2,128)S(1)} %get-tuple-element.613), channel_id=1, source_target_pairs={{0,16},{16,32},{32,48},{48,64},{64,80},{80,96},{96,112},{112,0},{1... | collective-permute-start | bytes 12296 | tf_op jit(solution)/shard_map/ppermute | solution.py:39
  356.8 25.7 %gather_fusion.1 = f32[4096]{0:T(1024)S(1)} fusion(f32[256]{0:T(256)S(1)} %scatter_custom_fusion, s32[4096]{0:T(1024)S(1)} %broadcast_clamp_fusion), kind=kCustom, calls=%fused_computation.1.clone | custom fusion | bytes 49152 | tf_op jit(solution)/shard_map/jit(_take)/gather | solution.py:194
  382.7 25.7 %gather_fusion = f32[4096]{0:T(1024)S(1)} fusion(f32[256]{0:T(256)S(1)} %reshape.1737, s32[4096]{0:T(1024)S(1)} %broadcast_clamp_fusion), kind=kCustom, calls=%fused_computation.clone | custom fusion | bytes 49152 | tf_op jit(solution)/shard_map/jit(_take)/gather | solution.py:193
  408.5 3.5 collective-permute-start.10
  412.1 6.0 %collective-permute-start.11 = (f32[4,10,1,128]{3,2,1,0:T(1,128)S(1)}, f32[4,10,1,128]{3,2,1,0:T(1,128)S(1)}, u32[]{:S(2)}, u32[]{:S(2)}) collective-permute-start(f32[4,10,1,128]{3,2,1,0:T(1,128)S(1)} %get-tuple-element.612), channel_id=1, source_target_pairs={{1,0},{2,1},{3,2},{4,3},{5,4},{6,5},{7,6},{8,7},{9,8},{10,9},{11,1... | collective-permute-start | bytes 61448 | tf_op jit(solution)/shard_map/ppermute | solution.py:40
  418.9 161.3 %while.28 = (s32[]{:T(128)}, f32[16,3,2,128]{3,2,1,0:T(2,128)S(1)}, s32[16]{0:T(128)S(1)}, f32[3,4,10,4,128]{4,3,2,1,0:T(4,128)S(1)}, f32[4,10,4,128]{3,2,1,0:T(...) while((s32[]{:T(128)}, f32[16,3,2,128]{3,2,1,0:T(2,128)S(1)}, ...), condition=%wide.region_111.112_spmd.clone, body=%wide.region_29.111_spmd.clone.sunk | while | flops 22168352 | bytes 572964 | solution.py:139
  (535 shorter events, 213.6 us)
Async XLA Ops:
  1.4 7.3 %copy-start.4 = (s32[2,8,2]{1,2,0:T(2,128)S(1)}, s32[2,8,2]{1,2,0:T(2,128)}, u32[]{:S(2)}) copy-start(s32[2,8,2]{1,2,0:T(2,128)} %param.13) | copy-start | bytes 388
  1.4 116.7 %collective-permute-start.12 = (f32[1,1,64]{2,0,1:T(1,128)S(1)}, f32[1,1,64]{2,0,1:T(1,128)S(1)}, u32[]{:S(2)}, u32[]{:S(2)}) collective-permute-start(f32[1,1,64]{2,0,1:T(1,128)S(1)} %get-tuple-element.644), channel_id=1, source_target_pairs={{128,0},{256,128},{384,256},{0,384},{129,1},{257,129},{385,257},{1... | collective-permute-start | bytes 776 | tf_op jit(solution)/shard_map/ppermute | solution.py:40
  6.7 111.3 %collective-permute-start.13 = (f32[1,1,64]{2,0,1:T(1,128)S(1)}, f32[1,1,64]{2,0,1:T(1,128)S(1)}, u32[]{:S(2)}, u32[]{:S(2)}) collective-permute-start(f32[1,1,64]{2,0,1:T(1,128)S(1)} %get-tuple-element.643), channel_id=1, source_target_pairs={{0,128},{128,256},{256,384},{384,0},{1,129},{129,257},{257,385},{3... | collective-permute-start | bytes 776 | tf_op jit(solution)/shard_map/ppermute | solution.py:39
  9.7 7.4 %copy-start = (f32[3,2,8,2,128]{4,3,2,1,0:T(2,128)S(1)}, f32[3,2,8,2,128]{4,3,2,1,0:T(2,128)}, u32[]{:S(2)}) copy-start(f32[3,2,8,2,128]{4,3,2,1,0:T(2,128)} %param.12) | copy-start | bytes 147460
  9.7 182.6 %collective-permute-start = (f32[3,1,8,2,128]{4,3,2,1,0:T(2,128)S(1)}, f32[3,1,8,2,128]{4,3,2,1,0:T(2,128)S(1)}, u32[]{:S(2)}, u32[]{:S(2)}) collective-permute-start(f32[3,1,8,2,128]{4,3,2,1,0:T(2,128)S(1)} %get-tuple-element.609), channel_id=1, source_target_pairs={{0,128},{128,256},{256,384},{384,0},{1,129},{129,257},{257,385},{3... | collective-permute-start | bytes 73736 | tf_op jit(solution)/shard_map/ppermute | solution.py:39
  11.8 180.5 %collective-permute-start.1 = (f32[3,1,8,2,128]{4,3,2,1,0:T(2,128)S(1)}, f32[3,1,8,2,128]{4,3,2,1,0:T(2,128)S(1)}, u32[]{:S(2)}, u32[]{:S(2)}) collective-permute-start(f32[3,1,8,2,128]{4,3,2,1,0:T(2,128)S(1)} %get-tuple-element.610), channel_id=1, source_target_pairs={{128,0},{256,128},{384,256},{0,384},{129,1},{257,129},{385,257},{1... | collective-permute-start | bytes 73736 | tf_op jit(solution)/shard_map/ppermute | solution.py:40
  17.1 0.7 copy-start.2
  118.1 18.8 %collective-permute-start.14 = (f32[6,1,64]{2,0,1:T(8,128)S(1)}, f32[6,1,64]{2,0,1:T(8,128)S(1)}, u32[]{:S(2)}, u32[]{:S(2)}) collective-permute-start(f32[6,1,64]{2,0,1:T(8,128)S(1)} %pad_maximum_fusion.12), channel_id=1, source_target_pairs={{1,0},{2,1},{3,2},{4,3},{5,4},{6,5},{7,6},{8,7},{9,8},{10,9},{11,1... | collective-permute-start | bytes 4616 | tf_op jit(solution)/shard_map/ppermute | solution.py:40
  135.0 8.8 %collective-permute-start.15 = (f32[6,1,64]{2,0,1:T(8,128)S(1)}, f32[6,1,64]{2,0,1:T(8,128)S(1)}, u32[]{:S(2)}, u32[]{:S(2)}) collective-permute-start(f32[6,1,64]{2,0,1:T(8,128)S(1)} %pad_maximum_fusion.12), channel_id=1, source_target_pairs={{0,1},{1,2},{2,3},{3,4},{4,5},{5,6},{6,7},{7,8},{8,9},{9,10},{10,1... | collective-permute-start | bytes 4616 | tf_op jit(solution)/shard_map/ppermute | solution.py:39
  144.6 5.7 collective-permute-start.16
  148.3 5.5 collective-permute-start.17
  153.8 5.3 collective-permute-start.18
  157.2 8.8 %collective-permute-start.19 = (f32[6,1,64]{2,0,1:T(8,128)S(1)}, f32[6,1,64]{2,0,1:T(8,128)S(1)}, u32[]{:S(2)}, u32[]{:S(2)}) collective-permute-start(f32[6,1,64]{2,0,1:T(8,128)S(1)} %pad_maximum_fusion.15), channel_id=1, source_target_pairs={{0,1},{1,2},{2,3},{3,4},{4,5},{5,6},{6,7},{7,8},{8,9},{9,10},{10,1... | collective-permute-start | bytes 4616 | tf_op jit(solution)/shard_map/ppermute | solution.py:39
  166.8 5.4 collective-permute-start.20
  168.7 5.5 collective-permute-start.21
  174.2 5.3 collective-permute-start.22
  177.4 8.8 %collective-permute-start.23 = (f32[6,1,64]{2,0,1:T(8,128)S(1)}, f32[6,1,64]{2,0,1:T(8,128)S(1)}, u32[]{:S(2)}, u32[]{:S(2)}) collective-permute-start(f32[6,1,64]{2,0,1:T(8,128)S(1)} %pad_maximum_fusion.18), channel_id=1, source_target_pairs={{0,1},{1,2},{2,3},{3,4},{4,5},{5,6},{6,7},{7,8},{8,9},{9,10},{10,1... | collective-permute-start | bytes 4616 | tf_op jit(solution)/shard_map/ppermute | solution.py:39
  187.1 15.4 %collective-permute-start.24 = (f32[1,1,64]{2,0,1:T(1,128)S(1)}, f32[1,1,64]{2,0,1:T(1,128)S(1)}, u32[]{:S(2)}, u32[]{:S(2)}) collective-permute-start(f32[1,1,64]{2,0,1:T(1,128)S(1)} %get-tuple-element.620), channel_id=1, source_target_pairs={{128,0},{256,128},{384,256},{0,384},{129,1},{257,129},{385,257},{1... | collective-permute-start | bytes 776 | tf_op jit(solution)/shard_map/ppermute | solution.py:40
  189.0 13.5 %collective-permute-start.25 = (f32[1,1,64]{2,0,1:T(1,128)S(1)}, f32[1,1,64]{2,0,1:T(1,128)S(1)}, u32[]{:S(2)}, u32[]{:S(2)}) collective-permute-start(f32[1,1,64]{2,0,1:T(1,128)S(1)} %get-tuple-element.619), channel_id=1, source_target_pairs={{0,128},{128,256},{256,384},{384,0},{1,129},{129,257},{257,385},{3... | collective-permute-start | bytes 776 | tf_op jit(solution)/shard_map/ppermute | solution.py:39
  192.4 15.4 %collective-permute-start.2 = (f32[3,4,1,2,128]{4,3,2,1,0:T(2,128)S(1)}, f32[3,4,1,2,128]{4,3,2,1,0:T(2,128)S(1)}, u32[]{:S(2)}, u32[]{:S(2)}) collective-permute-start(f32[3,4,1,2,128]{4,3,2,1,0:T(2,128)S(1)} %get-tuple-element.607), channel_id=1, source_target_pairs={{0,16},{16,32},{32,48},{48,64},{64,80},{80,96},{96,112},{112,0},{1... | collective-permute-start | bytes 36872 | tf_op jit(solution)/shard_map/ppermute | solution.py:39
  200.5 8.9 %collective-permute-start.3 = (f32[3,4,1,2,128]{4,3,2,1,0:T(2,128)S(1)}, f32[3,4,1,2,128]{4,3,2,1,0:T(2,128)S(1)}, u32[]{:S(2)}, u32[]{:S(2)}) collective-permute-start(f32[3,4,1,2,128]{4,3,2,1,0:T(2,128)S(1)} %get-tuple-element.608), channel_id=1, source_target_pairs={{16,0},{32,16},{48,32},{64,48},{80,64},{96,80},{112,96},{0,112},{1... | collective-permute-start | bytes 36872 | tf_op jit(solution)/shard_map/ppermute | solution.py:40
  202.5 135.0 %collective-permute-start.26 = (f32[6,1,64]{2,0,1:T(8,128)S(1)}, f32[6,1,64]{2,0,1:T(8,128)S(1)}, u32[]{:S(2)}, u32[]{:S(2)}) collective-permute-start(f32[6,1,64]{2,0,1:T(8,128)S(1)} %pad_maximum_fusion.21), channel_id=1, source_target_pairs={{1,0},{2,1},{3,2},{4,3},{5,4},{6,5},{7,6},{8,7},{9,8},{10,9},{11,1... | collective-permute-start | bytes 4616 | tf_op jit(solution)/shard_map/ppermute | solution.py:40
  204.4 133.1 %collective-permute-start.27 = (f32[6,1,64]{2,0,1:T(8,128)S(1)}, f32[6,1,64]{2,0,1:T(8,128)S(1)}, u32[]{:S(2)}, u32[]{:S(2)}) collective-permute-start(f32[6,1,64]{2,0,1:T(8,128)S(1)} %pad_maximum_fusion.21), channel_id=1, source_target_pairs={{0,1},{1,2},{2,3},{3,4},{4,5},{5,6},{6,7},{7,8},{8,9},{9,10},{10,1... | collective-permute-start | bytes 4616 | tf_op jit(solution)/shard_map/ppermute | solution.py:39
  209.6 9.2 %collective-permute-start.4 = (f32[3,4,10,1,128]{4,3,2,1,0:T(1,128)S(1)}, f32[3,4,10,1,128]{4,3,2,1,0:T(1,128)S(1)}, u32[]{:S(2)}, u32[]{:S(2)}) collective-permute-start(f32[3,4,10,1,128]{4,3,2,1,0:T(1,128)S(1)} %get-tuple-element.605), channel_id=1, source_target_pairs={{0,1},{1,2},{2,3},{3,4},{4,5},{5,6},{6,7},{7,8},{8,9},{9,10},{10,1... | collective-permute-start | bytes 184328 | tf_op jit(solution)/shard_map/ppermute | solution.py:39
  211.5 8.5 %collective-permute-start.5 = (f32[3,4,10,1,128]{4,3,2,1,0:T(1,128)S(1)}, f32[3,4,10,1,128]{4,3,2,1,0:T(1,128)S(1)}, u32[]{:S(2)}, u32[]{:S(2)}) collective-permute-start(f32[3,4,10,1,128]{4,3,2,1,0:T(1,128)S(1)} %get-tuple-element.606), channel_id=1, source_target_pairs={{1,0},{2,1},{3,2},{4,3},{5,4},{6,5},{7,6},{8,7},{9,8},{10,9},{11,1... | collective-permute-start | bytes 184328 | tf_op jit(solution)/shard_map/ppermute | solution.py:40
  331.0 15.1 %collective-permute-start.6 = (f32[1,8,2,128]{3,2,1,0:T(2,128)S(1)}, f32[1,8,2,128]{3,2,1,0:T(2,128)S(1)}, u32[]{:S(2)}, u32[]{:S(2)}) collective-permute-start(f32[1,8,2,128]{3,2,1,0:T(2,128)S(1)} %get-tuple-element.615), channel_id=1, source_target_pairs={{0,128},{128,256},{256,384},{384,0},{1,129},{129,257},{257,385},{3... | collective-permute-start | bytes 24584 | tf_op jit(solution)/shard_map/ppermute | solution.py:39
  333.4 12.6 %collective-permute-start.7 = (f32[1,8,2,128]{3,2,1,0:T(2,128)S(1)}, f32[1,8,2,128]{3,2,1,0:T(2,128)S(1)}, u32[]{:S(2)}, u32[]{:S(2)}) collective-permute-start(f32[1,8,2,128]{3,2,1,0:T(2,128)S(1)} %get-tuple-element.616), channel_id=1, source_target_pairs={{128,0},{256,128},{384,256},{0,384},{129,1},{257,129},{385,257},{1... | collective-permute-start | bytes 24584 | tf_op jit(solution)/shard_map/ppermute | solution.py:40
  339.0 43.5 %all-to-all-start = ((f32[4,1,64]{0,1,2:T(1,128)}), f32[4,1,64]{0,1,2:T(1,128)S(1)}, u32[]{:S(2)}, u32[]{:S(2)}) async-start(f32[4,1,64]{0,1,2:T(1,128)} %copy.79), calls=%async_computation | async-start | bytes 65536 | tf_op jit(solution)/shard_map/all_to_all | solution.py:192
  346.1 62.4 %collective-permute-start.8 = (f32[4,1,2,128]{3,2,1,0:T(2,128)S(1)}, f32[4,1,2,128]{3,2,1,0:T(2,128)S(1)}, u32[]{:S(2)}, u32[]{:S(2)}) collective-permute-start(f32[4,1,2,128]{3,2,1,0:T(2,128)S(1)} %get-tuple-element.613), channel_id=1, source_target_pairs={{0,16},{16,32},{32,48},{48,64},{64,80},{80,96},{96,112},{112,0},{1... | collective-permute-start | bytes 12296 | tf_op jit(solution)/shard_map/ppermute | solution.py:39
  354.8 53.6 %collective-permute-start.9 = (f32[4,1,2,128]{3,2,1,0:T(2,128)S(1)}, f32[4,1,2,128]{3,2,1,0:T(2,128)S(1)}, u32[]{:S(2)}, u32[]{:S(2)}) collective-permute-start(f32[4,1,2,128]{3,2,1,0:T(2,128)S(1)} %get-tuple-element.614), channel_id=1, source_target_pairs={{16,0},{32,16},{48,32},{64,48},{80,64},{96,80},{112,96},{0,112},{1... | collective-permute-start | bytes 12296 | tf_op jit(solution)/shard_map/ppermute | solution.py:40
  408.5 9.6 %collective-permute-start.10 = (f32[4,10,1,128]{3,2,1,0:T(1,128)S(1)}, f32[4,10,1,128]{3,2,1,0:T(1,128)S(1)}, u32[]{:S(2)}, u32[]{:S(2)}) collective-permute-start(f32[4,10,1,128]{3,2,1,0:T(1,128)S(1)} %get-tuple-element.611), channel_id=1, source_target_pairs={{0,1},{1,2},{2,3},{3,4},{4,5},{5,6},{6,7},{7,8},{8,9},{9,10},{10,1... | collective-permute-start | bytes 61448 | tf_op jit(solution)/shard_map/ppermute | solution.py:39
  412.1 6.7 %collective-permute-start.11 = (f32[4,10,1,128]{3,2,1,0:T(1,128)S(1)}, f32[4,10,1,128]{3,2,1,0:T(1,128)S(1)}, u32[]{:S(2)}, u32[]{:S(2)}) collective-permute-start(f32[4,10,1,128]{3,2,1,0:T(1,128)S(1)} %get-tuple-element.612), channel_id=1, source_target_pairs={{1,0},{2,1},{3,2},{4,3},{5,4},{6,5},{7,6},{8,7},{9,8},{10,9},{11,1... | collective-permute-start | bytes 61448 | tf_op jit(solution)/shard_map/ppermute | solution.py:40
  (2 other events, 1.4 us)
where the time goes:
time: 585 us; the launch traced here: 581 us
  other arithmetic  186 us (32%)
  starting transfers between devices  118 us (20%)
  local copies, waits for them, and re-layouts  89.4 us (15%)
  loops' own time  88 us (15%)
  blocking collectives  69.6 us (12%)
  waiting for transfers between devices  29.5 us (5%)
    reduce_sum x144, other arithmetic, forces_column(): jnp.sum(coefficient * deltas[axis_no], axis=-1)  100 us
    unnamed x1, blocking collectives  69.6 us
    ppermute x14, starting transfers between devices, extended_2(): after = lax.ppermute(first, axis, down)  63.7 us
    reduce_sum x96, other arithmetic, densities_column(): summed = summed + jnp.sum(weight, axis=-1)  47.8 us
    ppermute x14, starting transfers between devices, extended_2(): before = lax.ppermute(last, axis, up)  46.7 us
    another operation x1, loops' own time, densities(): lax.scan(densities_column, zero, jnp.arange(width_x * width_y, dtype=jnp....  45.3 us
    another operation x1, loops' own time, forces(): lax.scan(forces_column, zero, jnp.arange(width_x * width_y, dtype=jnp.int...  42.7 us
    scatter-add x1, other arithmetic, per_device(): jax.ops.segment_sum(kinetic.reshape(-1), flat_index.reshape(-1), num_segm...  28.8 us
  transfers between devices with their start and end apart: 29, of which 8 were waited for; matrix products, arithmetic and copies ran while one was open for 26% of the time, Pallas kernels for 0%

commit v1 on v0

v1 whole, which is shorter than its diff:
```python
import functools
import numpy as np
import jax
import jax.numpy as jnp
from jax import lax
from jax.experimental import pallas as pl
from jax.experimental.pallas import tpu as pltpu
from jax.sharding import PartitionSpec as P

CUT = 30.25
EDGE = 11.0
HALF = 5.5
BIG = 10000.0
F32 = jnp.float32
BF = jnp.bfloat16


def split3(v):
    hi = v.astype(BF).astype(F32)
    rest = v - hi
    mid = rest.astype(BF).astype(F32)
    return hi, mid, rest - mid


def shift_tables():
    m = np.zeros((27, 8, 128), np.float32)
    k = np.zeros((27, 8, 128), np.float32)
    n = 0
    for ox in (-1, 0, 1):
        for oy in (-1, 0, 1):
            for oz in (-1, 0, 1):
                o = (ox, oy, oz)
                m[n, 0:5] = 1.0
                for a in range(3):
                    m[n, 5 + a] = o[a]
                    k[n, a] = -2.0 * EDGE * o[a]
                k[n, 4] = -EDGE * EDGE * sum(abs(a) for a in o)
                n += 1
    return m, k


def cell_rows(pos_ref, x, y, z):
    px = pos_ref[0, x, y, pl.ds(z, 1), :]
    py = pos_ref[1, x, y, pl.ds(z, 1), :]
    pz = pos_ref[2, x, y, pl.ds(z, 1), :]
    empty = px > 500.0
    qx = jnp.where(empty, 0.0, px - HALF)
    qy = jnp.where(empty, 0.0, py - HALF)
    qz = jnp.where(empty, 0.0, pz - HALF)
    s = jnp.where(empty, BIG, qx * qx + qy * qy + qz * qz)
    b = lambda v: jnp.broadcast_to(v, (8, 128))
    return b(qx), b(qy), b(qz), b(s)


def pick(row, *vals):
    out = vals[-1]
    for n in range(len(vals) - 2, -1, -1):
        out = jnp.where(row == n, vals[n], out)
    return out


def neighbour_block(row, rows):
    qx, qy, qz, s = rows
    v = pick(row, qx, qy, qz, s, jnp.float32(1.0), jnp.float32(2.0 * EDGE))
    hi, mid, lo = split3(v)
    z = jnp.zeros_like(hi)
    return jnp.concatenate([hi, mid, lo, hi, mid, hi, z, z], axis=0)


def centre_block(row, rows):
    qx, qy, qz, s = rows
    return pick(row, 2.0 * qx, 2.0 * qy, 2.0 * qz, jnp.float32(-1.0), CUT - s, qx, qy, qz)


def centre_weights(d, m, k):
    u1, u2, u3 = split3(d * m + k)
    z = jnp.zeros_like(u1)
    return jnp.concatenate([u1, u1, u1, u2, u2, u3, z, z], axis=0).astype(BF)


def dot(a, b):
    return jnp.dot(a, b, preferred_element_type=F32)


def pair_values(te_ref, base, odd, c0, c1):
    z64 = jnp.zeros((64, 128), BF)
    if not odd:
        lhs = te_ref[base]
        rhs = jnp.concatenate([jnp.concatenate([c0, z64], 1), jnp.concatenate([z64, c1], 1)], 0)
    else:
        lhs = jnp.concatenate([te_ref[base], te_ref[base + 1]], 1)
        rhs = jnp.concatenate(
            [jnp.concatenate([z64, c0, z64, z64], 0), jnp.concatenate([z64, z64, c1, z64], 0)], 1)
    return jnp.maximum(dot(lhs, rhs), 0.0)


def main_kernel(EX, EY, EZ, pos_ref, vel_ref, grid_ref, diff_ref, m_ref, k_ref, out_ref, te_ref, sl_ref, g_ref):
    NP = EZ // 2
    row = lax.broadcasted_iota(jnp.int32, (8, 128), 0)
    jj = lax.broadcasted_iota(jnp.int32, (128, 256), 0)
    ii = lax.broadcasted_iota(jnp.int32, (128, 256), 1)
    diag = (jj == ii) | (jj + 128 == ii)

    def prep(n, _):
        x = n // EY
        y = n % EY
        for p in range(NP):
            a = neighbour_block(row, cell_rows(pos_ref, x, y, 2 * p))
            b = neighbour_block(row, cell_rows(pos_ref, x, y, 2 * p + 1))
            te_ref[n * NP + p] = jnp.concatenate([a, b], 0).T.astype(BF)
        return 0
    lax.fori_loop(0, EX * EY, prep, 0)

    DY = EY - 2
    DP = (EZ - 2) // 2

    def dens(n, _):
        zp = n % DP
        c = n // DP
        y = c % DY + 1
        x = c // DY + 1
        z0 = 1 + 2 * zp
        d0 = centre_block(row, cell_rows(pos_ref, x, y, z0))
        d1 = centre_block(row, cell_rows(pos_ref, x, y, z0 + 1))
        acc = jnp.zeros((8, 256), F32)
        for ox in (-1, 0, 1):
            for oy in (-1, 0, 1):
                col = ((x + ox) * EY + y + oy) * NP + zp
                for oz in (-1, 0, 1):
                    o = (ox + 1) * 9 + (oy + 1) * 3 + oz + 1
                    m, k = m_ref[o], k_ref[o]
                    c0, c1 = centre_weights(d0, m, k), centre_weights(d1, m, k)
                    r = pair_values(te_ref, col + (1 if oz == 1 else 0), oz == 0, c0, c1)
                    if o == 13:
                        r = jnp.where(diag, 0.0, r)
                    w = r * r * r
                    acc = acc + w.reshape(16, 8, 256).sum(0)
        d = jnp.sum(acc, axis=0, keepdims=True) * (1.0 / CUT ** 3)
        sl = -0.5 / jnp.sqrt(d + 1.0)
        sl_ref[x, y, pl.ds(z0, 1), :] = sl[:, :128]
        sl_ref[x, y, pl.ds(z0 + 1, 1), :] = sl[:, 128:]
        return 0
    lax.fori_loop(0, (EX - 2) * DY * DP, dens, 0)

    def gprep(n, _):
        x = n // DY + 1
        y = n % DY + 1
        for z in range(1, EZ - 1):
            qx, qy, qz, _s = cell_rows(pos_ref, x, y, z)
            s = jnp.broadcast_to(sl_ref[x, y, pl.ds(z, 1), :], (8, 128))
            r4 = row % 4
            v = pick(r4, qx, qy, qz, jnp.ones_like(qx))
            v = v * jnp.where(row < 4, 1.0, s)
            hi, mid, lo = split3(v)
            g_ref[(x * EY + y) * EZ + z] = jnp.concatenate([hi, mid, lo, jnp.zeros_like(hi)], 0).astype(BF)
        return 0
    lax.fori_loop(0, (EX - 2) * DY, gprep, 0)

    FY = EY - 4

    def force(n, _):
        y = n % FY + 2
        x = n // FY + 2
        z0 = 2
        rows0 = cell_rows(pos_ref, x, y, z0)
        rows1 = cell_rows(pos_ref, x, y, z0 + 1)
        d0, d1 = centre_block(row, rows0), centre_block(row, rows1)
        zero = jnp.zeros((8, 128), F32)
        acc = [[zero] * 4, [zero] * 4]
        for ox in (-1, 0, 1):
            for oy in (-1, 0, 1):
                colxy = (x + ox) * EY + y + oy
                for oz in (-1, 0, 1):
                    o = (ox + 1) * 9 + (oy + 1) * 3 + oz + 1
                    m, k = m_ref[o], k_ref[o]
                    c0, c1 = centre_weights(d0, m, k), centre_weights(d1, m, k)
                    L = z0 + oz
                    r = pair_values(te_ref, colxy * NP + L // 2, L % 2 == 1, c0, c1)
                    if o == 13:
                        r = jnp.where(diag, 0.0, r)
                    t = r * r
                    hi = t.astype(BF)
                    lo = (t - hi.astype(F32)).astype(BF)
                    for half in range(2):
                        ls = slice(128 * half, 128 * half + 128)
                        tt = jnp.concatenate([hi[:, ls], lo[:, ls]], 0)
                        g = g_ref[colxy * EZ + L + half]
                        f = dot(jnp.concatenate([g, g], 1), tt)
                        f8 = f[0:8] + f[8:16] + f[16:24]
                        a = acc[half]
                        a[0] = a[0] + f8
                        for ax, s in ((1, ox), (2, oy), (3, oz)):
                            if s == 1:
                                a[ax] = a[ax] + f8
                            elif s == -1:
                                a[ax] = a[ax] - f8
        for half, rows in ((0, rows0), (1, rows1)):
            a = acc[half]
            z = z0 + half
            s = sl_ref[x, y, pl.ds(z, 1), :]
            gi = grid_ref[x - 2, y - 2, pl.ds(half, 1), :]
            dl = diff_ref[(x - 2) * FY + y - 2, pl.ds(half, 1), :]
            h = jnp.zeros((1, 128), F32)
            for kk in range(8):
                h = jnp.where(gi == kk, dl[:, kk:kk + 1], h)
            occ = gi < 8
            for ax in range(3):
                q = rows[ax][0:1]
                M = a[0][ax:ax + 1] + EDGE * a[1 + ax][3:4] - q * a[0][3:4]
                N = a[0][4 + ax:5 + ax] + EDGE * a[1 + ax][7:8] - q * a[0][7:8]
                fo = (2.0 / CUT ** 2) * ((-3.0 / CUT) * (s * M + N) + (-1.5 / CUT) * M)
                v = vel_ref[ax, x - 2, y - 2, pl.ds(half, 1), :]
                o_ = v + 0.2 * fo + 0.02 * h * v
                out_ref[ax, x - 2, y - 2, pl.ds(half, 1), :] = jnp.where(occ, o_, 0.0)
        return 0
    lax.fori_loop(0, (EX - 4) * FY, force, 0)


def main_call(pos, vel, gidx, diff):
    EX, EY, EZ = pos.shape[1:4]
    m, k = shift_tables()
    vm = pl.BlockSpec(memory_space=pltpu.VMEM)
    return pl.pallas_call(
        functools.partial(main_kernel, EX, EY, EZ),
        out_shape=jax.ShapeDtypeStruct(vel.shape, F32),
        in_specs=[vm] * 6,
        out_specs=vm,
        scratch_shapes=[
            pltpu.VMEM((EX * EY * EZ // 2, 128, 128), BF),
            pltpu.VMEM((EX, EY, EZ, 128), F32),
            pltpu.VMEM((EX * EY * EZ, 32, 128), BF),
        ],
        compiler_params=pltpu.CompilerParams(vmem_limit_bytes=56 * 2 ** 20),
        name="pair_forces",
    )(pos, vel, gidx, diff, jnp.asarray(m), jnp.asarray(k))


def diffuse_kernel(EX, EY, EZ, g_ref, e_out, diff_out, e_ref):
    rows = EX * EY * EZ
    pad = EY * EZ + 8 - (EY * EZ) % 8
    lat = g_ref[...]
    e_ref[...] = jnp.zeros(e_ref.shape, F32)
    e = pltpu.roll(lat, 120, 1)
    lane = lax.broadcasted_iota(jnp.int32, (rows, 128), 1)
    for step in range(4):
        e_ref[pl.ds(pad, rows), :] = e
        beside = None
        for bit, stride in ((1, 1), (2, EZ), (4, EY * EZ)):
            after = e_ref[pl.ds(pad + stride, rows), :]
            before = e_ref[pl.ds(pad - stride, rows), :]
            low = pltpu.roll(e + before, 128 - bit, 1)
            high = pltpu.roll(e + after, bit, 1)
            s = jnp.where((lane & bit) == 0, low, high)
            beside = s if beside is None else beside + s
        e = e + 0.15 * (beside - 6.0 * e) - 0.05 * (e - lat)
    d = e - lat
    e_ref[pl.ds(pad, rows), :] = e
    for x in range(2, EX - 2):
        for y in range(2, EY - 2):
            r = (x * EY + y) * EZ + 2
            n = (x - 2) * (EY - 4) + y - 2
            e_out[n] = e[r:r + EZ - 4]
            diff_out[n] = d[r:r + EZ - 4]


def diffuse_call(grid):
    EX, EY, EZ = grid.shape[:3]
    rows = EX * EY * EZ
    pad = EY * EZ + 8 - (EY * EZ) % 8
    vm = pl.BlockSpec(memory_space=pltpu.VMEM)
    shape = jax.ShapeDtypeStruct(((EX - 4) * (EY - 4), EZ - 4, 128), F32)
    return pl.pallas_call(
        functools.partial(diffuse_kernel, EX, EY, EZ),
        out_shape=(shape, shape),
        in_specs=[vm],
        out_specs=(vm, vm),
        scratch_shapes=[pltpu.VMEM((rows + 2 * pad, 128), F32)],
        name="diffusion",
    )(grid.reshape(rows, 128))


def extend(value, sides, width):
    for axis, dim in sides:
        devices, length = lax.axis_size(axis), value.shape[dim]
        up = [(i, (i + 1) % devices) for i in range(devices)]
        down = [(j, i) for i, j in up]
        before = lax.ppermute(lax.slice_in_dim(value, length - width, length, axis=dim), axis, up)
        after = lax.ppermute(lax.slice_in_dim(value, 0, width, axis=dim), axis, down)
        value = jnp.concatenate([before, value, after], axis=dim)
    return value


def per_device(positions, velocities, counts, grid_cells, electron_temp):
    nx, ny, nz = counts.shape
    slot = lax.broadcasted_iota(jnp.int32, grid_cells.shape, 3)
    occupied = slot < counts[..., None]
    e = lax.all_to_all(electron_temp, "gz", split_axis=2, concat_axis=1, tiled=True)
    e = e.reshape(nx, 2, ny, 2, nz, 2).transpose(0, 2, 4, 1, 3, 5).reshape(nx, ny, nz, 8)
    kinetic = jnp.where(occupied, 0.5 * jnp.sum(velocities * velocities, axis=0), 0.0)
    sub = lax.broadcasted_iota(jnp.int32, (nx, ny, nz, 8, 128), 3)
    lat = jnp.sum(jnp.where(grid_cells[..., None, :] == sub, kinetic[..., None, :], 0.0), axis=-1)
    row = jnp.concatenate([lat, e, jnp.zeros((nx, ny, nz, 112), F32)], axis=-1)
    parked = jnp.where(occupied[None], positions, 1000.0)
    field = jnp.concatenate([parked, row[None]], axis=0)
    field = extend(field, (("gx", 1), ("gz", 3), ("gy", 2)), 2)
    e_new, diff = diffuse_call(field[3])
    heat = e_new[..., :8].reshape(nx, ny, nz, 2, 2, 2).transpose(0, 3, 1, 4, 2, 5)
    heat = heat.reshape(2 * nx, 2 * ny, 2 * nz)
    heat = lax.all_to_all(heat, "gz", split_axis=1, concat_axis=2, tiled=True)
    gidx = jnp.where(occupied, grid_cells, 8)
    velocity_out = main_call(field[:3], velocities, gidx, diff)
    return velocity_out, heat


def solution(mesh):
    return jax.shard_map(
        per_device,
        mesh=mesh,
        in_specs=(
            P(None, "gx", "gy", "gz", None),
            P(None, "gx", "gy", "gz", None),
            P("gx", "gy", "gz"),
            P("gx", "gy", "gz", None),
            P("gx", ("gy", "gz"), None),
        ),
        out_specs=(P(None, "gx", "gy", "gz", None), P("gx", ("gy", "gz"), None)),
        check_vma=False,
    )
```

time: 585 us -> 174 us (0.30)
  other arithmetic: 186 us -> 3.99 us
  Pallas kernels: 0 us -> 92.9 us
  loops' own time: 88 us -> 0 us
  local copies, waits for them, and re-layouts: 89.4 us -> 6.88 us
  starting transfers between devices: 118 us -> 48.3 us
  blocking collectives: 69.6 us -> 0 us
  waiting for transfers between devices: 29.5 us -> 20.3 us
    reduce_sum x240 -> x1, other arithmetic: 148 us -> 0.83 us  [per_device(): jnp.sum(jnp.where(grid_cells[..., None, :] == sub, kinetic[..., None, :],...]
    pallas_call x0 -> x2, Pallas kernels: none -> 92.9 us  [the longest x1 89.6 us: main_call(): pl.pallas_call(functools.partial(main_kernel, EX, EY, EZ), out_shape=jax....]
    another operation x2 -> x0, loops' own time: 88 us -> none  [the longest x1 45.3 us: densities(): lax.scan(densities_column, zero, jnp.arange(width_x * width_y, dtype=jnp....]
    ppermute x28 -> x6, starting transfers between devices: 110 us -> 31 us  [the longest x3 18.6 us: extend(): lax.ppermute(lax.slice_in_dim(value, length - width, length, axis=dim), a...]
    unnamed x1 -> x0, blocking collectives: 69.6 us -> none
    gather x2 -> x0, local copies, waits for them, and re-layouts: 51.5 us -> none  [the longest x1 25.7 us: per_device(): electron_here = jnp.take(returned.reshape(-1), flat_index)]
    scatter-add x1 -> x0, other arithmetic: 28.8 us -> none  [per_device(): jax.ops.segment_sum(kinetic.reshape(-1), flat_index.reshape(-1), num_segm...]
    dynamic_slice x32 -> x0, local copies, waits for them, and re-layouts: 20 us -> none  [densities(): lax.scan(densities_column, zero, jnp.arange(width_x * width_y, dtype=jnp....]
  transfers between devices with their start and end apart: 29 -> 8, of which waited for: 8 -> 6; matrix products, arithmetic and copies ran while one was open for 26% -> 3% of each run, Pallas kernels for 0% -> 52%
where the time goes in v1:
time: 174 us; the launch traced here: 173 us
  Pallas kernels  92.9 us (53%)
  starting transfers between devices  48.3 us (28%)
  waiting for transfers between devices  20.3 us (12%)
  local copies, waits for them, and re-layouts  6.88 us (4%)
  other arithmetic  3.99 us (2%)
    pallas_call x1, Pallas kernels, main_call(): pl.pallas_call(functools.partial(main_kernel, EX, EY, EZ), out_shape=jax....  89.6 us
    ppermute x3, starting transfers between devices, extend(): lax.ppermute(lax.slice_in_dim(value, length - width, length, axis=dim), a...  18.6 us
    ppermute x3, starting transfers between devices, extend(): lax.ppermute(lax.slice_in_dim(value, 0, width, axis=dim), axis, down)  12.3 us
    ppermute x3, waiting for transfers between devices, extend(): lax.ppermute(lax.slice_in_dim(value, 0, width, axis=dim), axis, down)  9.89 us
    all_to_all x1, starting transfers between devices, per_device(): lax.all_to_all(electron_temp, 'gz', split_axis=2, concat_axis=1, tiled=True)  9.19 us
    all_to_all x1, starting transfers between devices, per_device(): heat = lax.all_to_all(heat, 'gz', split_axis=1, concat_axis=2, tiled=True)  8.15 us
    ppermute x3, waiting for transfers between devices, extend(): lax.ppermute(lax.slice_in_dim(value, length - width, length, axis=dim), a...  7.13 us
  transfers between devices with their start and end apart: 8, of which 6 were waited for; matrix products, arithmetic and copies ran while one was open for 3% of the time, Pallas kernels for 52%

profile of v1, /device:TPU:1, one launch (start us, length us, event | category | flops | bytes accessed | tf_op | source)
XLA Modules:
  0.0 173.2 jit_solution(11057898431282077825)
XLA Ops:
  0.6 1.4 copy.39
  2.0 9.2 %all-to-all-start = ((f32[4,1,64]{0,1,2:T(1,128)}), f32[4,1,64]{0,1,2:T(1,128)S(1)}, u32[]{:S(2)}, u32[]{:S(2)}) async-start(f32[4,1,64]{0,1,2:T(1,128)} %copy.39), calls=%async_computation | async-start | bytes 65536 | tf_op jit(solution)/shard_map/all_to_all | solution.py:297
  11.2 0.8 copy.38
  12.0 0.8 multiply_reduce_fusion
  13.0 0.8 broadcast_select_fusion
  13.8 0.8 select_reduce_fusion
  14.7 3.3 %all-to-all-done = f32[4,1,64]{0,1,2:T(1,128)S(1)} async-done(((f32[4,1,64]{0,1,2:T(1,128)}), f32[4,1,64]{0,1,2:T(1,128)S(1)}, u32[]{:S(2)}, u32[]{:S(2)}) %all-to-all-start) | async-done | bytes 1056 | tf_op jit(solution)/shard_map/all_to_all | solution.py:297
  18.1 0.2 reshape.37
  18.3 0.2 copy.41
  18.7 3.1 %collective-permute-start = (f32[4,2,8,2,128]{4,3,2,1,0:T(2,128)S(1)}, f32[4,2,8,2,128]{4,3,2,1,0:T(2,128)S(1)}, u32[]{:S(2)}, u32[]{:S(2)}) collective-permute-start(f32[4,2,8,2,128]{4,3,2,1,0:T(2,128)S(1)} %pad_maximum_fusion.8), channel_id=1, source_target_pairs={{0,128},{128,256},{256,384},{384,0},{1,129},{129,257},{257,385},{3... | collective-permute-start | bytes 196616 | tf_op jit(solution)/shard_map/ppermute | solution.py:287
  21.8 3.4 %collective-permute-start.1 = (f32[4,2,8,2,128]{4,3,2,1,0:T(2,128)S(1)}, f32[4,2,8,2,128]{4,3,2,1,0:T(2,128)S(1)}, u32[]{:S(2)}, u32[]{:S(2)}) collective-permute-start(f32[4,2,8,2,128]{4,3,2,1,0:T(2,128)S(1)} %pad_maximum_fusion.8), channel_id=1, source_target_pairs={{128,0},{256,128},{384,256},{0,384},{129,1},{257,129},{385,257},{1... | collective-permute-start | bytes 196616 | tf_op jit(solution)/shard_map/ppermute | solution.py:288
  25.2 1.6 collective-permute-done.1
  26.9 2.1 %collective-permute-start.2 = (f32[4,6,8,2,128]{4,3,2,1,0:T(2,128)S(1)}, f32[4,6,8,2,128]{4,3,2,1,0:T(2,128)S(1)}, u32[]{:S(2)}, u32[]{:S(2)}) collective-permute-start(f32[4,6,8,2,128]{4,3,2,1,0:T(2,128)S(1)} %pad_maximum_fusion.7), channel_id=1, source_target_pairs={{0,1},{1,2},{2,3},{3,4},{4,5},{5,6},{6,7},{7,8},{8,9},{9,10},{10,1... | collective-permute-start | bytes 589832 | tf_op jit(solution)/shard_map/ppermute | solution.py:287
  29.1 7.0 %collective-permute-start.3 = (f32[4,6,8,2,128]{4,3,2,1,0:T(2,128)S(1)}, f32[4,6,8,2,128]{4,3,2,1,0:T(2,128)S(1)}, u32[]{:S(2)}, u32[]{:S(2)}) collective-permute-start(f32[4,6,8,2,128]{4,3,2,1,0:T(2,128)S(1)} %pad_maximum_fusion.7), channel_id=1, source_target_pairs={{1,0},{2,1},{3,2},{4,3},{5,4},{6,5},{7,6},{8,7},{9,8},{10,9},{11,1... | collective-permute-start | bytes 589832 | tf_op jit(solution)/shard_map/ppermute | solution.py:288
  36.1 1.3 collective-permute-done.2
  37.4 1.3 collective-permute-done.3
  38.7 0.1 pad_maximum_fusion.6
  38.9 13.4 %collective-permute-start.4 = (f32[4,6,2,6,128]{4,3,2,1,0:T(8,128)S(1)}, f32[4,6,2,6,128]{4,3,2,1,0:T(8,128)S(1)}, u32[]{:S(2)}, u32[]{:S(2)}) collective-permute-start(f32[4,6,2,6,128]{4,3,2,1,0:T(8,128)S(1)} %get-tuple-element.14), channel_id=1, source_target_pairs={{0,16},{16,32},{32,48},{48,64},{64,80},{80,96},{96,112},{112,0},{1... | collective-permute-start | bytes 442376 | tf_op jit(solution)/shard_map/ppermute | solution.py:287
  52.2 1.9 %collective-permute-start.5 = (f32[4,6,2,6,128]{4,3,2,1,0:T(8,128)S(1)}, f32[4,6,2,6,128]{4,3,2,1,0:T(8,128)S(1)}, u32[]{:S(2)}, u32[]{:S(2)}) collective-permute-start(f32[4,6,2,6,128]{4,3,2,1,0:T(8,128)S(1)} %get-tuple-element.15), channel_id=1, source_target_pairs={{16,0},{32,16},{48,32},{64,48},{80,64},{96,80},{112,96},{0,112},{1... | collective-permute-start | bytes 442376 | tf_op jit(solution)/shard_map/ppermute | solution.py:288
  54.2 5.9 %collective-permute-done.4 = f32[4,6,2,6,128]{4,3,2,1,0:T(8,128)S(1)} collective-permute-done((f32[4,6,2,6,128]{4,3,2,1,0:T(8,128)S(1)}, f32[4,6,2,6,128]{4,3,2,1,0:T(8,128)S(1)}, u32[]{:S(2)}, u32[]{:S(2)}) %collective-permute-start.4) | collective-permute-done | bytes 147488 | tf_op jit(solution)/shard_map/ppermute | solution.py:287
  60.0 7.0 %collective-permute-done.5 = f32[4,6,2,6,128]{4,3,2,1,0:T(8,128)S(1)} collective-permute-done((f32[4,6,2,6,128]{4,3,2,1,0:T(8,128)S(1)}, f32[4,6,2,6,128]{4,3,2,1,0:T(8,128)S(1)}, u32[]{:S(2)}, u32[]{:S(2)}) %collective-permute-start.5) | collective-permute-done | bytes 147488 | tf_op jit(solution)/shard_map/ppermute | solution.py:288
  67.0 0.3 pad_maximum_fusion
  67.3 0.7 reshape_squeeze.3.g_ref
  68.0 3.3 %diffusion.1 = (f32[16,2,128]{2,1,0:T(2,128)}, f32[16,2,128]{2,1,0:T(2,128)}) custom-call(f32[432,128]{1,0:T(8,128)} %reshape_squeeze.3.g_ref), custom_call_target="tpu_custom_call" | custom-call | tf_op jit(solution)/shard_map/diffusion/pallas_call | solution.py:272
  71.3 0.8 copy.43
  72.2 0.2 copy.48
  72.4 0.7 reshape.41
  73.1 8.1 %all-to-all-start.1 = ((f32[4,16,4]{2,0,1:T(4,128)}), f32[4,16,4]{2,0,1:T(4,128)S(1)}, u32[]{:S(2)}, u32[]{:S(2)}) async-start(f32[4,16,4]{2,0,1:T(4,128)} %reshape.41), calls=%async_computation.1 | async-start | bytes 65536 | tf_op jit(solution)/shard_map/all_to_all | solution.py:309
  81.3 0.7 broadcast_select_fusion.1.grid_ref
  82.0 1.0 slice.20.pos_ref
  83.0 89.6 %pair_forces.1 = f32[3,2,8,2,128]{4,3,2,1,0:T(2,128)} custom-call(f32[3,6,12,6,128]{4,3,2,1,0:T(8,128)} %slice.20.pos_ref, f32[3,2,8,2,128]{4,3,2,1,0:T(2,128)} %vel_ref.1, s32[2,8,2,128]{3,2,1,0:T(2,128)} %broadcast_select_fusion.1.grid_ref, f32[16,2,128]{2,1,0:T(2,128)} %get-tuple-element.4.diff_ref, f32[27,8,128]{2,1,0:T(8,128)} %constant.5.clone.m_ref, ...), custom_call_target="tpu_custom_call" | custom-call | tf_op jit(solution)/shard_map/pair_forces/pallas_call | solution.py:223
  172.5 0.7 all_to_all.8
  (16 shorter events, 0.7 us)
Async XLA Ops:
  2.0 16.0 %all-to-all-start = ((f32[4,1,64]{0,1,2:T(1,128)}), f32[4,1,64]{0,1,2:T(1,128)S(1)}, u32[]{:S(2)}, u32[]{:S(2)}) async-start(f32[4,1,64]{0,1,2:T(1,128)} %copy.39), calls=%async_computation | async-start | bytes 65536 | tf_op jit(solution)/shard_map/all_to_all | solution.py:297
  18.7 6.5 %collective-permute-start = (f32[4,2,8,2,128]{4,3,2,1,0:T(2,128)S(1)}, f32[4,2,8,2,128]{4,3,2,1,0:T(2,128)S(1)}, u32[]{:S(2)}, u32[]{:S(2)}) collective-permute-start(f32[4,2,8,2,128]{4,3,2,1,0:T(2,128)S(1)} %pad_maximum_fusion.8), channel_id=1, source_target_pairs={{0,128},{128,256},{256,384},{384,0},{1,129},{129,257},{257,385},{3... | collective-permute-start | bytes 196616 | tf_op jit(solution)/shard_map/ppermute | solution.py:287
  21.8 5.0 %collective-permute-start.1 = (f32[4,2,8,2,128]{4,3,2,1,0:T(2,128)S(1)}, f32[4,2,8,2,128]{4,3,2,1,0:T(2,128)S(1)}, u32[]{:S(2)}, u32[]{:S(2)}) collective-permute-start(f32[4,2,8,2,128]{4,3,2,1,0:T(2,128)S(1)} %pad_maximum_fusion.8), channel_id=1, source_target_pairs={{128,0},{256,128},{384,256},{0,384},{129,1},{257,129},{385,257},{1... | collective-permute-start | bytes 196616 | tf_op jit(solution)/shard_map/ppermute | solution.py:288
  26.9 10.5 %collective-permute-start.2 = (f32[4,6,8,2,128]{4,3,2,1,0:T(2,128)S(1)}, f32[4,6,8,2,128]{4,3,2,1,0:T(2,128)S(1)}, u32[]{:S(2)}, u32[]{:S(2)}) collective-permute-start(f32[4,6,8,2,128]{4,3,2,1,0:T(2,128)S(1)} %pad_maximum_fusion.7), channel_id=1, source_target_pairs={{0,1},{1,2},{2,3},{3,4},{4,5},{5,6},{6,7},{7,8},{8,9},{9,10},{10,1... | collective-permute-start | bytes 589832 | tf_op jit(solution)/shard_map/ppermute | solution.py:287
  29.1 9.6 %collective-permute-start.3 = (f32[4,6,8,2,128]{4,3,2,1,0:T(2,128)S(1)}, f32[4,6,8,2,128]{4,3,2,1,0:T(2,128)S(1)}, u32[]{:S(2)}, u32[]{:S(2)}) collective-permute-start(f32[4,6,8,2,128]{4,3,2,1,0:T(2,128)S(1)} %pad_maximum_fusion.7), channel_id=1, source_target_pairs={{1,0},{2,1},{3,2},{4,3},{5,4},{6,5},{7,6},{8,7},{9,8},{10,9},{11,1... | collective-permute-start | bytes 589832 | tf_op jit(solution)/shard_map/ppermute | solution.py:288
  38.9 21.2 %collective-permute-start.4 = (f32[4,6,2,6,128]{4,3,2,1,0:T(8,128)S(1)}, f32[4,6,2,6,128]{4,3,2,1,0:T(8,128)S(1)}, u32[]{:S(2)}, u32[]{:S(2)}) collective-permute-start(f32[4,6,2,6,128]{4,3,2,1,0:T(8,128)S(1)} %get-tuple-element.14), channel_id=1, source_target_pairs={{0,16},{16,32},{32,48},{48,64},{64,80},{80,96},{96,112},{112,0},{1... | collective-permute-start | bytes 442376 | tf_op jit(solution)/shard_map/ppermute | solution.py:287
  52.2 14.7 %collective-permute-start.5 = (f32[4,6,2,6,128]{4,3,2,1,0:T(8,128)S(1)}, f32[4,6,2,6,128]{4,3,2,1,0:T(8,128)S(1)}, u32[]{:S(2)}, u32[]{:S(2)}) collective-permute-start(f32[4,6,2,6,128]{4,3,2,1,0:T(8,128)S(1)} %get-tuple-element.15), channel_id=1, source_target_pairs={{16,0},{32,16},{48,32},{64,48},{80,64},{96,80},{112,96},{0,112},{1... | collective-permute-start | bytes 442376 | tf_op jit(solution)/shard_map/ppermute | solution.py:288
  67.3 14.0 %copy-start = (s32[2,8,2,128]{3,2,1,0:T(2,128)S(1)}, s32[2,8,2,128]{3,2,1,0:T(2,128)}, u32[]{:S(2)}) copy-start(s32[2,8,2,128]{3,2,1,0:T(2,128)} %param.10) | copy-start | bytes 49156
  73.1 99.4 %all-to-all-start.1 = ((f32[4,16,4]{2,0,1:T(4,128)}), f32[4,16,4]{2,0,1:T(4,128)S(1)}, u32[]{:S(2)}, u32[]{:S(2)}) async-start(f32[4,16,4]{2,0,1:T(4,128)} %reshape.41), calls=%async_computation.1 | async-start | bytes 65536 | tf_op jit(solution)/shard_map/all_to_all | solution.py:309

commit v2 on v1

v2 whole, which is shorter than its diff:
```python
import functools
import numpy as np
import jax
import jax.numpy as jnp
from jax import lax
from jax.experimental import pallas as pl
from jax.experimental.pallas import tpu as pltpu
from jax.sharding import PartitionSpec as P

CUT = 30.25
EDGE = 11.0
HALF = 5.5
BIG = 10000.0
GROUP = 4
F32 = jnp.float32
BF = jnp.bfloat16
VM = pl.BlockSpec(memory_space=pltpu.VMEM)
SHIFTS = [(x, y, z) for x in (-1, 0, 1) for y in (-1, 0, 1) for z in (-1, 0, 1)]


def split3(v):
    hi = v.astype(BF).astype(F32)
    rest = v - hi
    mid = rest.astype(BF).astype(F32)
    return hi, mid, rest - mid


def shift_tables():
    m = np.zeros((27, 8, 128), np.float32)
    k = np.zeros((27, 8, 128), np.float32)
    for n, o in enumerate(SHIFTS):
        m[n, 0:5] = 1.0
        for a in range(3):
            m[n, 5 + a] = o[a]
            k[n, a] = -2.0 * EDGE * o[a]
            k[n, 4] -= EDGE * EDGE * abs(o[a])
    return jnp.asarray(m), jnp.asarray(k)


def cell_rows(pos_ref, x, y, z):
    px = pos_ref[0, x, y, pl.ds(z, 1), :]
    py = pos_ref[1, x, y, pl.ds(z, 1), :]
    pz = pos_ref[2, x, y, pl.ds(z, 1), :]
    empty = px > 500.0
    qx = jnp.where(empty, 0.0, px - HALF)
    qy = jnp.where(empty, 0.0, py - HALF)
    qz = jnp.where(empty, 0.0, pz - HALF)
    s = jnp.where(empty, BIG, qx * qx + qy * qy + qz * qz)
    return [jnp.broadcast_to(v, (8, 128)) for v in (qx, qy, qz, s)]


def pick(row, *vals):
    out = vals[-1]
    for n in range(len(vals) - 2, -1, -1):
        out = jnp.where(row == n, vals[n], out)
    return out


def neighbour_block(row, rows):
    qx, qy, qz, s = rows
    hi, mid, lo = split3(pick(row, qx, qy, qz, s, jnp.float32(1.0), jnp.float32(2.0 * EDGE)))
    return jnp.concatenate([hi, mid, lo, hi, mid, hi, jnp.zeros_like(hi), jnp.zeros_like(hi)], axis=0)


def centre_block(row, rows):
    qx, qy, qz, s = rows
    return pick(row, 2.0 * qx, 2.0 * qy, 2.0 * qz, jnp.float32(-1.0), CUT - s, qx, qy, qz)


def weights(d, m, k):
    u1, u2, u3 = split3(d * m + k)
    z = jnp.zeros((16, 128), BF)
    c = lambda p, q: jnp.concatenate([p, q], axis=0).astype(BF)
    return jnp.concatenate([c(u1, u1), c(u1, u2), c(u2, u3), z], axis=0)


def dot(a, b):
    return jnp.dot(a, b, preferred_element_type=F32)


def pair_values(table, odd, c0, c1):
    z = jnp.zeros((64, 128), BF)
    left, right = (c0, z), (z, c1)
    if odd:
        left, right = (z, c0), (c1, z)
    rhs = jnp.concatenate([jnp.concatenate(left, 0), jnp.concatenate(right, 0)], 1)
    return jnp.maximum(dot(table, rhs), 0.0)


def same_slot():
    jj = lax.broadcasted_iota(jnp.int32, (128, 256), 0)
    ii = lax.broadcasted_iota(jnp.int32, (128, 256), 1)
    return (jj == ii) | (jj + 128 == ii)


def density_kernel(dims, pos_ref, m_ref, k_ref, sl_ref, te_ref):
    EX, EY, EZ = dims
    NT = EZ - 1
    row = lax.broadcasted_iota(jnp.int32, (8, 128), 0)
    low = lax.broadcasted_iota(jnp.int32, (128, 128), 1) < 64

    def prep(n, carry):
        x = n // EY
        y = n % EY
        tables = []
        for p in range(EZ // 2):
            a = neighbour_block(row, cell_rows(pos_ref, x, y, 2 * p))
            b = neighbour_block(row, cell_rows(pos_ref, x, y, 2 * p + 1))
            tables.append(jnp.concatenate([a, b], 0).T)
        for layer in range(NT):
            p = layer // 2
            t = tables[p] if layer % 2 == 0 else jnp.where(low, tables[p + 1], tables[p])
            te_ref[n * NT + layer] = t.astype(BF)
        return carry

    lax.fori_loop(0, EX * EY, prep, 0)
    sl_ref[...] = jnp.zeros(sl_ref.shape, F32)
    diag = same_slot()
    DY = EY - 2
    DP = (EZ - 2) // 2

    def dens(n, carry):
        y = n % DY + 1
        x = n // DY + 1
        centres = [centre_block(row, cell_rows(pos_ref, x, y, z)) for z in range(1, EZ - 1)]
        acc = [jnp.zeros((8, 256), F32) for _ in range(DP)]
        for n_shift, (ox, oy, oz) in enumerate(SHIFTS):
            m, k = m_ref[n_shift], k_ref[n_shift]
            base = ((x + ox) * EY + y + oy) * NT + oz
            for p in range(DP):
                z0 = 1 + 2 * p
                c0, c1 = [weights(d, m, k) for d in centres[2 * p:2 * p + 2]]
                r = pair_values(te_ref[base + z0], oz == 0, c0, c1)
                if n_shift == 13:
                    r = jnp.where(diag, 0.0, r)
                w = r * r * r
                acc[p] = acc[p] + w.reshape(16, 8, 256).sum(0)
        for p in range(DP):
            d = jnp.sum(acc[p], axis=0, keepdims=True) * (1.0 / CUT ** 3)
            sl = -0.5 / jnp.sqrt(d + 1.0)
            sl_ref[x - 1, y, pl.ds(1 + 2 * p, 1), :] = sl[:, :128]
            sl_ref[x - 1, y, pl.ds(2 + 2 * p, 1), :] = sl[:, 128:]
        return carry

    lax.fori_loop(0, (EX - 2) * DY, dens, 0)


def density_call(pos):
    EX, EY, EZ = pos.shape[1:4]
    m, k = shift_tables()
    return pl.pallas_call(
        functools.partial(density_kernel, (EX, EY, EZ)),
        out_shape=(
            jax.ShapeDtypeStruct((EX - 2, EY, EZ, 128), F32),
            jax.ShapeDtypeStruct((EX * EY * (EZ - 1), 128, 128), BF),
        ),
        in_specs=[VM] * 3,
        out_specs=(VM, VM),
        compiler_params=pltpu.CompilerParams(vmem_limit_bytes=24 * 2 ** 20),
        name="density",
    )(pos, m, k)


def force_kernel(dims, pos_ref, te_ref, sl_ref, vel_ref, grid_ref, diff_ref, m_ref, k_ref, out_ref, g_ref):
    EX, EY, EZ = dims
    NT = EZ - 1
    GY, GZ = EY - 2, EZ - 2
    row = lax.broadcasted_iota(jnp.int32, (8, 128), 0)
    diag = same_slot()

    def gprep(n, carry):
        x = n // GY
        y = n % GY + 1
        for z in range(1, EZ - 1):
            qx, qy, qz, _ = cell_rows(pos_ref, x, y, z)
            s = jnp.broadcast_to(sl_ref[x, y, pl.ds(z, 1), :], (8, 128))
            v = pick(row % 4, qx, qy, qz, jnp.ones_like(qx))
            hi, mid, lo = split3(v * jnp.where(row < 4, 1.0, s))
            g_ref[n * GZ + z - 1] = jnp.concatenate([hi, mid, lo, jnp.zeros_like(hi)], 0).astype(BF)
        return carry

    lax.fori_loop(0, EX * GY, gprep, 0)
    FY = EY - 4

    def force(n, carry):
        x = n // (FY // GROUP) + 1
        first = n % (FY // GROUP) * GROUP + 2
        z0 = 2
        rows = [[cell_rows(pos_ref, x, first + c, z0 + h) for h in range(2)] for c in range(GROUP)]
        centres = [[centre_block(row, r) for r in pair] for pair in rows]
        zero = jnp.zeros((8, 128), F32)
        acc = [[[zero] * 4, [zero] * 4] for c in range(GROUP)]
        for n_shift, shift in enumerate(SHIFTS):
            ox, oy, oz = shift
            m, k = m_ref[n_shift], k_ref[n_shift]
            layer = z0 + oz
            for c in range(GROUP):
                y = first + c
                base = ((x + ox) * EY + y + oy) * NT + layer
                c0, c1 = [weights(d, m, k) for d in centres[c]]
                r = pair_values(te_ref[base], layer % 2 == 1, c0, c1)
                if n_shift == 13:
                    r = jnp.where(diag, 0.0, r)
                t = r * r
                hi = t.astype(BF)
                lo = (t - hi.astype(F32)).astype(BF)
                gbase = ((x + ox) * GY + y + oy - 1) * GZ + layer - 1
                for h in range(2):
                    ls = slice(128 * h, 128 * h + 128)
                    tt = jnp.concatenate([hi[:, ls], lo[:, ls]], 0)
                    g = g_ref[gbase + h]
                    f = dot(jnp.concatenate([g, g], 1), tt)
                    f = f[0:8] + f[8:16] + f[16:24]
                    total = acc[c][h]
                    total[0] = total[0] + f
                    for a in range(3):
                        if shift[a] == 1:
                            total[a + 1] = total[a + 1] + f
                        elif shift[a] == -1:
                            total[a + 1] = total[a + 1] - f
        for c, h in [(c, h) for c in range(GROUP) for h in range(2)]:
            y = first + c
            total = acc[c][h]
            s = sl_ref[x, y, pl.ds(z0 + h, 1), :]
            sub = grid_ref[x - 1, y - 2, pl.ds(h, 1), :]
            both = diff_ref[pl.ds(y * EZ + z0 + h, 1), :]
            here = jnp.where(x == 1, both[:, 16:24], both[:, 24:32])
            heat = jnp.zeros((1, 128), F32)
            for kk in range(8):
                heat = jnp.where(sub == kk, here[:, kk:kk + 1], heat)
            for a in range(3):
                q = rows[c][h][a][0:1]
                plain = total[0][a:a + 1] + EDGE * total[1 + a][3:4] - q * total[0][3:4]
                sloped = total[0][4 + a:5 + a] + EDGE * total[1 + a][7:8] - q * total[0][7:8]
                f = (2.0 / CUT ** 2) * ((-3.0 / CUT) * (s * plain + sloped) + (-1.5 / CUT) * plain)
                v = vel_ref[a, x - 1, y - 2, pl.ds(h, 1), :]
                moved = v + 0.2 * f + 0.02 * heat * v
                out_ref[a, x - 1, y - 2, pl.ds(h, 1), :] = jnp.where(sub < 8, moved, 0.0)
        return carry

    lax.fori_loop(0, (EX - 2) * FY // GROUP, force, 0)


def force_call(pos, te, slopes, vel, sub, diff):
    EX, EY, EZ = pos.shape[1:4]
    m, k = shift_tables()
    return pl.pallas_call(
        functools.partial(force_kernel, (EX, EY, EZ)),
        out_shape=jax.ShapeDtypeStruct(vel.shape, F32),
        in_specs=[VM] * 8,
        out_specs=VM,
        scratch_shapes=[pltpu.VMEM((EX * (EY - 2) * (EZ - 2), 32, 128), BF)],
        compiler_params=pltpu.CompilerParams(vmem_limit_bytes=24 * 2 ** 20),
        name="force",
    )(pos, te, slopes, vel, sub, diff, m, k)


def diffuse_kernel(EZ, x_ref, e_out, diff_out, e_ref):
    rows = x_ref.shape[0]
    own = x_ref[...]
    lane = lax.broadcasted_iota(jnp.int32, (rows, 128), 1)
    lat = pltpu.roll(own, 64, 1)
    e = own
    e_ref[...] = jnp.zeros(e_ref.shape, F32)
    for step in range(4):
        e_ref[pl.ds(8, rows), :] = e
        beside = pltpu.roll(e, 4, 1) + pltpu.roll(e, 124, 1)
        for bit, stride in ((1, 1), (2, EZ)):
            after = e_ref[pl.ds(8 + stride, rows), :]
            before = e_ref[pl.ds(8 - stride, rows), :]
            low = pltpu.roll(e + before, 128 - bit, 1)
            high = pltpu.roll(e + after, bit, 1)
            beside = beside + jnp.where((lane & bit) == 0, low, high)
        e = e + 0.15 * (beside - 6.0 * e) - 0.05 * (e - lat)
    e_out[...] = e
    diff_out[...] = e - lat


def diffuse_call(grid):
    EY, EZ = grid.shape[:2]
    rows = EY * EZ
    shape = jax.ShapeDtypeStruct((rows, 128), F32)
    return pl.pallas_call(
        functools.partial(diffuse_kernel, EZ),
        out_shape=(shape, shape),
        in_specs=[VM],
        out_specs=(VM, VM),
        scratch_shapes=[pltpu.VMEM((rows + 16, 128), F32)],
        name="diffusion",
    )(grid.reshape(rows, 128))


def ring(value, axis, step):
    n = lax.axis_size(axis)
    return lax.ppermute(value, axis, [(i, (i + step) % n) for i in range(n)])


def around(value, axis, dim, width):
    length = value.shape[dim]
    before = ring(lax.slice_in_dim(value, length - width, length, axis=dim), axis, 1)
    after = ring(lax.slice_in_dim(value, 0, width, axis=dim), axis, -1)
    return before, after


def per_device(positions, velocities, counts, grid_cells, electron_temp):
    nx, ny, nz = counts.shape
    slot = lax.broadcasted_iota(jnp.int32, grid_cells.shape, 3)
    occupied = slot < counts[..., None]
    blocks = electron_temp.reshape(2 * nx, 1, -1, 4)
    wide = jnp.concatenate([jnp.roll(blocks, 1, 2), blocks, jnp.roll(blocks, -1, 2)], -1)
    wide = wide.reshape(2 * nx, 1, -1)
    e = lax.all_to_all(wide, "gz", split_axis=2, concat_axis=1, tiled=True)
    e = e.reshape(2 * nx, ny, 2, 6, 2).transpose(1, 3, 0, 2, 4).reshape(ny, 6, 8 * nx)
    kinetic = jnp.where(occupied, 0.5 * jnp.sum(velocities * velocities, axis=0), 0.0)
    sub = lax.broadcasted_iota(jnp.int32, (nx, ny, nz, 8, 128), 3)
    lat = jnp.sum(jnp.where(grid_cells[..., None, :] == sub, kinetic[..., None, :], 0.0), axis=-1)
    lat = lat.transpose(1, 2, 0, 3).reshape(1, ny, nz, 8 * nx)
    lat = jnp.pad(lat, ((0, 0), (0, 0), (0, 0), (0, 128 - 8 * nx)))
    parked = jnp.where(occupied[None], positions, 1000.0).reshape(3 * nx, ny, nz, 128)
    planes = jnp.concatenate([parked, lat], 0)
    before, after = around(planes, "gz", 2, 2)
    planes = jnp.concatenate([before, planes, after], 2)
    pos = planes[:3 * nx].reshape(3, nx, ny, 6, 128)
    field = jnp.concatenate([planes[3 * nx, ..., :8 * nx], e], -1)
    field = jnp.pad(field, ((0, 0), (0, 0), (0, 128 - 16 * nx)))[None]
    before = ring(jnp.concatenate([pos[:, -1], field], 0), "gx", 1)
    after = ring(jnp.concatenate([pos[:, 0], field], 0), "gx", -1)
    pos = jnp.concatenate([before[:3, None], pos, after[:3, None]], 1)
    three = [before[3], field[0], after[3]]
    gap = jnp.zeros((ny, 6, 64 - 24 * nx), F32)
    w = 8 * nx
    row = jnp.concatenate([t[..., w:2 * w] for t in three] + [gap] + [t[..., :w] for t in three] + [gap], -1)
    planes = jnp.concatenate([pos.reshape(3 * nx + 6, ny, 6, 128), row[None]], 0)
    before, after = around(planes, "gy", 1, 2)
    planes = jnp.concatenate([before, planes, after], 1)
    pos = planes[:-1].reshape(3, nx + 2, ny + 4, 6, 128)
    e_new, diff = diffuse_call(planes[-1])
    slopes, te = density_call(pos)
    s_before, s_after = around(slopes, "gx", 0, 1)
    slopes = jnp.concatenate([s_before, slopes, s_after], 0)
    heat = e_new.reshape(ny + 4, 6, 128)[2:-2, 2:-2, w:2 * w].reshape(ny, nz, 2 * nx, 2, 2)
    heat = heat.transpose(2, 0, 3, 1, 4).reshape(2 * nx, 2 * ny, 2 * nz)
    heat = lax.all_to_all(heat, "gz", split_axis=1, concat_axis=2, tiled=True)
    velocity_out = force_call(pos, te, slopes, velocities, jnp.where(occupied, grid_cells, 8), diff)
    return velocity_out, heat


def solution(mesh):
    return jax.shard_map(
        per_device,
        mesh=mesh,
        in_specs=(
            P(None, "gx", "gy", "gz", None),
            P(None, "gx", "gy", "gz", None),
            P("gx", "gy", "gz"),
            P("gx", "gy", "gz", None),
            P("gx", ("gy", "gz"), None),
        ),
        out_specs=(P(None, "gx", "gy", "gz", None), P("gx", ("gy", "gz"), None)),
        check_vma=False,
    )
```

time: 174 us -> 140 us (0.80)
  Pallas kernels: 92.9 us -> 50.5 us
  blocking collectives: 0 us -> 13.7 us
  waiting for transfers between devices: 20.3 us -> 14 us
  starting transfers between devices: 48.3 us -> 42.6 us
  local copies, waits for them, and re-layouts: 6.88 us -> 12.5 us
    pallas_call x2 -> x3, Pallas kernels: 92.9 us -> 50.5 us  [the longest x1 30.5 us: density_call(): pl.pallas_call(functools.partial(density_kernel, (EX, EY, EZ)), out_shape...]
    all_to_all x0 -> x1, blocking collectives: none -> 13.7 us  [per_device(): e = lax.all_to_all(wide, 'gz', split_axis=2, concat_axis=1, tiled=True)]
    all_to_all x1 -> x0, starting transfers between devices: 9.19 us -> none  [per_device(): lax.all_to_all(electron_temp, 'gz', split_axis=2, concat_axis=1, tiled=True)]
    ppermute x6 -> x8, starting transfers between devices: 31 us -> 39.1 us  [ring(): return lax.ppermute(value, axis, [(i, (i + step) % n) for i in range(n)])]
    unnamed x4 -> x19, local copies, waits for them, and re-layouts: 2.16 us -> 9.2 us
    all_to_all x1, starting transfers between devices: 8.15 us -> 3.5 us  [per_device(): heat = lax.all_to_all(heat, 'gz', split_axis=1, concat_axis=2, tiled=True)]
    all_to_all x1 -> x0, waiting for transfers between devices: 3.31 us -> none  [per_device(): lax.all_to_all(electron_temp, 'gz', split_axis=2, concat_axis=1, tiled=True)]
    ppermute x6 -> x8, waiting for transfers between devices: 17 us -> 14 us  [ring(): return lax.ppermute(value, axis, [(i, (i + step) % n) for i in range(n)])]
  transfers between devices with their start and end apart: 8 -> 9, of which waited for: 6 -> 5; matrix products, arithmetic and copies ran while one was open for 3% -> 2% of each run, Pallas kernels for 52% -> 22%
where the time goes in v2:
time: 140 us; the launch traced here: 139 us
  Pallas kernels  50.5 us (36%)
  starting transfers between devices  42.6 us (30%)
  waiting for transfers between devices  14 us (10%)
  blocking collectives  13.7 us (10%)
  local copies, waits for them, and re-layouts  12.5 us (9%)
  other arithmetic  4.42 us (3%)
    ppermute x8, starting transfers between devices, ring(): return lax.ppermute(value, axis, [(i, (i + step) % n) for i in range(n)])  39.1 us
    pallas_call x1, Pallas kernels, density_call(): pl.pallas_call(functools.partial(density_kernel, (EX, EY, EZ)), out_shape...  30.5 us
    pallas_call x1, Pallas kernels, force_call(): pl.pallas_call(functools.partial(force_kernel, (EX, EY, EZ)), out_shape=j...  18 us
    ppermute x8, waiting for transfers between devices, ring(): return lax.ppermute(value, axis, [(i, (i + step) % n) for i in range(n)])  14 us
    all_to_all x1, blocking collectives, per_device(): e = lax.all_to_all(wide, 'gz', split_axis=2, concat_axis=1, tiled=True)  13.7 us
    unnamed x19, local copies, waits for them, and re-layouts  9.2 us
    all_to_all x1, starting transfers between devices, per_device(): heat = lax.all_to_all(heat, 'gz', split_axis=1, concat_axis=2, tiled=True)  3.5 us
  transfers between devices with their start and end apart: 9, of which 5 were waited for; matrix products, arithmetic and copies ran while one was open for 2% of the time, Pallas kernels for 22%

profile of v2, /device:TPU:1, one launch (start us, length us, event | category | flops | bytes accessed | tf_op | source)
XLA Modules:
  0.0 138.8 jit_solution(7006050129450579071)
XLA Ops:
  0.7 0.8 copy.71
  1.6 0.8 multiply_reduce_fusion
  2.5 0.8 select_reduce_fusion
  3.5 0.8 broadcast_select_fusion
  4.3 9.5 %collective-permute-start.1 = (f32[7,8,2,128]{3,1,2,0:T(8,128)S(1)}, f32[7,8,2,128]{3,1,2,0:T(8,128)S(1)}, u32[]{:S(2)}, u32[]{:S(2)}) collective-permute-start(f32[7,8,2,128]{3,1,2,0:T(8,128)S(1)} %pad_maximum_fusion.6), channel_id=1, source_target_pairs={{0,15},{1,0},{2,1},{3,2},{4,3},{5,4},{6,5},{7,6},{8,7},{9,8},{10,9... | collective-permute-start | bytes 172040 | tf_op jit(solution)/shard_map/ppermute | solution.py:295
  13.9 1.9 %collective-permute-start = (f32[7,8,2,128]{3,1,2,0:T(8,128)S(1)}, f32[7,8,2,128]{3,1,2,0:T(8,128)S(1)}, u32[]{:S(2)}, u32[]{:S(2)}) collective-permute-start(f32[7,8,2,128]{3,1,2,0:T(8,128)S(1)} %pad_maximum_fusion.6), channel_id=1, source_target_pairs={{0,1},{1,2},{2,3},{3,4},{4,5},{5,6},{6,7},{7,8},{8,9},{9,10},{10,1... | collective-permute-start | bytes 172040 | tf_op jit(solution)/shard_map/ppermute | solution.py:295
  15.8 0.5 broadcast.31
  16.3 1.3 reduce.3
  18.0 0.1 copy.75
  18.1 13.7 %all_to_all.21 = f32[4,1,192]{0,1,2:T(1,128)S(1)} all-to-all(f32[4,1,192]{0,1,2:T(1,128)S(1)} %copy.75), channel_id=1, replica_groups=mesh['gx'=4,'gy'=8,'gz'=16] {'gz'}, dimensions={2} | all-to-all | bytes 6144 | tf_op jit(solution)/shard_map/all_to_all | solution.py:312
  31.8 0.2 copy.76
  32.3 3.1 %collective-permute-start.2 = (f32[4,8,6,128]{3,1,2,0:T(8,128)S(1)}, f32[4,8,6,128]{3,1,2,0:T(8,128)S(1)}, u32[]{:S(2)}, u32[]{:S(2)}) collective-permute-start(f32[4,8,6,128]{3,1,2,0:T(8,128)S(1)} %get-tuple-element.32), channel_id=1, source_target_pairs={{0,128},{128,256},{256,384},{384,0},{1,129},{129,257},{257,385},{3... | collective-permute-start | bytes 294920 | tf_op jit(solution)/shard_map/ppermute | solution.py:295
  35.4 3.4 %collective-permute-start.3 = (f32[4,8,6,128]{3,1,2,0:T(8,128)S(1)}, f32[4,8,6,128]{3,1,2,0:T(8,128)S(1)}, u32[]{:S(2)}, u32[]{:S(2)}) collective-permute-start(f32[4,8,6,128]{3,1,2,0:T(8,128)S(1)} %get-tuple-element.33), channel_id=1, source_target_pairs={{0,384},{128,0},{256,128},{384,256},{1,385},{129,1},{257,129},{385... | collective-permute-start | bytes 294920 | tf_op jit(solution)/shard_map/ppermute | solution.py:295
  38.9 1.8 %collective-permute-done.3 = f32[4,8,6,128]{3,1,2,0:T(8,128)S(1)} collective-permute-done((f32[4,8,6,128]{3,1,2,0:T(8,128)S(1)}, f32[4,8,6,128]{3,1,2,0:T(8,128)S(1)}, u32[]{:S(2)}, u32[]{:S(2)}) %collective-permute-start.3) | collective-permute-done | bytes 98336 | tf_op jit(solution)/shard_map/ppermute | solution.py:295
  41.2 12.8 %collective-permute-start.4 = (f32[13,2,6,128]{3,2,1,0:T(8,128)S(1)}, f32[13,2,6,128]{3,2,1,0:T(8,128)S(1)}, u32[]{:S(2)}, u32[]{:S(2)}) collective-permute-start(f32[13,2,6,128]{3,2,1,0:T(8,128)S(1)} %get-tuple-element.18), channel_id=1, source_target_pairs={{0,16},{16,32},{32,48},{48,64},{64,80},{80,96},{96,112},{112,0},{1... | collective-permute-start | bytes 239624 | tf_op jit(solution)/shard_map/ppermute | solution.py:295
  53.9 1.9 %collective-permute-start.5 = (f32[13,2,6,128]{3,2,1,0:T(8,128)S(1)}, f32[13,2,6,128]{3,2,1,0:T(8,128)S(1)}, u32[]{:S(2)}, u32[]{:S(2)}) collective-permute-start(f32[13,2,6,128]{3,2,1,0:T(8,128)S(1)} %get-tuple-element.19), channel_id=1, source_target_pairs={{0,112},{16,0},{32,16},{48,32},{64,48},{80,64},{96,80},{112,96},{1... | collective-permute-start | bytes 239624 | tf_op jit(solution)/shard_map/ppermute | solution.py:295
  55.9 11.4 %collective-permute-done.5 = f32[13,2,6,128]{3,2,1,0:T(8,128)S(1)} collective-permute-done((f32[13,2,6,128]{3,2,1,0:T(8,128)S(1)}, f32[13,2,6,128]{3,2,1,0:T(8,128)S(1)}, u32[]{:S(2)}, u32[]{:S(2)}) %collective-permute-start.5) | collective-permute-done | bytes 79904 | tf_op jit(solution)/shard_map/ppermute | solution.py:295
  67.3 0.6 reshape_squeeze.3.x_ref
  68.0 1.9 %diffusion.1 = (f32[72,128]{1,0:T(8,128)}, f32[72,128]{1,0:T(8,128)}) custom-call(f32[72,128]{1,0:T(8,128)} %reshape_squeeze.3.x_ref), custom_call_target="tpu_custom_call" | custom-call | tf_op jit(solution)/shard_map/diffusion/pallas_call | solution.py:283
  70.0 0.8 reshape.70
  70.9 0.1 copy.85
  71.0 0.6 copy.86
  71.7 3.5 %all-to-all-start.1 = ((f32[4,16,4]{0,2,1:T(4,128)}), f32[4,16,4]{0,2,1:T(4,128)S(1)}, u32[]{:S(2)}, u32[]{:S(2)}) async-start(f32[4,16,4]{0,2,1:T(4,128)} %copy.86), calls=%async_computation.1 | async-start | bytes 65536 | tf_op jit(solution)/shard_map/all_to_all | solution.py:343
  75.2 30.5 %density.1 = (f32[2,12,6,128]{3,2,1,0:T(8,128)S(1)}, bf16[240,128,128]{2,1,0:T(8,128)(2,1)S(1)}) custom-call(f32[3,4,12,6,128]{4,3,2,1,0:T(8,128)S(1)} %bitcast.45, f32[27,8,128]{2,1,0:T(8,128)S(1)} %copy-done.3, f32[27,8,128]{2,1,0:T(8,128)S(1)} %copy-done.2), custom_call_target="tpu_custom_call" | custom-call | tf_op jit(solution)/shard_map/density/pallas_call | solution.py:151
  105.7 3.0 %copy-done = bf16[240,128,128]{2,1,0:T(8,128)(2,1)} copy-done((bf16[240,128,128]{2,1,0:T(8,128)(2,1)}, bf16[240,128,128]{2,1,0:T(8,128)(2,1)S(1)}, u32[]{:S(2)}) %copy-start) | copy-done | bytes 7864344
  108.7 3.1 %collective-permute-start.6 = (f32[1,12,6,128]{3,2,1,0:T(8,128)S(1)}, f32[1,12,6,128]{3,2,1,0:T(8,128)S(1)}, u32[]{:S(2)}, u32[]{:S(2)}) collective-permute-start(f32[1,12,6,128]{3,2,1,0:T(8,128)S(1)} %get-tuple-element.22), channel_id=1, source_target_pairs={{0,128},{128,256},{256,384},{384,0},{1,129},{129,257},{257,385},{3... | collective-permute-start | bytes 110600 | tf_op jit(solution)/shard_map/ppermute | solution.py:295
  111.9 3.4 %collective-permute-start.7 = (f32[1,12,6,128]{3,2,1,0:T(8,128)S(1)}, f32[1,12,6,128]{3,2,1,0:T(8,128)S(1)}, u32[]{:S(2)}, u32[]{:S(2)}) collective-permute-start(f32[1,12,6,128]{3,2,1,0:T(8,128)S(1)} %get-tuple-element.23), channel_id=1, source_target_pairs={{0,384},{128,0},{256,128},{384,256},{1,385},{129,1},{257,129},{385... | collective-permute-start | bytes 110600 | tf_op jit(solution)/shard_map/ppermute | solution.py:295
  115.4 0.7 copy.88
  116.0 0.7 collective-permute-done.7
  116.7 3.2 %copy-done.1 = bf16[240,128,128]{2,1,0:T(8,128)(2,1)S(1)} copy-done((bf16[240,128,128]{2,1,0:T(8,128)(2,1)S(1)}, bf16[240,128,128]{2,1,0:T(8,128)(2,1)}, u32[]{:S(2)}) %copy-start.1) | copy-done | bytes 7864344
  120.0 0.8 copy-done.5
  120.7 18.0 %force.1 = f32[3,2,8,2,128]{4,3,2,1,0:T(2,128)} custom-call(f32[3,4,12,6,128]{4,3,2,1,0:T(8,128)S(1)} %bitcast.46, bf16[240,128,128]{2,1,0:T(8,128)(2,1)S(1)} %copy-done.1, f32[4,12,6,128]{3,2,1,0:T(8,128)S(1)} %pad_maximum_fusion.2.sl_ref, f32[3,2,8,2,128]{4,3,2,1,0:T(2,128)S(1)} %copy-done.4, s32[2,8,2,128]{3,2,1,0:T(2,128)S(1)} %broadcast_select_fusion.1.grid_ref, ...), custom_call_target="tpu_custom_call" | custom-call | tf_op jit(solution)/shard_map/force/pallas_call | solution.py:247
  (56 shorter events, 1.7 us)
Async XLA Ops:
  0.6 74.5 %copy-start.2 = (f32[27,8,128]{2,1,0:T(8,128)S(1)}, f32[27,8,128]{2,1,0:T(8,128)}, u32[]{:S(2)}) copy-start(f32[27,8,128]{2,1,0:T(8,128)} %constant.16.clone.k_ref) | copy-start | bytes 331780
  0.6 74.5 %copy-start.3 = (f32[27,8,128]{2,1,0:T(8,128)S(1)}, f32[27,8,128]{2,1,0:T(8,128)}, u32[]{:S(2)}) copy-start(f32[27,8,128]{2,1,0:T(8,128)} %constant.5.clone.m_ref) | copy-start | bytes 331780
  0.7 116.1 %copy-start.4 = (f32[3,2,8,2,128]{4,3,2,1,0:T(2,128)S(1)}, f32[3,2,8,2,128]{4,3,2,1,0:T(2,128)}, u32[]{:S(2)}) copy-start(f32[3,2,8,2,128]{4,3,2,1,0:T(2,128)} %vel_ref.1) | copy-start | bytes 147460
  0.7 114.6 %copy-start.6 = (s32[2,8,2,128]{3,2,1,0:T(2,128)S(1)}, s32[2,8,2,128]{3,2,1,0:T(2,128)}, u32[]{:S(2)}) copy-start(s32[2,8,2,128]{3,2,1,0:T(2,128)} %param.12) | copy-start | bytes 49156
  4.3 27.8 %collective-permute-start.1 = (f32[7,8,2,128]{3,1,2,0:T(8,128)S(1)}, f32[7,8,2,128]{3,1,2,0:T(8,128)S(1)}, u32[]{:S(2)}, u32[]{:S(2)}) collective-permute-start(f32[7,8,2,128]{3,1,2,0:T(8,128)S(1)} %pad_maximum_fusion.6), channel_id=1, source_target_pairs={{0,15},{1,0},{2,1},{3,2},{4,3},{5,4},{6,5},{7,6},{8,7},{9,8},{10,9... | collective-permute-start | bytes 172040 | tf_op jit(solution)/shard_map/ppermute | solution.py:295
  13.9 18.2 %collective-permute-start = (f32[7,8,2,128]{3,1,2,0:T(8,128)S(1)}, f32[7,8,2,128]{3,1,2,0:T(8,128)S(1)}, u32[]{:S(2)}, u32[]{:S(2)}) collective-permute-start(f32[7,8,2,128]{3,1,2,0:T(8,128)S(1)} %pad_maximum_fusion.6), channel_id=1, source_target_pairs={{0,1},{1,2},{2,3},{3,4},{4,5},{5,6},{6,7},{7,8},{8,9},{9,10},{10,1... | collective-permute-start | bytes 172040 | tf_op jit(solution)/shard_map/ppermute | solution.py:295
  32.3 6.6 %collective-permute-start.2 = (f32[4,8,6,128]{3,1,2,0:T(8,128)S(1)}, f32[4,8,6,128]{3,1,2,0:T(8,128)S(1)}, u32[]{:S(2)}, u32[]{:S(2)}) collective-permute-start(f32[4,8,6,128]{3,1,2,0:T(8,128)S(1)} %get-tuple-element.32), channel_id=1, source_target_pairs={{0,128},{128,256},{256,384},{384,0},{1,129},{129,257},{257,385},{3... | collective-permute-start | bytes 294920 | tf_op jit(solution)/shard_map/ppermute | solution.py:295
  35.4 5.4 %collective-permute-start.3 = (f32[4,8,6,128]{3,1,2,0:T(8,128)S(1)}, f32[4,8,6,128]{3,1,2,0:T(8,128)S(1)}, u32[]{:S(2)}, u32[]{:S(2)}) collective-permute-start(f32[4,8,6,128]{3,1,2,0:T(8,128)S(1)} %get-tuple-element.33), channel_id=1, source_target_pairs={{0,384},{128,0},{256,128},{384,256},{1,385},{129,1},{257,129},{385... | collective-permute-start | bytes 294920 | tf_op jit(solution)/shard_map/ppermute | solution.py:295
  41.2 14.8 %collective-permute-start.4 = (f32[13,2,6,128]{3,2,1,0:T(8,128)S(1)}, f32[13,2,6,128]{3,2,1,0:T(8,128)S(1)}, u32[]{:S(2)}, u32[]{:S(2)}) collective-permute-start(f32[13,2,6,128]{3,2,1,0:T(8,128)S(1)} %get-tuple-element.18), channel_id=1, source_target_pairs={{0,16},{16,32},{32,48},{48,64},{64,80},{80,96},{96,112},{112,0},{1... | collective-permute-start | bytes 239624 | tf_op jit(solution)/shard_map/ppermute | solution.py:295
  53.9 13.4 %collective-permute-start.5 = (f32[13,2,6,128]{3,2,1,0:T(8,128)S(1)}, f32[13,2,6,128]{3,2,1,0:T(8,128)S(1)}, u32[]{:S(2)}, u32[]{:S(2)}) collective-permute-start(f32[13,2,6,128]{3,2,1,0:T(8,128)S(1)} %get-tuple-element.19), channel_id=1, source_target_pairs={{0,112},{16,0},{32,16},{48,32},{64,48},{80,64},{96,80},{112,96},{1... | collective-permute-start | bytes 239624 | tf_op jit(solution)/shard_map/ppermute | solution.py:295
  71.7 43.7 %all-to-all-start.1 = ((f32[4,16,4]{0,2,1:T(4,128)}), f32[4,16,4]{0,2,1:T(4,128)S(1)}, u32[]{:S(2)}, u32[]{:S(2)}) async-start(f32[4,16,4]{0,2,1:T(4,128)} %copy.86), calls=%async_computation.1 | async-start | bytes 65536 | tf_op jit(solution)/shard_map/all_to_all | solution.py:343
  105.7 3.0 %copy-start = (bf16[240,128,128]{2,1,0:T(8,128)(2,1)}, bf16[240,128,128]{2,1,0:T(8,128)(2,1)S(1)}, u32[]{:S(2)}) copy-start(bf16[240,128,128]{2,1,0:T(8,128)(2,1)S(1)} %get-tuple-element.6.te_ref) | copy-start | bytes 23592964
  108.7 7.3 %collective-permute-start.6 = (f32[1,12,6,128]{3,2,1,0:T(8,128)S(1)}, f32[1,12,6,128]{3,2,1,0:T(8,128)S(1)}, u32[]{:S(2)}, u32[]{:S(2)}) collective-permute-start(f32[1,12,6,128]{3,2,1,0:T(8,128)S(1)} %get-tuple-element.22), channel_id=1, source_target_pairs={{0,128},{128,256},{256,384},{384,0},{1,129},{129,257},{257,385},{3... | collective-permute-start | bytes 110600 | tf_op jit(solution)/shard_map/ppermute | solution.py:295
  111.9 4.8 %collective-permute-start.7 = (f32[1,12,6,128]{3,2,1,0:T(8,128)S(1)}, f32[1,12,6,128]{3,2,1,0:T(8,128)S(1)}, u32[]{:S(2)}, u32[]{:S(2)}) collective-permute-start(f32[1,12,6,128]{3,2,1,0:T(8,128)S(1)} %get-tuple-element.23), channel_id=1, source_target_pairs={{0,384},{128,0},{256,128},{384,256},{1,385},{129,1},{257,129},{385... | collective-permute-start | bytes 110600 | tf_op jit(solution)/shard_map/ppermute | solution.py:295
  116.7 3.2 %copy-start.1 = (bf16[240,128,128]{2,1,0:T(8,128)(2,1)S(1)}, bf16[240,128,128]{2,1,0:T(8,128)(2,1)}, u32[]{:S(2)}) copy-start(bf16[240,128,128]{2,1,0:T(8,128)(2,1)} %copy-done) | copy-start | bytes 23592964
  120.0 0.8 copy-start.5

commit v3 on v2

v3 whole, which is shorter than its diff:
```python
import functools
import numpy as np
import jax
import jax.numpy as jnp
from jax import lax
from jax.experimental import pallas as pl
from jax.experimental.pallas import tpu as pltpu
from jax.sharding import PartitionSpec as P

CUT = 30.25
EDGE = 11.0
HALF = 5.5
BIG = 10000.0
GROUP = 4
F32 = jnp.float32
BF = jnp.bfloat16
VM = pl.BlockSpec(memory_space=pltpu.VMEM)
SHIFTS = [(x, y, z) for x in (-1, 0, 1) for y in (-1, 0, 1) for z in (-1, 0, 1)]


def split3(v):
    hi = v.astype(BF).astype(F32)
    rest = v - hi
    mid = rest.astype(BF).astype(F32)
    return hi, mid, rest - mid


def shift_tables():
    m = np.zeros((27, 8, 128), np.float32)
    k = np.zeros((27, 8, 128), np.float32)
    for n, o in enumerate(SHIFTS):
        m[n, 0:5] = 1.0
        for a in range(3):
            m[n, 5 + a] = o[a]
            k[n, a] = -2.0 * EDGE * o[a]
            k[n, 4] -= EDGE * EDGE * abs(o[a])
    return jnp.asarray(m), jnp.asarray(k)


def cell_rows(pos_ref, x, y, z):
    px = pos_ref[x, y, pl.ds(z, 1), :]
    py = pos_ref[4 + x, y, pl.ds(z, 1), :]
    pz = pos_ref[8 + x, y, pl.ds(z, 1), :]
    empty = px > 500.0
    qx = jnp.where(empty, 0.0, px - HALF)
    qy = jnp.where(empty, 0.0, py - HALF)
    qz = jnp.where(empty, 0.0, pz - HALF)
    s = jnp.where(empty, BIG, qx * qx + qy * qy + qz * qz)
    return [jnp.broadcast_to(v, (8, 128)) for v in (qx, qy, qz, s)]


def pick(row, *vals):
    out = vals[-1]
    for n in range(len(vals) - 2, -1, -1):
        out = jnp.where(row == n, vals[n], out)
    return out


def neighbour_block(row, rows):
    qx, qy, qz, s = rows
    hi, mid, lo = split3(pick(row, qx, qy, qz, s, jnp.float32(1.0), jnp.float32(2.0 * EDGE)))
    return jnp.concatenate([hi, mid, lo, hi, mid, hi, jnp.zeros_like(hi), jnp.zeros_like(hi)], axis=0)


def centre_block(row, rows):
    qx, qy, qz, s = rows
    return pick(row, 2.0 * qx, 2.0 * qy, 2.0 * qz, jnp.float32(-1.0), CUT - s, qx, qy, qz)


def weights(d, m, k):
    u1, u2, u3 = split3(d * m + k)
    z = jnp.zeros((16, 128), BF)
    c = lambda p, q: jnp.concatenate([p, q], axis=0).astype(BF)
    return jnp.concatenate([c(u1, u1), c(u1, u2), c(u2, u3), z], axis=0)


def dot(a, b):
    return jnp.dot(a, b, preferred_element_type=F32)


def pair_values(table, c0, c1):
    z = jnp.zeros((64, 128), BF)
    rhs = jnp.concatenate([jnp.concatenate([c0, z], 0), jnp.concatenate([z, c1], 0)], 1)
    return jnp.maximum(dot(table, rhs), 0.0)


def same_slot():
    return lax.broadcasted_iota(jnp.int32, (128, 128), 0) == lax.broadcasted_iota(jnp.int32, (128, 128), 1)


TABLES = ((0, 1), (2, 1), (2, 3))
DENSITY_TILES = ((0, 0, 1), (0, 1, 0), (1, 1, 2), (2, 2, 3), (2, 3, 2))
FORCE_TILES = ((0, 1, 1), (1, 1, 2), (2, 2, 2))


def main_kernel(own_ref, xb_ref, xa_ref, yb_ref, ya_ref, vel_ref, sub_ref, diff_ref, m_ref, k_ref,
                out_ref, pos_ref, te_ref, cen_ref, sl_ref, g_ref):
    NX, NY = 4, 10
    row = lax.broadcasted_iota(jnp.int32, (8, 128), 0)
    low = lax.broadcasted_iota(jnp.int32, (128, 128), 1) < 64
    diag = same_slot()
    for a in range(3):
        pos_ref[4 * a, 1:9] = xb_ref[a]
        pos_ref[4 * a + 1, 1:9] = own_ref[2 * a]
        pos_ref[4 * a + 2, 1:9] = own_ref[2 * a + 1]
        pos_ref[4 * a + 3, 1:9] = xa_ref[a]
    pos_ref[:, 0] = yb_ref[0:12]
    pos_ref[:, 9] = ya_ref[0:12]

    def prep(n, carry):
        x = n // NY
        y = n % NY
        blocks = []
        for z in range(4):
            rows = cell_rows(pos_ref, x, y, z + 1)
            blocks.append(neighbour_block(row, rows))
            cen_ref[(x * NY + y) * 4 + z] = centre_block(row, rows)
        a = jnp.concatenate(blocks[:2], 0).T
        b = jnp.concatenate(blocks[2:], 0).T
        base = (x * (NY + 2) + y + 1) * 3
        te_ref[base] = a.astype(BF)
        te_ref[base + 1] = jnp.where(low, b, a).astype(BF)
        te_ref[base + 2] = b.astype(BF)
        return carry

    lax.fori_loop(0, NX * NY, prep, 0)
    for x in range(NX):
        for y in (0, NY + 1):
            te_ref[pl.ds((x * (NY + 2) + y) * 3, 3)] = jnp.zeros((3, 128, 128), BF)

    def dens(y, carry):
        for x in range(NX):
            centres = [cen_ref[(x * NY + y) * 4 + z] for z in range(4)]
            acc = [jnp.zeros((8, 128), F32) for z in range(4)]
            for ox in (-1, 0, 1):
                if not 0 <= x + ox < NX:
                    continue
                for oy in (-1, 0, 1):
                    base = ((x + ox) * (NY + 2) + y + 1 + oy) * 3
                    for t, ca, cb in DENSITY_TILES:
                        w = []
                        for half, c in ((0, ca), (1, cb)):
                            o = SHIFTS.index((ox, oy, TABLES[t][half] - c))
                            w.append(weights(centres[c], m_ref[o], k_ref[o]))
                        r = pair_values(te_ref[base + t], *w)
                        r3 = r * r * r
                        for half, c in ((0, ca), (1, cb)):
                            part = r3[:, 128 * half:128 * half + 128]
                            if (ox, oy) == (0, 0) and TABLES[t][half] == c:
                                part = jnp.where(diag, 0.0, part)
                            acc[c] = acc[c] + part.reshape(16, 8, 128).sum(0)
            for z in range(4):
                d = jnp.sum(acc[z], axis=0, keepdims=True) * (1.0 / CUT ** 3)
                sl_ref[x, y, pl.ds(z, 1), :] = -0.5 / jnp.sqrt(d + 1.0)
        return carry

    lax.fori_loop(0, NY, dens, 0)

    def gprep(n, carry):
        x = n // NY
        y = n % NY
        for z in range(4):
            qx, qy, qz, _ = cell_rows(pos_ref, x, y, z + 1)
            s = jnp.broadcast_to(sl_ref[x, y, pl.ds(z, 1), :], (8, 128))
            v = pick(row % 4, qx, qy, qz, jnp.ones_like(qx))
            hi, mid, lo = split3(v * jnp.where(row < 4, 1.0, s))
            g_ref[n * 4 + z] = jnp.concatenate([hi, mid, lo, jnp.zeros_like(hi)], 0).astype(BF)
        return carry

    lax.fori_loop(0, NX * NY, gprep, 0)

    def force(n, carry):
        x = n // (8 // GROUP) + 1
        first = n % (8 // GROUP) * GROUP + 1
        zero = jnp.zeros((8, 128), F32)
        acc = [[[zero] * 4, [zero] * 4] for c in range(GROUP)]
        for ox in (-1, 0, 1):
            for oy in (-1, 0, 1):
                for c in range(GROUP):
                    y = first + c
                    col = (x + ox) * NY + y + oy
                    base = ((x + ox) * (NY + 2) + y + 1 + oy) * 3
                    for t, ca, cb in FORCE_TILES:
                        w = []
                        for half, z in ((0, ca), (1, cb)):
                            o = SHIFTS.index((ox, oy, TABLES[t][half] - z))
                            w.append(weights(cen_ref[(x * NY + y) * 4 + z], m_ref[o], k_ref[o]))
                        r = pair_values(te_ref[base + t], *w)
                        for half, z in ((0, ca), (1, cb)):
                            layer = TABLES[t][half]
                            shift = (ox, oy, layer - z)
                            p = r[:, 128 * half:128 * half + 128]
                            if shift == (0, 0, 0):
                                p = jnp.where(diag, 0.0, p)
                            p = p * p
                            hi = p.astype(BF)
                            lo = (p - hi.astype(F32)).astype(BF)
                            g = g_ref[col * 4 + layer]
                            f = dot(jnp.concatenate([g, g], 1), jnp.concatenate([hi, lo], 0))
                            f = f[0:8] + f[8:16] + f[16:24]
                            total = acc[c][z - 1]
                            total[0] = total[0] + f
                            for a in range(3):
                                if shift[a] == 1:
                                    total[a + 1] = total[a + 1] + f
                                elif shift[a] == -1:
                                    total[a + 1] = total[a + 1] - f
        for c, h in [(c, h) for c in range(GROUP) for h in range(2)]:
            y = first + c
            total = acc[c][h]
            rows = cell_rows(pos_ref, x, y, h + 2)
            s = sl_ref[x, y, pl.ds(h + 1, 1), :]
            sub = sub_ref[x - 1, y - 1, pl.ds(h, 1), :]
            both = diff_ref[pl.ds((y + 1) * 6 + 2 + h, 1), :]
            here = jnp.where(x == 1, both[:, 16:24], both[:, 24:32])
            heat = jnp.zeros((1, 128), F32)
            for kk in range(8):
                heat = jnp.where(sub == kk, here[:, kk:kk + 1], heat)
            for a in range(3):
                q = rows[a][0:1]
                plain = total[0][a:a + 1] + EDGE * total[1 + a][3:4] - q * total[0][3:4]
                sloped = total[0][4 + a:5 + a] + EDGE * total[1 + a][7:8] - q * total[0][7:8]
                f = (2.0 / CUT ** 2) * ((-3.0 / CUT) * (s * plain + sloped) + (-1.5 / CUT) * plain)
                v = vel_ref[a, x - 1, y - 1, pl.ds(h, 1), :]
                moved = v + 0.2 * f + 0.02 * heat * v
                out_ref[a, x - 1, y - 1, pl.ds(h, 1), :] = jnp.where(sub < 8, moved, 0.0)
        return carry

    lax.fori_loop(0, 16 // GROUP, force, 0)


def main_call(own, xb, xa, yb, ya, vel, sub, diff):
    m, k = shift_tables()
    return pl.pallas_call(
        main_kernel,
        out_shape=jax.ShapeDtypeStruct(vel.shape, F32),
        in_specs=[VM] * 10,
        out_specs=VM,
        scratch_shapes=[
            pltpu.VMEM((12, 10, 6, 128), F32),
            pltpu.VMEM((4 * 12 * 3, 128, 128), BF),
            pltpu.VMEM((160, 8, 128), F32),
            pltpu.VMEM((4, 10, 4, 128), F32),
            pltpu.VMEM((160, 32, 128), BF),
        ],
        compiler_params=pltpu.CompilerParams(vmem_limit_bytes=24 * 2 ** 20),
        name="pair_forces",
    )(own, xb, xa, yb, ya, vel, sub, diff, m, k)


def pack_kernel(own_ref, e_ref, xb_ref, xa_ref, up_ref, down_ref, mid_ref):
    lane = lax.broadcasted_iota(jnp.int32, (6, 128), 1)
    for y in range(8):
        lat = own_ref[6, y]
        mine = e_ref[y]
        e_part = jnp.where(lane < 16, pltpu.roll(xb_ref[3, y], 112, 1),
                           jnp.where(lane < 32, mine, pltpu.roll(xa_ref[3, y], 16, 1)))
        l_part = jnp.where(lane < 80, pltpu.roll(xb_ref[3, y], 64, 1),
                           jnp.where(lane < 96, pltpu.roll(lat, 80, 1), pltpu.roll(xa_ref[3, y], 96, 1)))
        used = (lane < 48) | ((lane >= 64) & (lane < 112))
        mid_ref[y] = jnp.where(used, jnp.where(lane < 64, e_part, l_part), 0.0)
    for ref, y in ((up_ref, 7), (down_ref, 0)):
        for a in range(3):
            ref[4 * a] = xb_ref[a, y]
            ref[4 * a + 1] = own_ref[2 * a, y]
            ref[4 * a + 2] = own_ref[2 * a + 1, y]
            ref[4 * a + 3] = xa_ref[a, y]
        for n in range(2):
            ref[12 + n] = mid_ref[(y // 7) * 6 + n]


def pack_call(own, e, xb, xa):
    message = jax.ShapeDtypeStruct((14, 6, 128), F32)
    return pl.pallas_call(
        pack_kernel,
        out_shape=(message, message, jax.ShapeDtypeStruct((8, 6, 128), F32)),
        in_specs=[VM] * 4,
        out_specs=(VM, VM, VM),
        compiler_params=pltpu.CompilerParams(vmem_limit_bytes=2 * 2 ** 20),
        name="pack",
    )(own, e, xb, xa)


def diffuse_kernel(mid_ref, yb_ref, ya_ref, e_out, diff_out, x_ref, e_ref):
    for n in range(2):
        x_ref[pl.ds(6 * n, 6)] = yb_ref[12 + n]
        x_ref[pl.ds(60 + 6 * n, 6)] = ya_ref[12 + n]
    for y in range(8):
        x_ref[pl.ds(12 + 6 * y, 6)] = mid_ref[y]
    rows = 72
    own = x_ref[...]
    lane = lax.broadcasted_iota(jnp.int32, (rows, 128), 1)
    lat = pltpu.roll(own, 64, 1)
    e = own
    e_ref[...] = jnp.zeros(e_ref.shape, F32)
    for step in range(4):
        e_ref[pl.ds(8, rows), :] = e
        beside = pltpu.roll(e, 4, 1) + pltpu.roll(e, 124, 1)
        for bit, stride in ((1, 1), (2, 6)):
            after = e_ref[pl.ds(8 + stride, rows), :]
            before = e_ref[pl.ds(8 - stride, rows), :]
            low = pltpu.roll(e + before, 128 - bit, 1)
            high = pltpu.roll(e + after, bit, 1)
            beside = beside + jnp.where((lane & bit) == 0, low, high)
        e = e + 0.15 * (beside - 6.0 * e) - 0.05 * (e - lat)
    e_ref[pl.ds(8, rows), :] = e
    for y in range(8):
        e_out[y] = e_ref[pl.ds(8 + 6 * (y + 2) + 2, 2), :]
    diff_out[...] = e - lat


def diffuse_call(mid, yb, ya):
    return pl.pallas_call(
        diffuse_kernel,
        out_shape=(jax.ShapeDtypeStruct((8, 2, 128), F32), jax.ShapeDtypeStruct((72, 128), F32)),
        in_specs=[VM] * 3,
        out_specs=(VM, VM),
        scratch_shapes=[pltpu.VMEM((72, 128), F32), pltpu.VMEM((88, 128), F32)],
        compiler_params=pltpu.CompilerParams(vmem_limit_bytes=2 * 2 ** 20),
        name="diffusion",
    )(mid, yb, ya)


def ring(value, axis, step):
    n = lax.axis_size(axis)
    return lax.ppermute(value, axis, [(i, (i + step) % n) for i in range(n)])


def per_device(positions, velocities, counts, grid_cells, electron_temp):
    nx, ny, nz = counts.shape
    slot = lax.broadcasted_iota(jnp.int32, grid_cells.shape, 3)
    occupied = slot < counts[..., None]
    shifted = [jnp.roll(electron_temp, 4, 2), electron_temp, jnp.roll(electron_temp, -4, 2)]
    e = lax.all_to_all(jnp.concatenate(shifted, 0), "gz", split_axis=2, concat_axis=1, tiled=True)
    e = e.reshape(3, 4, ny, 2, nz, 2).transpose(2, 0, 4, 1, 3, 5).reshape(ny, 6, 16)
    e = jnp.pad(e, ((0, 0), (0, 0), (16, 96)))
    kinetic = jnp.where(occupied, 0.5 * jnp.sum(velocities * velocities, axis=0), 0.0)
    sub = lax.broadcasted_iota(jnp.int32, (nx, ny, nz, 8, 128), 3)
    lat = jnp.sum(jnp.where(grid_cells[..., None, :] == sub, kinetic[..., None, :], 0.0), axis=-1)
    lat = lat.transpose(1, 2, 0, 3).reshape(1, ny, nz, 16)
    lat = jnp.pad(lat, ((0, 0), (0, 0), (0, 0), (0, 112)))
    parked = jnp.where(occupied[None], positions, 1000.0).reshape(6, ny, nz, 128)
    planes = jnp.concatenate([parked, lat], 0)
    own = jnp.concatenate([ring(planes, "gz", 1), planes, ring(planes, "gz", -1)], 2)
    field = (own[6] + e)[None]
    xb = ring(jnp.concatenate([own[1:6:2], field], 0), "gx", 1)
    xa = ring(jnp.concatenate([own[0:6:2], field], 0), "gx", -1)
    up, down, mid = pack_call(own, e, xb, xa)
    yb = ring(up, "gy", 1)
    ya = ring(down, "gy", -1)
    e_new, diff = diffuse_call(mid, yb, ya)
    heat = e_new[..., 16:32].reshape(ny, nz, 4, 2, 2).transpose(2, 0, 3, 1, 4).reshape(4, 2 * ny, 2 * nz)
    heat = lax.all_to_all(heat, "gz", split_axis=1, concat_axis=2, tiled=True)
    vel_out = main_call(own, xb, xa, yb, ya, velocities, jnp.where(occupied, grid_cells, 8), diff)
    return vel_out, heat


def solution(mesh):
    return jax.shard_map(
        per_device,
        mesh=mesh,
        in_specs=(
            P(None, "gx", "gy", "gz", None),
            P(None, "gx", "gy", "gz", None),
            P("gx", "gy", "gz"),
            P("gx", "gy", "gz", None),
            P("gx", ("gy", "gz"), None),
        ),
        out_specs=(P(None, "gx", "gy", "gz", None), P("gx", ("gy", "gz"), None)),
        check_vma=False,
    )
```

time: 140 us -> 123 us (0.88)
  local copies, waits for them, and re-layouts: 12.5 us -> 5.14 us
  Pallas kernels: 50.5 us -> 56.9 us
  starting transfers between devices: 42.6 us -> 36.3 us
  blocking collectives: 13.7 us -> 9.67 us
  waiting for transfers between devices: 14 us -> 11.5 us
  other arithmetic: 4.42 us -> 2.45 us
    pallas_call x3, Pallas kernels: 50.5 us -> 56.9 us  [the longest x1 56.3 us: main_call(): pl.pallas_call(main_kernel, out_shape=jax.ShapeDtypeStruct(vel.shape, F32...]
    ppermute x8 -> x6, starting transfers between devices: 39.1 us -> 32.7 us  [ring(): return lax.ppermute(value, axis, [(i, (i + step) % n) for i in range(n)])]
    unnamed x19 -> x15, local copies, waits for them, and re-layouts: 9.2 us -> 2.83 us
    all_to_all x1, blocking collectives: 13.7 us -> 9.67 us  [per_device(): lax.all_to_all(jnp.concatenate(shifted, 0), 'gz', split_axis=2, concat_ax...]
    ppermute x8 -> x6, waiting for transfers between devices: 14 us -> 11.5 us  [ring(): return lax.ppermute(value, axis, [(i, (i + step) % n) for i in range(n)])]
  transfers between devices with their start and end apart: 9 -> 7, of which waited for: 5 -> 3; matrix products, arithmetic and copies ran while one was open for 2% -> 2% of each run, Pallas kernels for 22% -> 46%
where the time goes in v3:
time: 123 us
  Pallas kernels  56.9 us (46%)
  starting transfers between devices  36.3 us (30%)
  waiting for transfers between devices  11.5 us (9%)
  blocking collectives  9.67 us (8%)
  local copies, waits for them, and re-layouts  5.14 us (4%)
  other arithmetic  2.45 us (2%)
    pallas_call x1, Pallas kernels, main_call(): pl.pallas_call(main_kernel, out_shape=jax.ShapeDtypeStruct(vel.shape, F32...  56.3 us
    ppermute x6, starting transfers between devices, ring(): return lax.ppermute(value, axis, [(i, (i + step) % n) for i in range(n)])  32.7 us
    ppermute x6, waiting for transfers between devices, ring(): return lax.ppermute(value, axis, [(i, (i + step) % n) for i in range(n)])  11.5 us
    all_to_all x1, blocking collectives, per_device(): lax.all_to_all(jnp.concatenate(shifted, 0), 'gz', split_axis=2, concat_ax...  9.67 us
    all_to_all x1, starting transfers between devices, per_device(): heat = lax.all_to_all(heat, 'gz', split_axis=1, concat_axis=2, tiled=True)  3.6 us
    unnamed x15, local copies, waits for them, and re-layouts  2.83 us
  transfers between devices with their start and end apart: 7, of which 3 were waited for; matrix products, arithmetic and copies ran while one was open for 2% of the time, Pallas kernels for 46%

profile of v3, /device:TPU:1, one launch (start us, length us, event | category | flops | bytes accessed | tf_op | source)
XLA Modules:
  0.0 122.9 jit_solution(16037760768865506339)
XLA Ops:
  0.6 0.8 copy.46
  1.4 0.8 multiply_reduce_fusion
  2.4 0.6 copy-done.3
  3.0 0.1 select_reduce_fusion
  3.2 0.1 reshape.44
  3.3 0.7 copy-done.5
  4.0 4.4 %collective-permute-start = (f32[7,8,2,128]{3,2,1,0:T(2,128)S(1)}, f32[7,8,2,128]{3,2,1,0:T(2,128)S(1)}, u32[]{:S(2)}, u32[]{:S(2)}) collective-permute-start(f32[7,8,2,128]{3,2,1,0:T(2,128)S(1)} %pad_maximum_fusion.3), channel_id=1, source_target_pairs={{0,1},{1,2},{2,3},{3,4},{4,5},{5,6},{6,7},{7,8},{8,9},{9,10},{10,1... | collective-permute-start | bytes 172040 | tf_op jit(solution)/shard_map/ppermute | solution.py:326
  8.4 7.1 %collective-permute-start.1 = (f32[7,8,2,128]{3,2,1,0:T(2,128)S(1)}, f32[7,8,2,128]{3,2,1,0:T(2,128)S(1)}, u32[]{:S(2)}, u32[]{:S(2)}) collective-permute-start(f32[7,8,2,128]{3,2,1,0:T(2,128)S(1)} %pad_maximum_fusion.3), channel_id=1, source_target_pairs={{0,15},{1,0},{2,1},{3,2},{4,3},{5,4},{6,5},{7,6},{8,7},{9,8},{10,9... | collective-permute-start | bytes 172040 | tf_op jit(solution)/shard_map/ppermute | solution.py:326
  15.7 0.1 copy.53
  15.8 0.1 copy.52
  15.9 0.1 copy.54
  16.0 0.2 pad_maximum_fusion.4
  16.2 9.7 %all_to_all.21 = f32[12,1,64]{0,1,2:T(1,128)S(1)} all-to-all(f32[12,1,64]{0,1,2:T(1,128)S(1)} %pad_maximum_fusion.4), channel_id=1, replica_groups=mesh['gx'=4,'gy'=8,'gz'=16] {'gz'}, dimensions={2} | all-to-all | bytes 6144 | tf_op jit(solution)/shard_map/all_to_all | solution.py:334
  25.9 0.5 broadcast.25
  26.4 0.7 reduce.3
  27.2 0.1 reshape.45
  27.3 0.2 copy.55
  27.6 0.1 pad_maximum_fusion.own_ref
  27.8 3.1 %collective-permute-start.2 = (f32[4,8,6,128]{3,2,1,0:T(8,128)S(1)}, f32[4,8,6,128]{3,2,1,0:T(8,128)S(1)}, u32[]{:S(2)}, u32[]{:S(2)}) collective-permute-start(f32[4,8,6,128]{3,2,1,0:T(8,128)S(1)} %get-tuple-element.25), channel_id=1, source_target_pairs={{0,128},{128,256},{256,384},{384,0},{1,129},{129,257},{257,385},{3... | collective-permute-start | bytes 294920 | tf_op jit(solution)/shard_map/ppermute | solution.py:326
  31.0 3.4 %collective-permute-start.3 = (f32[4,8,6,128]{3,2,1,0:T(8,128)S(1)}, f32[4,8,6,128]{3,2,1,0:T(8,128)S(1)}, u32[]{:S(2)}, u32[]{:S(2)}) collective-permute-start(f32[4,8,6,128]{3,2,1,0:T(8,128)S(1)} %get-tuple-element.24), channel_id=1, source_target_pairs={{0,384},{128,0},{256,128},{384,256},{1,385},{129,1},{257,129},{385... | collective-permute-start | bytes 294920 | tf_op jit(solution)/shard_map/ppermute | solution.py:326
  34.3 0.4 collective-permute-done.2.xb_ref
  34.8 1.9 %collective-permute-done.3.xa_ref = f32[4,8,6,128]{3,2,1,0:T(8,128)S(1)} collective-permute-done((f32[4,8,6,128]{3,2,1,0:T(8,128)S(1)}, f32[4,8,6,128]{3,2,1,0:T(8,128)S(1)}, u32[]{:S(2)}, u32[]{:S(2)}) %collective-permute-start.3) | collective-permute-done | bytes 98336 | tf_op jit(solution)/shard_map/ppermute | solution.py:326
  36.7 0.1 pack.1
  36.8 12.8 %collective-permute-start.4 = (f32[14,6,128]{2,1,0:T(8,128)S(1)}, f32[14,6,128]{2,1,0:T(8,128)S(1)}, u32[]{:S(2)}, u32[]{:S(2)}) collective-permute-start(f32[14,6,128]{2,1,0:T(8,128)S(1)} %get-tuple-element.7), channel_id=1, source_target_pairs={{0,16},{16,32},{32,48},{48,64},{64,80},{80,96},{96,112},{112,0},{1... | collective-permute-start | bytes 129032 | tf_op jit(solution)/shard_map/ppermute | solution.py:326
  49.6 1.9 %collective-permute-start.5 = (f32[14,6,128]{2,1,0:T(8,128)S(1)}, f32[14,6,128]{2,1,0:T(8,128)S(1)}, u32[]{:S(2)}, u32[]{:S(2)}) collective-permute-start(f32[14,6,128]{2,1,0:T(8,128)S(1)} %get-tuple-element.8), channel_id=1, source_target_pairs={{0,112},{16,0},{32,16},{48,32},{64,48},{80,64},{96,80},{112,96},{1... | collective-permute-start | bytes 129032 | tf_op jit(solution)/shard_map/ppermute | solution.py:326
  51.5 9.2 %collective-permute-done.5.ya_ref = f32[14,6,128]{2,1,0:T(8,128)S(1)} collective-permute-done((f32[14,6,128]{2,1,0:T(8,128)S(1)}, f32[14,6,128]{2,1,0:T(8,128)S(1)}, u32[]{:S(2)}, u32[]{:S(2)}) %collective-permute-start.5) | collective-permute-done | bytes 43040 | tf_op jit(solution)/shard_map/ppermute | solution.py:326
  60.7 0.5 diffusion.1
  61.4 0.1 copy.58
  61.6 0.6 copy.59
  62.2 3.6 %all-to-all-start.1 = ((f32[4,16,4]{0,2,1:T(4,128)}), f32[4,16,4]{0,2,1:T(4,128)S(1)}, u32[]{:S(2)}, u32[]{:S(2)}) async-start(f32[4,16,4]{0,2,1:T(4,128)} %copy.59), calls=%async_computation.1 | async-start | bytes 65536 | tf_op jit(solution)/shard_map/all_to_all | solution.py:353
  65.9 56.3 %pair_forces.1 = f32[3,2,8,2,128]{4,3,2,1,0:T(2,128)} custom-call(f32[7,8,6,128]{3,2,1,0:T(8,128)S(1)} %pad_maximum_fusion.own_ref, f32[4,8,6,128]{3,2,1,0:T(8,128)S(1)} %collective-permute-done.2.xb_ref, f32[4,8,6,128]{3,2,1,0:T(8,128)S(1)} %collective-permute-done.3.xa_ref, f32[14,6,128]{2,1,0:T(8,128)S(1)} %collective-permute-done.4.yb_ref, ...), custom_call_target="tpu_custom_call" | custom-call | tf_op jit(solution)/shard_map/pair_forces/pallas_call | solution.py:234
  122.2 0.7 copy.61
  (30 shorter events, 0.9 us)
Async XLA Ops:
  2.3 0.7 copy-start.3
  3.2 0.8 copy-start.5
  4.0 11.5 %copy-start.4 = (f32[4,1,64]{2,1,0:T(1,128)S(1)}, f32[4,1,64]{2,1,0:T(1,128)}, u32[]{:S(2)}) copy-start(f32[4,1,64]{2,1,0:T(1,128)} %param.11) | copy-start | bytes 3076
  4.0 23.6 %collective-permute-start = (f32[7,8,2,128]{3,2,1,0:T(2,128)S(1)}, f32[7,8,2,128]{3,2,1,0:T(2,128)S(1)}, u32[]{:S(2)}, u32[]{:S(2)}) collective-permute-start(f32[7,8,2,128]{3,2,1,0:T(2,128)S(1)} %pad_maximum_fusion.3), channel_id=1, source_target_pairs={{0,1},{1,2},{2,3},{3,4},{4,5},{5,6},{6,7},{7,8},{8,9},{9,10},{10,1... | collective-permute-start | bytes 172040 | tf_op jit(solution)/shard_map/ppermute | solution.py:326
  8.4 19.2 %collective-permute-start.1 = (f32[7,8,2,128]{3,2,1,0:T(2,128)S(1)}, f32[7,8,2,128]{3,2,1,0:T(2,128)S(1)}, u32[]{:S(2)}, u32[]{:S(2)}) collective-permute-start(f32[7,8,2,128]{3,2,1,0:T(2,128)S(1)} %pad_maximum_fusion.3), channel_id=1, source_target_pairs={{0,15},{1,0},{2,1},{3,2},{4,3},{5,4},{6,5},{7,6},{8,7},{9,8},{10,9... | collective-permute-start | bytes 172040 | tf_op jit(solution)/shard_map/ppermute | solution.py:326
  27.8 6.9 %collective-permute-start.2 = (f32[4,8,6,128]{3,2,1,0:T(8,128)S(1)}, f32[4,8,6,128]{3,2,1,0:T(8,128)S(1)}, u32[]{:S(2)}, u32[]{:S(2)}) collective-permute-start(f32[4,8,6,128]{3,2,1,0:T(8,128)S(1)} %get-tuple-element.25), channel_id=1, source_target_pairs={{0,128},{128,256},{256,384},{384,0},{1,129},{129,257},{257,385},{3... | collective-permute-start | bytes 294920 | tf_op jit(solution)/shard_map/ppermute | solution.py:326
  31.0 5.7 %collective-permute-start.3 = (f32[4,8,6,128]{3,2,1,0:T(8,128)S(1)}, f32[4,8,6,128]{3,2,1,0:T(8,128)S(1)}, u32[]{:S(2)}, u32[]{:S(2)}) collective-permute-start(f32[4,8,6,128]{3,2,1,0:T(8,128)S(1)} %get-tuple-element.24), channel_id=1, source_target_pairs={{0,384},{128,0},{256,128},{384,256},{1,385},{129,1},{257,129},{385... | collective-permute-start | bytes 294920 | tf_op jit(solution)/shard_map/ppermute | solution.py:326
  36.8 14.7 %collective-permute-start.4 = (f32[14,6,128]{2,1,0:T(8,128)S(1)}, f32[14,6,128]{2,1,0:T(8,128)S(1)}, u32[]{:S(2)}, u32[]{:S(2)}) collective-permute-start(f32[14,6,128]{2,1,0:T(8,128)S(1)} %get-tuple-element.7), channel_id=1, source_target_pairs={{0,16},{16,32},{32,48},{48,64},{64,80},{80,96},{96,112},{112,0},{1... | collective-permute-start | bytes 129032 | tf_op jit(solution)/shard_map/ppermute | solution.py:326
  49.6 11.1 %collective-permute-start.5 = (f32[14,6,128]{2,1,0:T(8,128)S(1)}, f32[14,6,128]{2,1,0:T(8,128)S(1)}, u32[]{:S(2)}, u32[]{:S(2)}) collective-permute-start(f32[14,6,128]{2,1,0:T(8,128)S(1)} %get-tuple-element.8), channel_id=1, source_target_pairs={{0,112},{16,0},{32,16},{48,32},{64,48},{80,64},{96,80},{112,96},{1... | collective-permute-start | bytes 129032 | tf_op jit(solution)/shard_map/ppermute | solution.py:326
  60.7 5.2 %copy-start.2 = (f32[27,8,128]{2,1,0:T(8,128)S(1)}, f32[27,8,128]{2,1,0:T(8,128)}, u32[]{:S(2)}) copy-start(f32[27,8,128]{2,1,0:T(8,128)} %constant.15.clone.k_ref) | copy-start | bytes 331780
  61.4 4.5 %copy-start.1 = (f32[27,8,128]{2,1,0:T(8,128)S(1)}, f32[27,8,128]{2,1,0:T(8,128)}, u32[]{:S(2)}) copy-start(f32[27,8,128]{2,1,0:T(8,128)} %constant.14.clone.m_ref) | copy-start | bytes 331780
  62.2 3.7 %copy-start = (f32[3,2,8,2,128]{4,3,2,1,0:T(2,128)S(1)}, f32[3,2,8,2,128]{4,3,2,1,0:T(2,128)}, u32[]{:S(2)}) copy-start(f32[3,2,8,2,128]{4,3,2,1,0:T(2,128)} %vel_ref.1) | copy-start | bytes 147460
  62.2 60.0 %all-to-all-start.1 = ((f32[4,16,4]{0,2,1:T(4,128)}), f32[4,16,4]{0,2,1:T(4,128)S(1)}, u32[]{:S(2)}, u32[]{:S(2)}) async-start(f32[4,16,4]{0,2,1:T(4,128)} %copy.59), calls=%async_computation.1 | async-start | bytes 65536 | tf_op jit(solution)/shard_map/all_to_all | solution.py:353

commit v4 on v3

--- a/solution.py
+++ b/solution.py
@@ -90,11 +90,12 @@
 
 TABLES = ((0, 1), (2, 1), (2, 3))
 DENSITY_TILES = ((0, 0, 1), (0, 1, 0), (1, 1, 2), (2, 2, 3), (2, 3, 2))
+OWN_TILES = ((0, 0, 1), (2, 2, 3), (1, 1, 0), (2, None, 2))
 FORCE_TILES = ((0, 1, 1), (1, 1, 2), (2, 2, 2))
 
 
 def main_kernel(own_ref, xb_ref, xa_ref, yb_ref, ya_ref, vel_ref, sub_ref, diff_ref, m_ref, k_ref,
-                out_ref, pos_ref, te_ref, cen_ref, sl_ref, g_ref):
+                out_ref, pos_ref, te_ref, cen_ref, sl_ref, g_ref, row_ref, col_ref):
     NX, NY = 4, 10
     row = lax.broadcasted_iota(jnp.int32, (8, 128), 0)
     low = lax.broadcasted_iota(jnp.int32, (128, 128), 1) < 64
@@ -107,67 +108,84 @@
     pos_ref[:, 0] = yb_ref[0:12]
     pos_ref[:, 9] = ya_ref[0:12]
 
-    def prep(n, carry):
-        x = n // NY
-        y = n % NY
-        blocks = []
-        for z in range(4):
-            rows = cell_rows(pos_ref, x, y, z + 1)
-            blocks.append(neighbour_block(row, rows))
-            cen_ref[(x * NY + y) * 4 + z] = centre_block(row, rows)
-        a = jnp.concatenate(blocks[:2], 0).T
-        b = jnp.concatenate(blocks[2:], 0).T
-        base = (x * (NY + 2) + y + 1) * 3
-        te_ref[base] = a.astype(BF)
-        te_ref[base + 1] = jnp.where(low, b, a).astype(BF)
-        te_ref[base + 2] = b.astype(BF)
-        return carry
-
-    lax.fori_loop(0, NX * NY, prep, 0)
+    def prep(y, carry):
+        for x in range(NX):
+            blocks = []
+            for z in range(4):
+                rows = cell_rows(pos_ref, x, y, z + 1)
+                blocks.append(neighbour_block(row, rows))
+                cen_ref[(x * NY + y) * 4 + z] = centre_block(row, rows)
+            a = jnp.concatenate(blocks[:2], 0).T
+            b = jnp.concatenate(blocks[2:], 0).T
+            base = (x * (NY + 2) + y + 1) * 3
+            te_ref[base] = a.astype(BF)
+            te_ref[base + 1] = jnp.where(low, b, a).astype(BF)
+            te_ref[base + 2] = b.astype(BF)
+        return carry
+
+    lax.fori_loop(0, NY, prep, 0)
     for x in range(NX):
         for y in (0, NY + 1):
             te_ref[pl.ds((x * (NY + 2) + y) * 3, 3)] = jnp.zeros((3, 128, 128), BF)
+
+    row_ref[...] = jnp.zeros(row_ref.shape, F32)
 
     def dens(y, carry):
         for x in range(NX):
             centres = [cen_ref[(x * NY + y) * 4 + z] for z in range(4)]
             acc = [jnp.zeros((8, 128), F32) for z in range(4)]
-            for ox in (-1, 0, 1):
-                if not 0 <= x + ox < NX:
+            for ox, oy in ((0, 0), (0, 1), (1, -1), (1, 0), (1, 1)):
+                if x + ox >= NX:
                     continue
-                for oy in (-1, 0, 1):
-                    base = ((x + ox) * (NY + 2) + y + 1 + oy) * 3
-                    for t, ca, cb in DENSITY_TILES:
-                        w = []
-                        for half, c in ((0, ca), (1, cb)):
-                            o = SHIFTS.index((ox, oy, TABLES[t][half] - c))
-                            w.append(weights(centres[c], m_ref[o], k_ref[o]))
-                        r = pair_values(te_ref[base + t], *w)
-                        r3 = r * r * r
-                        for half, c in ((0, ca), (1, cb)):
-                            part = r3[:, 128 * half:128 * half + 128]
-                            if (ox, oy) == (0, 0) and TABLES[t][half] == c:
-                                part = jnp.where(diag, 0.0, part)
-                            acc[c] = acc[c] + part.reshape(16, 8, 128).sum(0)
+                col = (x + ox) * (NY + 2) + y + 1 + oy
+                tiles = OWN_TILES if (ox, oy) == (0, 0) else DENSITY_TILES
+                for t, ca, cb in tiles:
+                    w = []
+                    for half, c in ((0, ca), (1, cb)):
+                        if c is None:
+                            w.append(jnp.zeros((64, 128), BF))
+                            continue
+                        o = SHIFTS.index((ox, oy, TABLES[t][half] - c))
+                        w.append(weights(centres[c], m_ref[o], k_ref[o]))
+                    r = pair_values(te_ref[col * 3 + t], *w)
+                    r3 = r * r * r
+                    for half, c in ((0, ca), (1, cb)):
+                        if c is None:
+                            continue
+                        layer = TABLES[t][half]
+                        part = r3[:, 128 * half:128 * half + 128]
+                        if (ox, oy) == (0, 0) and layer == c:
+                            part = jnp.where(diag, 0.0, part)
+                        else:
+                            row_ref[col * 4 + layer] = row_ref[col * 4 + layer] + part
+                        acc[c] = acc[c] + part.reshape(16, 8, 128).sum(0)
             for z in range(4):
-                d = jnp.sum(acc[z], axis=0, keepdims=True) * (1.0 / CUT ** 3)
+                col_ref[(x * NY + y) * 4 + z] = acc[z]
+        return carry
+
+    lax.fori_loop(0, NY, dens, 0)
+    def slope(y, carry):
+        for x in range(NX):
+            for z in range(4):
+                v = row_ref[(x * (NY + 2) + y + 1) * 4 + z]
+                other = jnp.sum(v.T.reshape(16, 8, 128), axis=0) + col_ref[(x * NY + y) * 4 + z]
+                d = jnp.sum(other, axis=0, keepdims=True) * (1.0 / CUT ** 3)
                 sl_ref[x, y, pl.ds(z, 1), :] = -0.5 / jnp.sqrt(d + 1.0)
         return carry
 
-    lax.fori_loop(0, NY, dens, 0)
-
-    def gprep(n, carry):
-        x = n // NY
-        y = n % NY
-        for z in range(4):
-            qx, qy, qz, _ = cell_rows(pos_ref, x, y, z + 1)
-            s = jnp.broadcast_to(sl_ref[x, y, pl.ds(z, 1), :], (8, 128))
-            v = pick(row % 4, qx, qy, qz, jnp.ones_like(qx))
-            hi, mid, lo = split3(v * jnp.where(row < 4, 1.0, s))
-            g_ref[n * 4 + z] = jnp.concatenate([hi, mid, lo, jnp.zeros_like(hi)], 0).astype(BF)
-        return carry
-
-    lax.fori_loop(0, NX * NY, gprep, 0)
+    lax.fori_loop(0, NY, slope, 0)
+
+    def gprep(y, carry):
+        for x in range(NX):
+            for z in range(4):
+                qx, qy, qz, _ = cell_rows(pos_ref, x, y, z + 1)
+                s = jnp.broadcast_to(sl_ref[x, y, pl.ds(z, 1), :], (8, 128))
+                v = pick(row % 4, qx, qy, qz, jnp.ones_like(qx))
+                hi, mid, lo = split3(v * jnp.where(row < 4, 1.0, s))
+                g_ref[(x * NY + y) * 4 + z] = jnp.concatenate([hi, mid, lo, jnp.zeros_like(hi)], 0).astype(BF)
+        return carry
+
+    lax.fori_loop(0, NY, gprep, 0)
 
     def force(n, carry):
         x = n // (8 // GROUP) + 1
@@ -242,8 +260,10 @@
             pltpu.VMEM((160, 8, 128), F32),
             pltpu.VMEM((4, 10, 4, 128), F32),
             pltpu.VMEM((160, 32, 128), BF),
+            pltpu.VMEM((4 * 12 * 4, 128, 128), F32),
+            pltpu.VMEM((160, 8, 128), F32),
         ],
-        compiler_params=pltpu.CompilerParams(vmem_limit_bytes=24 * 2 ** 20),
+        compiler_params=pltpu.CompilerParams(vmem_limit_bytes=40 * 2 ** 20),
         name="pair_forces",
     )(own, xb, xa, yb, ya, vel, sub, diff, m, k)
 

time: 123 us -> 114 us (0.927)
  Pallas kernels: 56.9 us -> 47.7 us
    pallas_call x1, Pallas kernels: 56.3 us -> 47 us  [main_call(): pl.pallas_call(main_kernel, out_shape=jax.ShapeDtypeStruct(vel.shape, F32...]
  transfers between devices with their start and end apart: 7 -> 7, of which waited for: 3 -> 3; matrix products, arithmetic and copies ran while one was open for 2% -> 2% of each run, Pallas kernels for 46% -> 41%
where the time goes in v4:
time: 114 us
  Pallas kernels  47.7 us (42%)
  starting transfers between devices  36.3 us (32%)
  waiting for transfers between devices  11.5 us (10%)
  blocking collectives  9.67 us (8%)
  local copies, waits for them, and re-layouts  5.14 us (5%)
  other arithmetic  2.45 us (2%)
    pallas_call x1, Pallas kernels, main_call(): pl.pallas_call(main_kernel, out_shape=jax.ShapeDtypeStruct(vel.shape, F32...  47 us
    ppermute x6, starting transfers between devices, ring(): return lax.ppermute(value, axis, [(i, (i + step) % n) for i in range(n)])  32.7 us
    ppermute x6, waiting for transfers between devices, ring(): return lax.ppermute(value, axis, [(i, (i + step) % n) for i in range(n)])  11.5 us
    all_to_all x1, blocking collectives, per_device(): lax.all_to_all(jnp.concatenate(shifted, 0), 'gz', split_axis=2, concat_ax...  9.67 us
    all_to_all x1, starting transfers between devices, per_device(): heat = lax.all_to_all(heat, 'gz', split_axis=1, concat_axis=2, tiled=True)  3.6 us
    unnamed x15, local copies, waits for them, and re-layouts  2.83 us
  transfers between devices with their start and end apart: 7, of which 3 were waited for; matrix products, arithmetic and copies ran while one was open for 2% of the time, Pallas kernels for 41%

profile of v4, /device:TPU:1, one launch (start us, length us, event | category | flops | bytes accessed | tf_op | source)
XLA Modules:
  0.0 113.6 jit_solution(14670760576944656853)
XLA Ops:
  0.6 0.8 copy.46
  1.4 0.8 multiply_reduce_fusion
  2.4 0.6 copy-done.3
  3.0 0.1 select_reduce_fusion
  3.2 0.1 reshape.44
  3.3 0.7 copy-done.5
  4.0 4.4 %collective-permute-start = (f32[7,8,2,128]{3,2,1,0:T(2,128)S(1)}, f32[7,8,2,128]{3,2,1,0:T(2,128)S(1)}, u32[]{:S(2)}, u32[]{:S(2)}) collective-permute-start(f32[7,8,2,128]{3,2,1,0:T(2,128)S(1)} %pad_maximum_fusion.3), channel_id=1, source_target_pairs={{0,1},{1,2},{2,3},{3,4},{4,5},{5,6},{6,7},{7,8},{8,9},{9,10},{10,1... | collective-permute-start | bytes 172040 | tf_op jit(solution)/shard_map/ppermute | solution.py:346
  8.4 7.1 %collective-permute-start.1 = (f32[7,8,2,128]{3,2,1,0:T(2,128)S(1)}, f32[7,8,2,128]{3,2,1,0:T(2,128)S(1)}, u32[]{:S(2)}, u32[]{:S(2)}) collective-permute-start(f32[7,8,2,128]{3,2,1,0:T(2,128)S(1)} %pad_maximum_fusion.3), channel_id=1, source_target_pairs={{0,15},{1,0},{2,1},{3,2},{4,3},{5,4},{6,5},{7,6},{8,7},{9,8},{10,9... | collective-permute-start | bytes 172040 | tf_op jit(solution)/shard_map/ppermute | solution.py:346
  15.7 0.1 copy.53
  15.8 0.1 copy.52
  15.9 0.1 copy.54
  16.0 0.2 pad_maximum_fusion.4
  16.2 9.7 %all_to_all.21 = f32[12,1,64]{0,1,2:T(1,128)S(1)} all-to-all(f32[12,1,64]{0,1,2:T(1,128)S(1)} %pad_maximum_fusion.4), channel_id=1, replica_groups=mesh['gx'=4,'gy'=8,'gz'=16] {'gz'}, dimensions={2} | all-to-all | bytes 6144 | tf_op jit(solution)/shard_map/all_to_all | solution.py:354
  25.9 0.5 broadcast.25
  26.4 0.7 reduce.3
  27.2 0.1 reshape.45
  27.3 0.2 copy.55
  27.6 0.1 pad_maximum_fusion.own_ref
  27.8 3.1 %collective-permute-start.2 = (f32[4,8,6,128]{3,2,1,0:T(8,128)S(1)}, f32[4,8,6,128]{3,2,1,0:T(8,128)S(1)}, u32[]{:S(2)}, u32[]{:S(2)}) collective-permute-start(f32[4,8,6,128]{3,2,1,0:T(8,128)S(1)} %get-tuple-element.25), channel_id=1, source_target_pairs={{0,128},{128,256},{256,384},{384,0},{1,129},{129,257},{257,385},{3... | collective-permute-start | bytes 294920 | tf_op jit(solution)/shard_map/ppermute | solution.py:346
  31.0 3.4 %collective-permute-start.3 = (f32[4,8,6,128]{3,2,1,0:T(8,128)S(1)}, f32[4,8,6,128]{3,2,1,0:T(8,128)S(1)}, u32[]{:S(2)}, u32[]{:S(2)}) collective-permute-start(f32[4,8,6,128]{3,2,1,0:T(8,128)S(1)} %get-tuple-element.24), channel_id=1, source_target_pairs={{0,384},{128,0},{256,128},{384,256},{1,385},{129,1},{257,129},{385... | collective-permute-start | bytes 294920 | tf_op jit(solution)/shard_map/ppermute | solution.py:346
  34.3 0.4 collective-permute-done.2.xb_ref
  34.8 1.9 %collective-permute-done.3.xa_ref = f32[4,8,6,128]{3,2,1,0:T(8,128)S(1)} collective-permute-done((f32[4,8,6,128]{3,2,1,0:T(8,128)S(1)}, f32[4,8,6,128]{3,2,1,0:T(8,128)S(1)}, u32[]{:S(2)}, u32[]{:S(2)}) %collective-permute-start.3) | collective-permute-done | bytes 98336 | tf_op jit(solution)/shard_map/ppermute | solution.py:346
  36.7 0.1 pack.1
  36.8 12.8 %collective-permute-start.4 = (f32[14,6,128]{2,1,0:T(8,128)S(1)}, f32[14,6,128]{2,1,0:T(8,128)S(1)}, u32[]{:S(2)}, u32[]{:S(2)}) collective-permute-start(f32[14,6,128]{2,1,0:T(8,128)S(1)} %get-tuple-element.7), channel_id=1, source_target_pairs={{0,16},{16,32},{32,48},{48,64},{64,80},{80,96},{96,112},{112,0},{1... | collective-permute-start | bytes 129032 | tf_op jit(solution)/shard_map/ppermute | solution.py:346
  49.6 1.9 %collective-permute-start.5 = (f32[14,6,128]{2,1,0:T(8,128)S(1)}, f32[14,6,128]{2,1,0:T(8,128)S(1)}, u32[]{:S(2)}, u32[]{:S(2)}) collective-permute-start(f32[14,6,128]{2,1,0:T(8,128)S(1)} %get-tuple-element.8), channel_id=1, source_target_pairs={{0,112},{16,0},{32,16},{48,32},{64,48},{80,64},{96,80},{112,96},{1... | collective-permute-start | bytes 129032 | tf_op jit(solution)/shard_map/ppermute | solution.py:346
  51.5 9.2 %collective-permute-done.5.ya_ref = f32[14,6,128]{2,1,0:T(8,128)S(1)} collective-permute-done((f32[14,6,128]{2,1,0:T(8,128)S(1)}, f32[14,6,128]{2,1,0:T(8,128)S(1)}, u32[]{:S(2)}, u32[]{:S(2)}) %collective-permute-start.5) | collective-permute-done | bytes 43040 | tf_op jit(solution)/shard_map/ppermute | solution.py:346
  60.7 0.5 diffusion.1
  61.4 0.1 copy.58
  61.6 0.6 copy.59
  62.2 3.6 %all-to-all-start.1 = ((f32[4,16,4]{0,2,1:T(4,128)}), f32[4,16,4]{0,2,1:T(4,128)S(1)}, u32[]{:S(2)}, u32[]{:S(2)}) async-start(f32[4,16,4]{0,2,1:T(4,128)} %copy.59), calls=%async_computation.1 | async-start | bytes 65536 | tf_op jit(solution)/shard_map/all_to_all | solution.py:373
  65.9 47.0 %pair_forces.1 = f32[3,2,8,2,128]{4,3,2,1,0:T(2,128)} custom-call(f32[7,8,6,128]{3,2,1,0:T(8,128)S(1)} %pad_maximum_fusion.own_ref, f32[4,8,6,128]{3,2,1,0:T(8,128)S(1)} %collective-permute-done.2.xb_ref, f32[4,8,6,128]{3,2,1,0:T(8,128)S(1)} %collective-permute-done.3.xa_ref, f32[14,6,128]{2,1,0:T(8,128)S(1)} %collective-permute-done.4.yb_ref, ...), custom_call_target="tpu_custom_call" | custom-call | tf_op jit(solution)/shard_map/pair_forces/pallas_call | solution.py:252
  113.0 0.7 copy.61
  (30 shorter events, 0.9 us)
Async XLA Ops:
  2.3 0.7 copy-start.3
  3.2 0.8 copy-start.5
  4.0 11.5 %copy-start.4 = (f32[4,1,64]{2,1,0:T(1,128)S(1)}, f32[4,1,64]{2,1,0:T(1,128)}, u32[]{:S(2)}) copy-start(f32[4,1,64]{2,1,0:T(1,128)} %param.11) | copy-start | bytes 3076
  4.0 23.6 %collective-permute-start = (f32[7,8,2,128]{3,2,1,0:T(2,128)S(1)}, f32[7,8,2,128]{3,2,1,0:T(2,128)S(1)}, u32[]{:S(2)}, u32[]{:S(2)}) collective-permute-start(f32[7,8,2,128]{3,2,1,0:T(2,128)S(1)} %pad_maximum_fusion.3), channel_id=1, source_target_pairs={{0,1},{1,2},{2,3},{3,4},{4,5},{5,6},{6,7},{7,8},{8,9},{9,10},{10,1... | collective-permute-start | bytes 172040 | tf_op jit(solution)/shard_map/ppermute | solution.py:346
  8.4 19.2 %collective-permute-start.1 = (f32[7,8,2,128]{3,2,1,0:T(2,128)S(1)}, f32[7,8,2,128]{3,2,1,0:T(2,128)S(1)}, u32[]{:S(2)}, u32[]{:S(2)}) collective-permute-start(f32[7,8,2,128]{3,2,1,0:T(2,128)S(1)} %pad_maximum_fusion.3), channel_id=1, source_target_pairs={{0,15},{1,0},{2,1},{3,2},{4,3},{5,4},{6,5},{7,6},{8,7},{9,8},{10,9... | collective-permute-start | bytes 172040 | tf_op jit(solution)/shard_map/ppermute | solution.py:346
  27.8 6.9 %collective-permute-start.2 = (f32[4,8,6,128]{3,2,1,0:T(8,128)S(1)}, f32[4,8,6,128]{3,2,1,0:T(8,128)S(1)}, u32[]{:S(2)}, u32[]{:S(2)}) collective-permute-start(f32[4,8,6,128]{3,2,1,0:T(8,128)S(1)} %get-tuple-element.25), channel_id=1, source_target_pairs={{0,128},{128,256},{256,384},{384,0},{1,129},{129,257},{257,385},{3... | collective-permute-start | bytes 294920 | tf_op jit(solution)/shard_map/ppermute | solution.py:346
  31.0 5.7 %collective-permute-start.3 = (f32[4,8,6,128]{3,2,1,0:T(8,128)S(1)}, f32[4,8,6,128]{3,2,1,0:T(8,128)S(1)}, u32[]{:S(2)}, u32[]{:S(2)}) collective-permute-start(f32[4,8,6,128]{3,2,1,0:T(8,128)S(1)} %get-tuple-element.24), channel_id=1, source_target_pairs={{0,384},{128,0},{256,128},{384,256},{1,385},{129,1},{257,129},{385... | collective-permute-start | bytes 294920 | tf_op jit(solution)/shard_map/ppermute | solution.py:346
  36.8 14.7 %collective-permute-start.4 = (f32[14,6,128]{2,1,0:T(8,128)S(1)}, f32[14,6,128]{2,1,0:T(8,128)S(1)}, u32[]{:S(2)}, u32[]{:S(2)}) collective-permute-start(f32[14,6,128]{2,1,0:T(8,128)S(1)} %get-tuple-element.7), channel_id=1, source_target_pairs={{0,16},{16,32},{32,48},{48,64},{64,80},{80,96},{96,112},{112,0},{1... | collective-permute-start | bytes 129032 | tf_op jit(solution)/shard_map/ppermute | solution.py:346
  49.6 11.1 %collective-permute-start.5 = (f32[14,6,128]{2,1,0:T(8,128)S(1)}, f32[14,6,128]{2,1,0:T(8,128)S(1)}, u32[]{:S(2)}, u32[]{:S(2)}) collective-permute-start(f32[14,6,128]{2,1,0:T(8,128)S(1)} %get-tuple-element.8), channel_id=1, source_target_pairs={{0,112},{16,0},{32,16},{48,32},{64,48},{80,64},{96,80},{112,96},{1... | collective-permute-start | bytes 129032 | tf_op jit(solution)/shard_map/ppermute | solution.py:346
  60.7 5.2 %copy-start.2 = (f32[27,8,128]{2,1,0:T(8,128)S(1)}, f32[27,8,128]{2,1,0:T(8,128)}, u32[]{:S(2)}) copy-start(f32[27,8,128]{2,1,0:T(8,128)} %constant.15.clone.k_ref) | copy-start | bytes 331780
  61.4 4.5 %copy-start.1 = (f32[27,8,128]{2,1,0:T(8,128)S(1)}, f32[27,8,128]{2,1,0:T(8,128)}, u32[]{:S(2)}) copy-start(f32[27,8,128]{2,1,0:T(8,128)} %constant.14.clone.m_ref) | copy-start | bytes 331780
  62.2 3.7 %copy-start = (f32[3,2,8,2,128]{4,3,2,1,0:T(2,128)S(1)}, f32[3,2,8,2,128]{4,3,2,1,0:T(2,128)}, u32[]{:S(2)}) copy-start(f32[3,2,8,2,128]{4,3,2,1,0:T(2,128)} %vel_ref.1) | copy-start | bytes 147460
  62.2 50.8 %all-to-all-start.1 = ((f32[4,16,4]{0,2,1:T(4,128)}), f32[4,16,4]{0,2,1:T(4,128)S(1)}, u32[]{:S(2)}, u32[]{:S(2)}) async-start(f32[4,16,4]{0,2,1:T(4,128)} %copy.59), calls=%async_computation.1 | async-start | bytes 65536 | tf_op jit(solution)/shard_map/all_to_all | solution.py:373

commit v5 on v4

--- a/solution.py
+++ b/solution.py
@@ -101,18 +101,21 @@
     low = lax.broadcasted_iota(jnp.int32, (128, 128), 1) < 64
     diag = same_slot()
     for a in range(3):
-        pos_ref[4 * a, 1:9] = xb_ref[a]
-        pos_ref[4 * a + 1, 1:9] = own_ref[2 * a]
-        pos_ref[4 * a + 2, 1:9] = own_ref[2 * a + 1]
-        pos_ref[4 * a + 3, 1:9] = xa_ref[a]
-    pos_ref[:, 0] = yb_ref[0:12]
-    pos_ref[:, 9] = ya_ref[0:12]
+        for y in range(8):
+            rows = pl.ds((a * 8 + y) * 4, 4)
+            pos_ref[4 * a, y + 1] = xb_ref[rows]
+            pos_ref[4 * a + 1, y + 1] = own_ref[2 * a, y, 1:5]
+            pos_ref[4 * a + 2, y + 1] = own_ref[2 * a + 1, y, 1:5]
+            pos_ref[4 * a + 3, y + 1] = xa_ref[rows]
+    for p in range(12):
+        pos_ref[p, 0] = yb_ref[pl.ds(4 * p, 4)]
+        pos_ref[p, 9] = ya_ref[pl.ds(4 * p, 4)]
 
     def prep(y, carry):
         for x in range(NX):
             blocks = []
             for z in range(4):
-                rows = cell_rows(pos_ref, x, y, z + 1)
+                rows = cell_rows(pos_ref, x, y, z)
                 blocks.append(neighbour_block(row, rows))
                 cen_ref[(x * NY + y) * 4 + z] = centre_block(row, rows)
             a = jnp.concatenate(blocks[:2], 0).T
@@ -178,7 +181,7 @@
     def gprep(y, carry):
         for x in range(NX):
             for z in range(4):
-                qx, qy, qz, _ = cell_rows(pos_ref, x, y, z + 1)
+                qx, qy, qz, _ = cell_rows(pos_ref, x, y, z)
                 s = jnp.broadcast_to(sl_ref[x, y, pl.ds(z, 1), :], (8, 128))
                 v = pick(row % 4, qx, qy, qz, jnp.ones_like(qx))
                 hi, mid, lo = split3(v * jnp.where(row < 4, 1.0, s))
@@ -226,7 +229,7 @@
         for c, h in [(c, h) for c in range(GROUP) for h in range(2)]:
             y = first + c
             total = acc[c][h]
-            rows = cell_rows(pos_ref, x, y, h + 2)
+            rows = cell_rows(pos_ref, x, y, h + 1)
             s = sl_ref[x, y, pl.ds(h + 1, 1), :]
             sub = sub_ref[x - 1, y - 1, pl.ds(h, 1), :]
             both = diff_ref[pl.ds((y + 1) * 6 + 2 + h, 1), :]
@@ -255,7 +258,7 @@
         in_specs=[VM] * 10,
         out_specs=VM,
         scratch_shapes=[
-            pltpu.VMEM((12, 10, 6, 128), F32),
+            pltpu.VMEM((12, 10, 4, 128), F32),
             pltpu.VMEM((4 * 12 * 3, 128, 128), BF),
             pltpu.VMEM((160, 8, 128), F32),
             pltpu.VMEM((4, 10, 4, 128), F32),
@@ -268,43 +271,117 @@
     )(own, xb, xa, yb, ya, vel, sub, diff, m, k)
 
 
-def pack_kernel(own_ref, e_ref, xb_ref, xa_ref, up_ref, down_ref, mid_ref):
+SMALL = pltpu.CompilerParams(vmem_limit_bytes=2 * 2 ** 20)
+
+
+def rows_of(n):
+    return jax.ShapeDtypeStruct((n, 128), F32)
+
+
+def front_kernel(cnt_ref, pos_ref, vel_ref, grid_ref, own_ref, up_ref, down_ref):
+    lane = lax.broadcasted_iota(jnp.int32, (2, 128), 1)
+    first = lax.broadcasted_iota(jnp.int32, (2, 128), 0) == 0
+    for y in range(8):
+        lat = jnp.zeros((2, 128), F32)
+        for x in range(2):
+            occupied = lane < jnp.where(first, cnt_ref[x, y, 0], cnt_ref[x, y, 1])
+            for a in range(3):
+                p = jnp.where(occupied, pos_ref[a, x, y], 1000.0)
+                plane = 2 * a + x
+                own_ref[plane, y] = p
+                down_ref[pl.ds(plane * 8 + y, 1)] = p[0:1]
+                up_ref[pl.ds(plane * 8 + y, 1)] = p[1:2]
+            v = [vel_ref[a, x, y] for a in range(3)]
+            kinetic = jnp.where(occupied, 0.5 * (v[0] * v[0] + v[1] * v[1] + v[2] * v[2]), 0.0)
+            sub = grid_ref[x, y]
+            for k in range(8):
+                total = jnp.sum(jnp.where(sub == k, kinetic, 0.0), axis=1, keepdims=True)
+                lat = jnp.where(lane == 8 * x + k, total, lat)
+        own_ref[6, y] = lat
+        down_ref[pl.ds(48 + 2 * y, 2)] = lat
+        up_ref[pl.ds(48 + 2 * y, 2)] = lat
+
+
+def front_call(counts, positions, velocities, grid_cells):
+    return pl.pallas_call(
+        front_kernel,
+        out_shape=(jax.ShapeDtypeStruct((7, 8, 2, 128), F32), rows_of(64), rows_of(64)),
+        in_specs=[pl.BlockSpec(memory_space=pltpu.SMEM)] + [VM] * 3,
+        out_specs=(VM, VM, VM),
+        compiler_params=SMALL,
+        name="front",
+    )(counts, positions, velocities, grid_cells)
+
+
+def pack_x_kernel(mine_ref, zb_ref, za_ref, e_ref, own_ref, up_ref, down_ref):
+    for y in range(8):
+        for plane in range(6):
+            row = pl.ds(plane * 8 + y, 1)
+            own_ref[plane, y, 1:2] = zb_ref[row]
+            own_ref[plane, y, 2:4] = mine_ref[plane, y]
+            own_ref[plane, y, 4:5] = za_ref[row]
+            message = down_ref if plane % 2 == 0 else up_ref
+            base = (plane // 2 * 8 + y) * 4
+            message[pl.ds(base, 1)] = zb_ref[row]
+            message[pl.ds(base + 1, 2)] = mine_ref[plane, y]
+            message[pl.ds(base + 3, 1)] = za_ref[row]
+        pair = pl.ds(48 + 2 * y, 2)
+        own_ref[6, y, 0:2] = zb_ref[pair]
+        own_ref[6, y, 2:4] = mine_ref[6, y]
+        own_ref[6, y, 4:6] = za_ref[pair]
+        field = own_ref[6, y] + e_ref[y]
+        up_ref[pl.ds(96 + 6 * y, 6)] = field
+        down_ref[pl.ds(96 + 6 * y, 6)] = field
+
+
+def pack_x_call(mine, zb, za, e):
+    return pl.pallas_call(
+        pack_x_kernel,
+        out_shape=(jax.ShapeDtypeStruct((7, 8, 6, 128), F32), rows_of(144), rows_of(144)),
+        in_specs=[VM] * 4,
+        out_specs=(VM, VM, VM),
+        compiler_params=SMALL,
+        name="pack_x",
+    )(mine, zb, za, e)
+
+
+def pack_y_kernel(own_ref, e_ref, xb_ref, xa_ref, up_ref, down_ref, mid_ref):
     lane = lax.broadcasted_iota(jnp.int32, (6, 128), 1)
+    used = (lane < 48) | ((lane >= 64) & (lane < 112))
     for y in range(8):
-        lat = own_ref[6, y]
-        mine = e_ref[y]
-        e_part = jnp.where(lane < 16, pltpu.roll(xb_ref[3, y], 112, 1),
-                           jnp.where(lane < 32, mine, pltpu.roll(xa_ref[3, y], 16, 1)))
-        l_part = jnp.where(lane < 80, pltpu.roll(xb_ref[3, y], 64, 1),
-                           jnp.where(lane < 96, pltpu.roll(lat, 80, 1), pltpu.roll(xa_ref[3, y], 96, 1)))
-        used = (lane < 48) | ((lane >= 64) & (lane < 112))
+        before, after = xb_ref[pl.ds(96 + 6 * y, 6)], xa_ref[pl.ds(96 + 6 * y, 6)]
+        lat, e = own_ref[6, y], e_ref[y]
+        e_part = jnp.where(lane < 16, pltpu.roll(before, 112, 1), jnp.where(lane < 32, e, pltpu.roll(after, 16, 1)))
+        l_part = jnp.where(lane < 80, pltpu.roll(before, 64, 1),
+                           jnp.where(lane < 96, pltpu.roll(lat, 80, 1), pltpu.roll(after, 96, 1)))
         mid_ref[y] = jnp.where(used, jnp.where(lane < 64, e_part, l_part), 0.0)
     for ref, y in ((up_ref, 7), (down_ref, 0)):
         for a in range(3):
-            ref[4 * a] = xb_ref[a, y]
-            ref[4 * a + 1] = own_ref[2 * a, y]
-            ref[4 * a + 2] = own_ref[2 * a + 1, y]
-            ref[4 * a + 3] = xa_ref[a, y]
+            rows = pl.ds((a * 8 + y) * 4, 4)
+            ref[pl.ds(16 * a, 4)] = xb_ref[rows]
+            ref[pl.ds(16 * a + 4, 4)] = own_ref[2 * a, y, 1:5]
+            ref[pl.ds(16 * a + 8, 4)] = own_ref[2 * a + 1, y, 1:5]
+            ref[pl.ds(16 * a + 12, 4)] = xa_ref[rows]
         for n in range(2):
-            ref[12 + n] = mid_ref[(y // 7) * 6 + n]
-
-
-def pack_call(own, e, xb, xa):
-    message = jax.ShapeDtypeStruct((14, 6, 128), F32)
+            ref[pl.ds(48 + 6 * n, 6)] = mid_ref[(y // 7) * 6 + n]
+        ref[pl.ds(60, 4)] = jnp.zeros((4, 128), F32)
+
+
+def pack_y_call(own, e, xb, xa):
     return pl.pallas_call(
-        pack_kernel,
-        out_shape=(message, message, jax.ShapeDtypeStruct((8, 6, 128), F32)),
+        pack_y_kernel,
+        out_shape=(rows_of(64), rows_of(64), jax.ShapeDtypeStruct((8, 6, 128), F32)),
         in_specs=[VM] * 4,
         out_specs=(VM, VM, VM),
-        compiler_params=pltpu.CompilerParams(vmem_limit_bytes=2 * 2 ** 20),
-        name="pack",
+        compiler_params=SMALL,
+        name="pack_y",
     )(own, e, xb, xa)
 
 
 def diffuse_kernel(mid_ref, yb_ref, ya_ref, e_out, diff_out, x_ref, e_ref):
     for n in range(2):
-        x_ref[pl.ds(6 * n, 6)] = yb_ref[12 + n]
-        x_ref[pl.ds(60 + 6 * n, 6)] = ya_ref[12 + n]
+        x_ref[pl.ds(6 * n, 6)] = yb_ref[pl.ds(48 + 6 * n, 6)]
+        x_ref[pl.ds(60 + 6 * n, 6)] = ya_ref[pl.ds(48 + 6 * n, 6)]
     for y in range(8):
         x_ref[pl.ds(12 + 6 * y, 6)] = mid_ref[y]
     rows = 72
@@ -336,7 +413,7 @@
         in_specs=[VM] * 3,
         out_specs=(VM, VM),
         scratch_shapes=[pltpu.VMEM((72, 128), F32), pltpu.VMEM((88, 128), F32)],
-        compiler_params=pltpu.CompilerParams(vmem_limit_bytes=2 * 2 ** 20),
+        compiler_params=SMALL,
         name="diffusion",
     )(mid, yb, ya)
 
@@ -354,20 +431,11 @@
     e = lax.all_to_all(jnp.concatenate(shifted, 0), "gz", split_axis=2, concat_axis=1, tiled=True)
     e = e.reshape(3, 4, ny, 2, nz, 2).transpose(2, 0, 4, 1, 3, 5).reshape(ny, 6, 16)
     e = jnp.pad(e, ((0, 0), (0, 0), (16, 96)))
-    kinetic = jnp.where(occupied, 0.5 * jnp.sum(velocities * velocities, axis=0), 0.0)
-    sub = lax.broadcasted_iota(jnp.int32, (nx, ny, nz, 8, 128), 3)
-    lat = jnp.sum(jnp.where(grid_cells[..., None, :] == sub, kinetic[..., None, :], 0.0), axis=-1)
-    lat = lat.transpose(1, 2, 0, 3).reshape(1, ny, nz, 16)
-    lat = jnp.pad(lat, ((0, 0), (0, 0), (0, 0), (0, 112)))
-    parked = jnp.where(occupied[None], positions, 1000.0).reshape(6, ny, nz, 128)
-    planes = jnp.concatenate([parked, lat], 0)
-    own = jnp.concatenate([ring(planes, "gz", 1), planes, ring(planes, "gz", -1)], 2)
-    field = (own[6] + e)[None]
-    xb = ring(jnp.concatenate([own[1:6:2], field], 0), "gx", 1)
-    xa = ring(jnp.concatenate([own[0:6:2], field], 0), "gx", -1)
-    up, down, mid = pack_call(own, e, xb, xa)
-    yb = ring(up, "gy", 1)
-    ya = ring(down, "gy", -1)
+    mine, up, down = front_call(counts, positions, velocities, grid_cells)
+    own, up, down = pack_x_call(mine, ring(up, "gz", 1), ring(down, "gz", -1), e)
+    xb, xa = ring(up, "gx", 1), ring(down, "gx", -1)
+    up, down, mid = pack_y_call(own, e, xb, xa)
+    yb, ya = ring(up, "gy", 1), ring(down, "gy", -1)
     e_new, diff = diffuse_call(mid, yb, ya)
     heat = e_new[..., 16:32].reshape(ny, nz, 4, 2, 2).transpose(2, 0, 3, 1, 4).reshape(4, 2 * ny, 2 * nz)
     heat = lax.all_to_all(heat, "gz", split_axis=1, concat_axis=2, tiled=True)

time: 114 us -> 113 us (level)
  waiting for transfers between devices: 11.5 us -> 9.87 us
  other arithmetic: 2.45 us -> 1.09 us
    ppermute x6, waiting for transfers between devices: 11.5 us -> 9.86 us  [ring(): return lax.ppermute(value, axis, [(i, (i + step) % n) for i in range(n)])]
    unnamed x15 -> x19, local copies, waits for them, and re-layouts: 2.83 us -> 3.84 us
  transfers between devices with their start and end apart: 7 -> 7, of which waited for: 3 -> 2; matrix products, arithmetic and copies ran while one was open for 2% -> 2% of each run, Pallas kernels for 41% -> 42%
where the time goes in v5:
time: 113 us; the launch traced here: 112 us
  Pallas kernels  48.6 us (43%)
  starting transfers between devices  36.3 us (32%)
  waiting for transfers between devices  9.87 us (9%)
  blocking collectives  9.67 us (9%)
  local copies, waits for them, and re-layouts  6.12 us (5%)
    pallas_call x1, Pallas kernels, main_call(): pl.pallas_call(main_kernel, out_shape=jax.ShapeDtypeStruct(vel.shape, F32...  47 us
    ppermute x6, starting transfers between devices, ring(): return lax.ppermute(value, axis, [(i, (i + step) % n) for i in range(n)])  32.7 us
    ppermute x6, waiting for transfers between devices, ring(): return lax.ppermute(value, axis, [(i, (i + step) % n) for i in range(n)])  9.86 us
    all_to_all x1, blocking collectives, per_device(): lax.all_to_all(jnp.concatenate(shifted, 0), 'gz', split_axis=2, concat_ax...  9.67 us
    unnamed x19, local copies, waits for them, and re-layouts  3.84 us
    all_to_all x1, starting transfers between devices, per_device(): heat = lax.all_to_all(heat, 'gz', split_axis=1, concat_axis=2, tiled=True)  3.62 us
  transfers between devices with their start and end apart: 7, of which 2 were waited for; matrix products, arithmetic and copies ran while one was open for 2% of the time, Pallas kernels for 42%

profile of v5, /device:TPU:1, one launch (start us, length us, event | category | flops | bytes accessed | tf_op | source)
XLA Modules:
  0.0 112.5 jit_solution(7543391754518974317)
XLA Ops:
  0.6 0.8 copy.50.cnt_ref
  1.4 0.8 copy-done
  2.2 0.7 copy-done.4
  2.9 0.8 copy-done.6
  3.7 0.9 front.1
  4.6 4.4 %collective-permute-start = (f32[64,128]{1,0:T(8,128)S(1)}, f32[64,128]{1,0:T(8,128)S(1)}, u32[]{:S(2)}, u32[]{:S(2)}) collective-permute-start(f32[64,128]{1,0:T(8,128)S(1)} %get-tuple-element.14), channel_id=1, source_target_pairs={{0,1},{1,2},{2,3},{3,4},{4,5},{5,6},{6,7},{7,8},{8,9},{9,10},{10,1... | collective-permute-start | bytes 98312 | tf_op jit(solution)/shard_map/ppermute | solution.py:423
  9.0 7.1 %collective-permute-start.1 = (f32[64,128]{1,0:T(8,128)S(1)}, f32[64,128]{1,0:T(8,128)S(1)}, u32[]{:S(2)}, u32[]{:S(2)}) collective-permute-start(f32[64,128]{1,0:T(8,128)S(1)} %get-tuple-element.15), channel_id=1, source_target_pairs={{0,15},{1,0},{2,1},{3,2},{4,3},{5,4},{6,5},{7,6},{8,7},{9,8},{10,9... | collective-permute-start | bytes 98312 | tf_op jit(solution)/shard_map/ppermute | solution.py:423
  16.2 0.1 copy.56
  16.4 0.1 copy.55
  16.5 0.1 copy.57
  16.6 0.2 pad_maximum_fusion
  16.8 9.7 %all_to_all.21 = f32[12,1,64]{0,1,2:T(1,128)S(1)} all-to-all(f32[12,1,64]{0,1,2:T(1,128)S(1)} %pad_maximum_fusion), channel_id=1, replica_groups=mesh['gx'=4,'gy'=8,'gz'=16] {'gz'}, dimensions={2} | all-to-all | bytes 6144 | tf_op jit(solution)/shard_map/all_to_all | solution.py:431
  26.5 0.5 broadcast.6
  27.0 0.7 reduce.3
  27.7 0.1 reshape.24
  27.8 0.2 copy.58
  28.1 0.1 pad.4.e_ref
  28.3 0.1 pack_x.1
  28.4 3.1 %collective-permute-start.2 = (f32[144,128]{1,0:T(8,128)S(1)}, f32[144,128]{1,0:T(8,128)S(1)}, u32[]{:S(2)}, u32[]{:S(2)}) collective-permute-start(f32[144,128]{1,0:T(8,128)S(1)} %get-tuple-element.17), channel_id=1, source_target_pairs={{0,128},{128,256},{256,384},{384,0},{1,129},{129,257},{257,385},{3... | collective-permute-start | bytes 221192 | tf_op jit(solution)/shard_map/ppermute | solution.py:423
  31.5 3.4 %collective-permute-start.3 = (f32[144,128]{1,0:T(8,128)S(1)}, f32[144,128]{1,0:T(8,128)S(1)}, u32[]{:S(2)}, u32[]{:S(2)}) collective-permute-start(f32[144,128]{1,0:T(8,128)S(1)} %get-tuple-element.18), channel_id=1, source_target_pairs={{0,384},{128,0},{256,128},{384,256},{1,385},{129,1},{257,129},{385... | collective-permute-start | bytes 221192 | tf_op jit(solution)/shard_map/ppermute | solution.py:423
  34.9 1.7 %collective-permute-done.3.xa_ref = f32[144,128]{1,0:T(8,128)S(1)} collective-permute-done((f32[144,128]{1,0:T(8,128)S(1)}, f32[144,128]{1,0:T(8,128)S(1)}, u32[]{:S(2)}, u32[]{:S(2)}) %collective-permute-start.3) | collective-permute-done | bytes 73760 | tf_op jit(solution)/shard_map/ppermute | solution.py:423
  36.6 0.1 pack_y.1
  36.7 12.8 %collective-permute-start.4 = (f32[64,128]{1,0:T(8,128)S(1)}, f32[64,128]{1,0:T(8,128)S(1)}, u32[]{:S(2)}, u32[]{:S(2)}) collective-permute-start(f32[64,128]{1,0:T(8,128)S(1)} %get-tuple-element.19), channel_id=1, source_target_pairs={{0,16},{16,32},{32,48},{48,64},{64,80},{80,96},{96,112},{112,0},{1... | collective-permute-start | bytes 98312 | tf_op jit(solution)/shard_map/ppermute | solution.py:423
  49.5 1.9 %collective-permute-start.5 = (f32[64,128]{1,0:T(8,128)S(1)}, f32[64,128]{1,0:T(8,128)S(1)}, u32[]{:S(2)}, u32[]{:S(2)}) collective-permute-start(f32[64,128]{1,0:T(8,128)S(1)} %get-tuple-element.20), channel_id=1, source_target_pairs={{0,112},{16,0},{32,16},{48,32},{64,48},{80,64},{96,80},{112,96},{1... | collective-permute-start | bytes 98312 | tf_op jit(solution)/shard_map/ppermute | solution.py:423
  51.4 8.1 %collective-permute-done.5.ya_ref = f32[64,128]{1,0:T(8,128)S(1)} collective-permute-done((f32[64,128]{1,0:T(8,128)S(1)}, f32[64,128]{1,0:T(8,128)S(1)}, u32[]{:S(2)}, u32[]{:S(2)}) %collective-permute-start.5) | collective-permute-done | bytes 32800 | tf_op jit(solution)/shard_map/ppermute | solution.py:423
  59.6 0.5 diffusion.1
  60.3 0.1 copy.62
  60.4 0.6 copy.63
  61.0 3.6 %all-to-all-start.1 = ((f32[4,16,4]{0,2,1:T(4,128)}), f32[4,16,4]{0,2,1:T(4,128)S(1)}, u32[]{:S(2)}, u32[]{:S(2)}) async-start(f32[4,16,4]{0,2,1:T(4,128)} %copy.63), calls=%async_computation.1 | async-start | bytes 65536 | tf_op jit(solution)/shard_map/all_to_all | solution.py:441
  64.7 0.1 compare_select_fusion.sub_ref
  64.8 47.0 %pair_forces.1 = f32[3,2,8,2,128]{4,3,2,1,0:T(2,128)} custom-call(f32[7,8,6,128]{3,2,1,0:T(8,128)S(1)} %get-tuple-element.16.own_ref, f32[144,128]{1,0:T(8,128)S(1)} %collective-permute-done.2.xb_ref, f32[144,128]{1,0:T(8,128)S(1)} %collective-permute-done.3.xa_ref, f32[64,128]{1,0:T(8,128)S(1)} %collective-permute-done.4.yb_ref, ...), custom_call_target="tpu_custom_call" | custom-call | tf_op jit(solution)/shard_map/pair_forces/pallas_call | solution.py:255
  111.8 0.7 copy.65
  (24 shorter events, 0.5 us)
Async XLA Ops:
  1.4 0.8 copy-start
  2.2 0.7 copy-start.4
  2.9 0.8 copy-start.6
  4.6 11.5 %copy-start.7 = (f32[4,1,64]{2,1,0:T(1,128)S(1)}, f32[4,1,64]{2,1,0:T(1,128)}, u32[]{:S(2)}) copy-start(f32[4,1,64]{2,1,0:T(1,128)} %param.11) | copy-start | bytes 3076
  4.6 23.6 %collective-permute-start = (f32[64,128]{1,0:T(8,128)S(1)}, f32[64,128]{1,0:T(8,128)S(1)}, u32[]{:S(2)}, u32[]{:S(2)}) collective-permute-start(f32[64,128]{1,0:T(8,128)S(1)} %get-tuple-element.14), channel_id=1, source_target_pairs={{0,1},{1,2},{2,3},{3,4},{4,5},{5,6},{6,7},{7,8},{8,9},{9,10},{10,1... | collective-permute-start | bytes 98312 | tf_op jit(solution)/shard_map/ppermute | solution.py:423
  9.0 19.3 %collective-permute-start.1 = (f32[64,128]{1,0:T(8,128)S(1)}, f32[64,128]{1,0:T(8,128)S(1)}, u32[]{:S(2)}, u32[]{:S(2)}) collective-permute-start(f32[64,128]{1,0:T(8,128)S(1)} %get-tuple-element.15), channel_id=1, source_target_pairs={{0,15},{1,0},{2,1},{3,2},{4,3},{5,4},{6,5},{7,6},{8,7},{9,8},{10,9... | collective-permute-start | bytes 98312 | tf_op jit(solution)/shard_map/ppermute | solution.py:423
  28.4 6.5 %collective-permute-start.2 = (f32[144,128]{1,0:T(8,128)S(1)}, f32[144,128]{1,0:T(8,128)S(1)}, u32[]{:S(2)}, u32[]{:S(2)}) collective-permute-start(f32[144,128]{1,0:T(8,128)S(1)} %get-tuple-element.17), channel_id=1, source_target_pairs={{0,128},{128,256},{256,384},{384,0},{1,129},{129,257},{257,385},{3... | collective-permute-start | bytes 221192 | tf_op jit(solution)/shard_map/ppermute | solution.py:423
  31.5 5.1 %collective-permute-start.3 = (f32[144,128]{1,0:T(8,128)S(1)}, f32[144,128]{1,0:T(8,128)S(1)}, u32[]{:S(2)}, u32[]{:S(2)}) collective-permute-start(f32[144,128]{1,0:T(8,128)S(1)} %get-tuple-element.18), channel_id=1, source_target_pairs={{0,384},{128,0},{256,128},{384,256},{1,385},{129,1},{257,129},{385... | collective-permute-start | bytes 221192 | tf_op jit(solution)/shard_map/ppermute | solution.py:423
  36.7 14.7 %collective-permute-start.4 = (f32[64,128]{1,0:T(8,128)S(1)}, f32[64,128]{1,0:T(8,128)S(1)}, u32[]{:S(2)}, u32[]{:S(2)}) collective-permute-start(f32[64,128]{1,0:T(8,128)S(1)} %get-tuple-element.19), channel_id=1, source_target_pairs={{0,16},{16,32},{32,48},{48,64},{64,80},{80,96},{96,112},{112,0},{1... | collective-permute-start | bytes 98312 | tf_op jit(solution)/shard_map/ppermute | solution.py:423
  49.5 10.1 %collective-permute-start.5 = (f32[64,128]{1,0:T(8,128)S(1)}, f32[64,128]{1,0:T(8,128)S(1)}, u32[]{:S(2)}, u32[]{:S(2)}) collective-permute-start(f32[64,128]{1,0:T(8,128)S(1)} %get-tuple-element.20), channel_id=1, source_target_pairs={{0,112},{16,0},{32,16},{48,32},{64,48},{80,64},{96,80},{112,96},{1... | collective-permute-start | bytes 98312 | tf_op jit(solution)/shard_map/ppermute | solution.py:423
  59.6 5.2 %copy-start.3 = (f32[27,8,128]{2,1,0:T(8,128)S(1)}, f32[27,8,128]{2,1,0:T(8,128)}, u32[]{:S(2)}) copy-start(f32[27,8,128]{2,1,0:T(8,128)} %constant.9.clone.m_ref) | copy-start | bytes 331780
  60.3 4.5 %copy-start.2 = (f32[27,8,128]{2,1,0:T(8,128)S(1)}, f32[27,8,128]{2,1,0:T(8,128)}, u32[]{:S(2)}) copy-start(f32[27,8,128]{2,1,0:T(8,128)} %constant.10.clone.k_ref) | copy-start | bytes 331780
  61.0 3.6 %copy-start.5 = (s32[2,8,2,128]{3,2,1,0:T(2,128)S(1)}, s32[2,8,2,128]{3,2,1,0:T(2,128)}, u32[]{:S(2)}) copy-start(s32[2,8,2,128]{3,2,1,0:T(2,128)} %grid_ref.1) | copy-start | bytes 49156
  61.0 3.8 %copy-start.1 = (f32[3,2,8,2,128]{4,3,2,1,0:T(2,128)S(1)}, f32[3,2,8,2,128]{4,3,2,1,0:T(2,128)}, u32[]{:S(2)}) copy-start(f32[3,2,8,2,128]{4,3,2,1,0:T(2,128)} %vel_ref.3) | copy-start | bytes 147460
  61.0 50.8 %all-to-all-start.1 = ((f32[4,16,4]{0,2,1:T(4,128)}), f32[4,16,4]{0,2,1:T(4,128)S(1)}, u32[]{:S(2)}, u32[]{:S(2)}) async-start(f32[4,16,4]{0,2,1:T(4,128)} %copy.63), calls=%async_computation.1 | async-start | bytes 65536 | tf_op jit(solution)/shard_map/all_to_all | solution.py:441

commit v6 on v5

--- a/solution.py
+++ b/solution.py
@@ -11,7 +11,7 @@
 EDGE = 11.0
 HALF = 5.5
 BIG = 10000.0
-GROUP = 4
+GROUP = 8
 F32 = jnp.float32
 BF = jnp.bfloat16
 VM = pl.BlockSpec(memory_space=pltpu.VMEM)
@@ -429,9 +429,10 @@
     occupied = slot < counts[..., None]
     shifted = [jnp.roll(electron_temp, 4, 2), electron_temp, jnp.roll(electron_temp, -4, 2)]
     e = lax.all_to_all(jnp.concatenate(shifted, 0), "gz", split_axis=2, concat_axis=1, tiled=True)
+    mine, up, down = front_call(counts, positions, velocities, grid_cells)
+    up, down, e = lax.optimization_barrier((up, down, e))
     e = e.reshape(3, 4, ny, 2, nz, 2).transpose(2, 0, 4, 1, 3, 5).reshape(ny, 6, 16)
     e = jnp.pad(e, ((0, 0), (0, 0), (16, 96)))
-    mine, up, down = front_call(counts, positions, velocities, grid_cells)
     own, up, down = pack_x_call(mine, ring(up, "gz", 1), ring(down, "gz", -1), e)
     xb, xa = ring(up, "gx", 1), ring(down, "gx", -1)
     up, down, mid = pack_y_call(own, e, xb, xa)

time: 113 us -> 117 us (1.035)
  starting transfers between devices: 36.3 us -> 47.6 us
  blocking collectives: 9.67 us -> 0 us
  waiting for transfers between devices: 9.87 us -> 15.3 us
  local copies, waits for them, and re-layouts: 6.12 us -> 3.4 us
    all_to_all x1 -> x0, blocking collectives: 9.67 us -> none  [per_device(): lax.all_to_all(jnp.concatenate(shifted, 0), 'gz', split_axis=2, concat_ax...]
    all_to_all x0 -> x1, starting transfers between devices: none -> 9.32 us  [per_device(): lax.all_to_all(jnp.concatenate(shifted, 0), 'gz', split_axis=2, concat_ax...]
    all_to_all x0 -> x1, waiting for transfers between devices: none -> 5.87 us  [per_device(): lax.all_to_all(jnp.concatenate(shifted, 0), 'gz', split_axis=2, concat_ax...]
    all_to_all x1, starting transfers between devices: 3.62 us -> 7.32 us  [per_device(): heat = lax.all_to_all(heat, 'gz', split_axis=1, concat_axis=2, tiled=True)]
    unnamed x19 -> x17, local copies, waits for them, and re-layouts: 3.84 us -> 0.86 us
    ppermute x6, starting transfers between devices: 32.7 us -> 31 us  [ring(): return lax.ppermute(value, axis, [(i, (i + step) % n) for i in range(n)])]
  transfers between devices with their start and end apart: 7 -> 8, of which waited for: 2 -> 4; matrix products, arithmetic and copies ran while one was open for 2% -> 1% of each run, Pallas kernels for 42% -> 41%
where the time goes in v6:
time: 117 us; the launch traced here: 116 us
  Pallas kernels  48 us (41%)
  starting transfers between devices  47.6 us (41%)
  waiting for transfers between devices  15.3 us (13%)
  local copies, waits for them, and re-layouts  3.4 us (3%)
    pallas_call x1, Pallas kernels, main_call(): pl.pallas_call(main_kernel, out_shape=jax.ShapeDtypeStruct(vel.shape, F32...  46.4 us
    ppermute x6, starting transfers between devices, ring(): return lax.ppermute(value, axis, [(i, (i + step) % n) for i in range(n)])  31 us
    ppermute x6, waiting for transfers between devices, ring(): return lax.ppermute(value, axis, [(i, (i + step) % n) for i in range(n)])  9.38 us
    all_to_all x1, starting transfers between devices, per_device(): lax.all_to_all(jnp.concatenate(shifted, 0), 'gz', split_axis=2, concat_ax...  9.32 us
    all_to_all x1, starting transfers between devices, per_device(): heat = lax.all_to_all(heat, 'gz', split_axis=1, concat_axis=2, tiled=True)  7.32 us
    all_to_all x1, waiting for transfers between devices, per_device(): lax.all_to_all(jnp.concatenate(shifted, 0), 'gz', split_axis=2, concat_ax...  5.87 us
  transfers between devices with their start and end apart: 8, of which 4 were waited for; matrix products, arithmetic and copies ran while one was open for 1% of the time, Pallas kernels for 41%

profile of v6, /device:TPU:1, one launch (start us, length us, event | category | flops | bytes accessed | tf_op | source)
XLA Modules:
  0.0 116.1 jit_solution(6162277414945770040)
XLA Ops:
  0.6 0.9 fusion.1
  1.6 0.1 copy.48
  1.7 0.1 copy.47
  1.8 0.1 copy.49
  1.9 0.8 pad_maximum_fusion
  2.8 9.3 %all-to-all-start = ((f32[12,1,64]{0,1,2:T(1,128)}), f32[12,1,64]{0,1,2:T(1,128)S(1)}, u32[]{:S(2)}, u32[]{:S(2)}) async-start(f32[12,1,64]{0,1,2:T(1,128)} %pad_maximum_fusion), calls=%async_computation | async-start | bytes 65536 | tf_op jit(solution)/shard_map/all_to_all | solution.py:431
  12.1 0.1 copy.42.cnt_ref
  12.2 0.9 front.1
  13.1 5.9 %all-to-all-done = f32[12,1,64]{0,1,2:T(1,128)S(1)} async-done(((f32[12,1,64]{0,1,2:T(1,128)}), f32[12,1,64]{0,1,2:T(1,128)S(1)}, u32[]{:S(2)}, u32[]{:S(2)}) %all-to-all-start) | async-done | bytes 3104 | tf_op jit(solution)/shard_map/all_to_all | solution.py:431
  19.0 2.3 %collective-permute-start = (f32[64,128]{1,0:T(8,128)S(1)}, f32[64,128]{1,0:T(8,128)S(1)}, u32[]{:S(2)}, u32[]{:S(2)}) collective-permute-start(f32[64,128]{1,0:T(8,128)S(1)} %get-tuple-element.19), channel_id=1, source_target_pairs={{0,1},{1,2},{2,3},{3,4},{4,5},{5,6},{6,7},{7,8},{8,9},{9,10},{10,1... | collective-permute-start | bytes 98312 | tf_op jit(solution)/shard_map/ppermute | solution.py:423
  21.3 6.9 %collective-permute-start.1 = (f32[64,128]{1,0:T(8,128)S(1)}, f32[64,128]{1,0:T(8,128)S(1)}, u32[]{:S(2)}, u32[]{:S(2)}) collective-permute-start(f32[64,128]{1,0:T(8,128)S(1)} %get-tuple-element.20), channel_id=1, source_target_pairs={{0,15},{1,0},{2,1},{3,2},{4,3},{5,4},{6,5},{7,6},{8,7},{9,8},{10,9... | collective-permute-start | bytes 98312 | tf_op jit(solution)/shard_map/ppermute | solution.py:423
  28.2 0.1 reshape.23
  28.3 0.2 copy.51
  28.5 0.1 copy.52
  28.6 0.1 pad.4.e_ref
  28.7 0.5 collective-permute-done.1.za_ref
  29.1 0.1 pack_x.1
  29.2 3.1 %collective-permute-start.2 = (f32[144,128]{1,0:T(8,128)S(1)}, f32[144,128]{1,0:T(8,128)S(1)}, u32[]{:S(2)}, u32[]{:S(2)}) collective-permute-start(f32[144,128]{1,0:T(8,128)S(1)} %get-tuple-element.23), channel_id=1, source_target_pairs={{0,128},{128,256},{256,384},{384,0},{1,129},{129,257},{257,385},{3... | collective-permute-start | bytes 221192 | tf_op jit(solution)/shard_map/ppermute | solution.py:423
  32.4 3.4 %collective-permute-start.3 = (f32[144,128]{1,0:T(8,128)S(1)}, f32[144,128]{1,0:T(8,128)S(1)}, u32[]{:S(2)}, u32[]{:S(2)}) collective-permute-start(f32[144,128]{1,0:T(8,128)S(1)} %get-tuple-element.24), channel_id=1, source_target_pairs={{0,384},{128,0},{256,128},{384,256},{1,385},{129,1},{257,129},{385... | collective-permute-start | bytes 221192 | tf_op jit(solution)/shard_map/ppermute | solution.py:423
  35.8 1.7 %collective-permute-done.3.xa_ref = f32[144,128]{1,0:T(8,128)S(1)} collective-permute-done((f32[144,128]{1,0:T(8,128)S(1)}, f32[144,128]{1,0:T(8,128)S(1)}, u32[]{:S(2)}, u32[]{:S(2)}) %collective-permute-start.3) | collective-permute-done | bytes 73760 | tf_op jit(solution)/shard_map/ppermute | solution.py:423
  37.5 0.1 pack_y.1
  37.6 13.4 %collective-permute-start.4 = (f32[64,128]{1,0:T(8,128)S(1)}, f32[64,128]{1,0:T(8,128)S(1)}, u32[]{:S(2)}, u32[]{:S(2)}) collective-permute-start(f32[64,128]{1,0:T(8,128)S(1)} %get-tuple-element.25), channel_id=1, source_target_pairs={{0,16},{16,32},{32,48},{48,64},{64,80},{80,96},{96,112},{112,0},{1... | collective-permute-start | bytes 98312 | tf_op jit(solution)/shard_map/ppermute | solution.py:423
  51.0 1.9 %collective-permute-start.5 = (f32[64,128]{1,0:T(8,128)S(1)}, f32[64,128]{1,0:T(8,128)S(1)}, u32[]{:S(2)}, u32[]{:S(2)}) collective-permute-start(f32[64,128]{1,0:T(8,128)S(1)} %get-tuple-element.26), channel_id=1, source_target_pairs={{0,112},{16,0},{32,16},{48,32},{64,48},{80,64},{96,80},{112,96},{1... | collective-permute-start | bytes 98312 | tf_op jit(solution)/shard_map/ppermute | solution.py:423
  52.9 7.2 %collective-permute-done.5.ya_ref = f32[64,128]{1,0:T(8,128)S(1)} collective-permute-done((f32[64,128]{1,0:T(8,128)S(1)}, f32[64,128]{1,0:T(8,128)S(1)}, u32[]{:S(2)}, u32[]{:S(2)}) %collective-permute-start.5) | collective-permute-done | bytes 32800 | tf_op jit(solution)/shard_map/ppermute | solution.py:423
  60.1 0.5 diffusion.1
  60.7 0.1 copy.54
  60.8 0.1 copy.55
  60.9 0.6 copy.56
  61.6 7.3 %all-to-all-start.1 = ((f32[4,16,4]{0,2,1:T(4,128)}), f32[4,16,4]{0,2,1:T(4,128)S(1)}, u32[]{:S(2)}, u32[]{:S(2)}) async-start(f32[4,16,4]{0,2,1:T(4,128)} %copy.56), calls=%async_computation.1 | async-start | bytes 65536 | tf_op jit(solution)/shard_map/all_to_all | solution.py:442
  68.9 0.1 compare_select_fusion.sub_ref
  69.0 46.4 %pair_forces.1 = f32[3,2,8,2,128]{4,3,2,1,0:T(2,128)} custom-call(f32[7,8,6,128]{3,2,1,0:T(8,128)S(1)} %get-tuple-element.22.own_ref, f32[144,128]{1,0:T(8,128)S(1)} %collective-permute-done.2.xb_ref, f32[144,128]{1,0:T(8,128)S(1)} %collective-permute-done.3.xa_ref, f32[64,128]{1,0:T(8,128)S(1)} %collective-permute-done.4.yb_ref, ...), custom_call_target="tpu_custom_call" | custom-call | tf_op jit(solution)/shard_map/pair_forces/pallas_call | solution.py:255
  115.4 0.7 copy.58
  (22 shorter events, 0.3 us)
Async XLA Ops:
  0.6 0.9 copy-start.5
  1.9 10.2 %copy-start.6 = (s32[2,8,2]{1,2,0:T(2,128)S(1)}, s32[2,8,2]{1,2,0:T(2,128)}, u32[]{:S(2)}) copy-start(s32[2,8,2]{1,2,0:T(2,128)} %param.9) | copy-start | bytes 388
  1.9 10.3 %copy-start.4 = (f32[3,2,8,2,128]{4,3,2,1,0:T(2,128)S(1)}, f32[3,2,8,2,128]{4,3,2,1,0:T(2,128)}, u32[]{:S(2)}) copy-start(f32[3,2,8,2,128]{4,3,2,1,0:T(2,128)} %pos_ref.1) | copy-start | bytes 147460
  2.8 9.4 %copy-start = (f32[3,2,8,2,128]{4,3,2,1,0:T(2,128)S(1)}, f32[3,2,8,2,128]{4,3,2,1,0:T(2,128)}, u32[]{:S(2)}) copy-start(f32[3,2,8,2,128]{4,3,2,1,0:T(2,128)} %vel_ref.3) | copy-start | bytes 147460
  2.8 9.4 %copy-start.3 = (s32[2,8,2,128]{3,2,1,0:T(2,128)S(1)}, s32[2,8,2,128]{3,2,1,0:T(2,128)}, u32[]{:S(2)}) copy-start(s32[2,8,2,128]{3,2,1,0:T(2,128)} %grid_ref.1) | copy-start | bytes 49156
  2.8 16.2 %all-to-all-start = ((f32[12,1,64]{0,1,2:T(1,128)}), f32[12,1,64]{0,1,2:T(1,128)S(1)}, u32[]{:S(2)}, u32[]{:S(2)}) async-start(f32[12,1,64]{0,1,2:T(1,128)} %pad_maximum_fusion), calls=%async_computation | async-start | bytes 65536 | tf_op jit(solution)/shard_map/all_to_all | solution.py:431
  19.0 9.7 %collective-permute-start = (f32[64,128]{1,0:T(8,128)S(1)}, f32[64,128]{1,0:T(8,128)S(1)}, u32[]{:S(2)}, u32[]{:S(2)}) collective-permute-start(f32[64,128]{1,0:T(8,128)S(1)} %get-tuple-element.19), channel_id=1, source_target_pairs={{0,1},{1,2},{2,3},{3,4},{4,5},{5,6},{6,7},{7,8},{8,9},{9,10},{10,1... | collective-permute-start | bytes 98312 | tf_op jit(solution)/shard_map/ppermute | solution.py:423
  21.3 7.9 %collective-permute-start.1 = (f32[64,128]{1,0:T(8,128)S(1)}, f32[64,128]{1,0:T(8,128)S(1)}, u32[]{:S(2)}, u32[]{:S(2)}) collective-permute-start(f32[64,128]{1,0:T(8,128)S(1)} %get-tuple-element.20), channel_id=1, source_target_pairs={{0,15},{1,0},{2,1},{3,2},{4,3},{5,4},{6,5},{7,6},{8,7},{9,8},{10,9... | collective-permute-start | bytes 98312 | tf_op jit(solution)/shard_map/ppermute | solution.py:423
  29.2 6.5 %collective-permute-start.2 = (f32[144,128]{1,0:T(8,128)S(1)}, f32[144,128]{1,0:T(8,128)S(1)}, u32[]{:S(2)}, u32[]{:S(2)}) collective-permute-start(f32[144,128]{1,0:T(8,128)S(1)} %get-tuple-element.23), channel_id=1, source_target_pairs={{0,128},{128,256},{256,384},{384,0},{1,129},{129,257},{257,385},{3... | collective-permute-start | bytes 221192 | tf_op jit(solution)/shard_map/ppermute | solution.py:423
  32.4 5.1 %collective-permute-start.3 = (f32[144,128]{1,0:T(8,128)S(1)}, f32[144,128]{1,0:T(8,128)S(1)}, u32[]{:S(2)}, u32[]{:S(2)}) collective-permute-start(f32[144,128]{1,0:T(8,128)S(1)} %get-tuple-element.24), channel_id=1, source_target_pairs={{0,384},{128,0},{256,128},{384,256},{1,385},{129,1},{257,129},{385... | collective-permute-start | bytes 221192 | tf_op jit(solution)/shard_map/ppermute | solution.py:423
  37.6 15.3 %collective-permute-start.4 = (f32[64,128]{1,0:T(8,128)S(1)}, f32[64,128]{1,0:T(8,128)S(1)}, u32[]{:S(2)}, u32[]{:S(2)}) collective-permute-start(f32[64,128]{1,0:T(8,128)S(1)} %get-tuple-element.25), channel_id=1, source_target_pairs={{0,16},{16,32},{32,48},{48,64},{64,80},{80,96},{96,112},{112,0},{1... | collective-permute-start | bytes 98312 | tf_op jit(solution)/shard_map/ppermute | solution.py:423
  51.0 9.1 %collective-permute-start.5 = (f32[64,128]{1,0:T(8,128)S(1)}, f32[64,128]{1,0:T(8,128)S(1)}, u32[]{:S(2)}, u32[]{:S(2)}) collective-permute-start(f32[64,128]{1,0:T(8,128)S(1)} %get-tuple-element.26), channel_id=1, source_target_pairs={{0,112},{16,0},{32,16},{48,32},{64,48},{80,64},{96,80},{112,96},{1... | collective-permute-start | bytes 98312 | tf_op jit(solution)/shard_map/ppermute | solution.py:423
  60.8 8.2 %copy-start.1 = (f32[27,8,128]{2,1,0:T(8,128)S(1)}, f32[27,8,128]{2,1,0:T(8,128)}, u32[]{:S(2)}) copy-start(f32[27,8,128]{2,1,0:T(8,128)} %constant.10.clone.k_ref) | copy-start | bytes 331780
  60.8 8.2 %copy-start.2 = (f32[27,8,128]{2,1,0:T(8,128)S(1)}, f32[27,8,128]{2,1,0:T(8,128)}, u32[]{:S(2)}) copy-start(f32[27,8,128]{2,1,0:T(8,128)} %constant.9.clone.m_ref) | copy-start | bytes 331780
  61.6 53.9 %all-to-all-start.1 = ((f32[4,16,4]{0,2,1:T(4,128)}), f32[4,16,4]{0,2,1:T(4,128)S(1)}, u32[]{:S(2)}, u32[]{:S(2)}) async-start(f32[4,16,4]{0,2,1:T(4,128)} %copy.56), calls=%async_computation.1 | async-start | bytes 65536 | tf_op jit(solution)/shard_map/all_to_all | solution.py:442

commit v7 on v5

--- a/solution.py
+++ b/solution.py
@@ -11,7 +11,7 @@
 EDGE = 11.0
 HALF = 5.5
 BIG = 10000.0
-GROUP = 4
+GROUP = 8
 F32 = jnp.float32
 BF = jnp.bfloat16
 VM = pl.BlockSpec(memory_space=pltpu.VMEM)

time: 113 us -> 113 us (level)
  transfers between devices with their start and end apart: 7 -> 7, of which waited for: 2 -> 2; matrix products, arithmetic and copies ran while one was open for 2% -> 2% of each run, Pallas kernels for 42% -> 41%
where the time goes in v7:
time: 113 us; the launch traced here: 112 us
  Pallas kernels  48.1 us (43%)
  starting transfers between devices  36.5 us (32%)
  waiting for transfers between devices  9.87 us (9%)
  blocking collectives  9.67 us (9%)
  local copies, waits for them, and re-layouts  6.12 us (5%)
    pallas_call x1, Pallas kernels, main_call(): pl.pallas_call(main_kernel, out_shape=jax.ShapeDtypeStruct(vel.shape, F32...  46.4 us
    ppermute x6, starting transfers between devices, ring(): return lax.ppermute(value, axis, [(i, (i + step) % n) for i in range(n)])  32.7 us
    ppermute x6, waiting for transfers between devices, ring(): return lax.ppermute(value, axis, [(i, (i + step) % n) for i in range(n)])  9.86 us
    all_to_all x1, blocking collectives, per_device(): lax.all_to_all(jnp.concatenate(shifted, 0), 'gz', split_axis=2, concat_ax...  9.67 us
    unnamed x19, local copies, waits for them, and re-layouts  3.84 us
    all_to_all x1, starting transfers between devices, per_device(): heat = lax.all_to_all(heat, 'gz', split_axis=1, concat_axis=2, tiled=True)  3.8 us
  transfers between devices with their start and end apart: 7, of which 2 were waited for; matrix products, arithmetic and copies ran while one was open for 2% of the time, Pallas kernels for 41%

profile of v7, /device:TPU:1, one launch (start us, length us, event | category | flops | bytes accessed | tf_op | source)
XLA Modules:
  0.0 112.1 jit_solution(10092124918696321748)
XLA Ops:
  0.6 0.8 copy.50.cnt_ref
  1.4 0.8 copy-done
  2.2 0.7 copy-done.4
  2.9 0.8 copy-done.6
  3.7 0.9 front.1
  4.6 4.4 %collective-permute-start = (f32[64,128]{1,0:T(8,128)S(1)}, f32[64,128]{1,0:T(8,128)S(1)}, u32[]{:S(2)}, u32[]{:S(2)}) collective-permute-start(f32[64,128]{1,0:T(8,128)S(1)} %get-tuple-element.14), channel_id=1, source_target_pairs={{0,1},{1,2},{2,3},{3,4},{4,5},{5,6},{6,7},{7,8},{8,9},{9,10},{10,1... | collective-permute-start | bytes 98312 | tf_op jit(solution)/shard_map/ppermute | solution.py:423
  9.0 7.1 %collective-permute-start.1 = (f32[64,128]{1,0:T(8,128)S(1)}, f32[64,128]{1,0:T(8,128)S(1)}, u32[]{:S(2)}, u32[]{:S(2)}) collective-permute-start(f32[64,128]{1,0:T(8,128)S(1)} %get-tuple-element.15), channel_id=1, source_target_pairs={{0,15},{1,0},{2,1},{3,2},{4,3},{5,4},{6,5},{7,6},{8,7},{9,8},{10,9... | collective-permute-start | bytes 98312 | tf_op jit(solution)/shard_map/ppermute | solution.py:423
  16.2 0.1 copy.56
  16.4 0.1 copy.55
  16.5 0.1 copy.57
  16.6 0.2 pad_maximum_fusion
  16.8 9.7 %all_to_all.21 = f32[12,1,64]{0,1,2:T(1,128)S(1)} all-to-all(f32[12,1,64]{0,1,2:T(1,128)S(1)} %pad_maximum_fusion), channel_id=1, replica_groups=mesh['gx'=4,'gy'=8,'gz'=16] {'gz'}, dimensions={2} | all-to-all | bytes 6144 | tf_op jit(solution)/shard_map/all_to_all | solution.py:431
  26.5 0.5 broadcast.6
  27.0 0.7 reduce.3
  27.7 0.1 reshape.24
  27.8 0.2 copy.58
  28.1 0.1 pad.4.e_ref
  28.3 0.1 pack_x.1
  28.4 3.1 %collective-permute-start.2 = (f32[144,128]{1,0:T(8,128)S(1)}, f32[144,128]{1,0:T(8,128)S(1)}, u32[]{:S(2)}, u32[]{:S(2)}) collective-permute-start(f32[144,128]{1,0:T(8,128)S(1)} %get-tuple-element.17), channel_id=1, source_target_pairs={{0,128},{128,256},{256,384},{384,0},{1,129},{129,257},{257,385},{3... | collective-permute-start | bytes 221192 | tf_op jit(solution)/shard_map/ppermute | solution.py:423
  31.5 3.4 %collective-permute-start.3 = (f32[144,128]{1,0:T(8,128)S(1)}, f32[144,128]{1,0:T(8,128)S(1)}, u32[]{:S(2)}, u32[]{:S(2)}) collective-permute-start(f32[144,128]{1,0:T(8,128)S(1)} %get-tuple-element.18), channel_id=1, source_target_pairs={{0,384},{128,0},{256,128},{384,256},{1,385},{129,1},{257,129},{385... | collective-permute-start | bytes 221192 | tf_op jit(solution)/shard_map/ppermute | solution.py:423
  34.9 1.7 %collective-permute-done.3.xa_ref = f32[144,128]{1,0:T(8,128)S(1)} collective-permute-done((f32[144,128]{1,0:T(8,128)S(1)}, f32[144,128]{1,0:T(8,128)S(1)}, u32[]{:S(2)}, u32[]{:S(2)}) %collective-permute-start.3) | collective-permute-done | bytes 73760 | tf_op jit(solution)/shard_map/ppermute | solution.py:423
  36.6 0.1 pack_y.1
  36.7 12.8 %collective-permute-start.4 = (f32[64,128]{1,0:T(8,128)S(1)}, f32[64,128]{1,0:T(8,128)S(1)}, u32[]{:S(2)}, u32[]{:S(2)}) collective-permute-start(f32[64,128]{1,0:T(8,128)S(1)} %get-tuple-element.19), channel_id=1, source_target_pairs={{0,16},{16,32},{32,48},{48,64},{64,80},{80,96},{96,112},{112,0},{1... | collective-permute-start | bytes 98312 | tf_op jit(solution)/shard_map/ppermute | solution.py:423
  49.5 1.9 %collective-permute-start.5 = (f32[64,128]{1,0:T(8,128)S(1)}, f32[64,128]{1,0:T(8,128)S(1)}, u32[]{:S(2)}, u32[]{:S(2)}) collective-permute-start(f32[64,128]{1,0:T(8,128)S(1)} %get-tuple-element.20), channel_id=1, source_target_pairs={{0,112},{16,0},{32,16},{48,32},{64,48},{80,64},{96,80},{112,96},{1... | collective-permute-start | bytes 98312 | tf_op jit(solution)/shard_map/ppermute | solution.py:423
  51.4 8.1 %collective-permute-done.5.ya_ref = f32[64,128]{1,0:T(8,128)S(1)} collective-permute-done((f32[64,128]{1,0:T(8,128)S(1)}, f32[64,128]{1,0:T(8,128)S(1)}, u32[]{:S(2)}, u32[]{:S(2)}) %collective-permute-start.5) | collective-permute-done | bytes 32800 | tf_op jit(solution)/shard_map/ppermute | solution.py:423
  59.6 0.5 diffusion.1
  60.3 0.1 copy.62
  60.4 0.6 copy.63
  61.0 3.8 %all-to-all-start.1 = ((f32[4,16,4]{0,2,1:T(4,128)}), f32[4,16,4]{0,2,1:T(4,128)S(1)}, u32[]{:S(2)}, u32[]{:S(2)}) async-start(f32[4,16,4]{0,2,1:T(4,128)} %copy.63), calls=%async_computation.1 | async-start | bytes 65536 | tf_op jit(solution)/shard_map/all_to_all | solution.py:441
  64.9 0.1 compare_select_fusion.sub_ref
  65.0 46.4 %pair_forces.1 = f32[3,2,8,2,128]{4,3,2,1,0:T(2,128)} custom-call(f32[7,8,6,128]{3,2,1,0:T(8,128)S(1)} %get-tuple-element.16.own_ref, f32[144,128]{1,0:T(8,128)S(1)} %collective-permute-done.2.xb_ref, f32[144,128]{1,0:T(8,128)S(1)} %collective-permute-done.3.xa_ref, f32[64,128]{1,0:T(8,128)S(1)} %collective-permute-done.4.yb_ref, ...), custom_call_target="tpu_custom_call" | custom-call | tf_op jit(solution)/shard_map/pair_forces/pallas_call | solution.py:255
  111.4 0.7 copy.65
  (24 shorter events, 0.5 us)
Async XLA Ops:
  1.4 0.8 copy-start
  2.2 0.7 copy-start.4
  2.9 0.8 copy-start.6
  4.6 11.5 %copy-start.7 = (f32[4,1,64]{2,1,0:T(1,128)S(1)}, f32[4,1,64]{2,1,0:T(1,128)}, u32[]{:S(2)}) copy-start(f32[4,1,64]{2,1,0:T(1,128)} %param.11) | copy-start | bytes 3076
  4.6 23.6 %collective-permute-start = (f32[64,128]{1,0:T(8,128)S(1)}, f32[64,128]{1,0:T(8,128)S(1)}, u32[]{:S(2)}, u32[]{:S(2)}) collective-permute-start(f32[64,128]{1,0:T(8,128)S(1)} %get-tuple-element.14), channel_id=1, source_target_pairs={{0,1},{1,2},{2,3},{3,4},{4,5},{5,6},{6,7},{7,8},{8,9},{9,10},{10,1... | collective-permute-start | bytes 98312 | tf_op jit(solution)/shard_map/ppermute | solution.py:423
  9.0 19.3 %collective-permute-start.1 = (f32[64,128]{1,0:T(8,128)S(1)}, f32[64,128]{1,0:T(8,128)S(1)}, u32[]{:S(2)}, u32[]{:S(2)}) collective-permute-start(f32[64,128]{1,0:T(8,128)S(1)} %get-tuple-element.15), channel_id=1, source_target_pairs={{0,15},{1,0},{2,1},{3,2},{4,3},{5,4},{6,5},{7,6},{8,7},{9,8},{10,9... | collective-permute-start | bytes 98312 | tf_op jit(solution)/shard_map/ppermute | solution.py:423
  28.4 6.5 %collective-permute-start.2 = (f32[144,128]{1,0:T(8,128)S(1)}, f32[144,128]{1,0:T(8,128)S(1)}, u32[]{:S(2)}, u32[]{:S(2)}) collective-permute-start(f32[144,128]{1,0:T(8,128)S(1)} %get-tuple-element.17), channel_id=1, source_target_pairs={{0,128},{128,256},{256,384},{384,0},{1,129},{129,257},{257,385},{3... | collective-permute-start | bytes 221192 | tf_op jit(solution)/shard_map/ppermute | solution.py:423
  31.5 5.1 %collective-permute-start.3 = (f32[144,128]{1,0:T(8,128)S(1)}, f32[144,128]{1,0:T(8,128)S(1)}, u32[]{:S(2)}, u32[]{:S(2)}) collective-permute-start(f32[144,128]{1,0:T(8,128)S(1)} %get-tuple-element.18), channel_id=1, source_target_pairs={{0,384},{128,0},{256,128},{384,256},{1,385},{129,1},{257,129},{385... | collective-permute-start | bytes 221192 | tf_op jit(solution)/shard_map/ppermute | solution.py:423
  36.7 14.7 %collective-permute-start.4 = (f32[64,128]{1,0:T(8,128)S(1)}, f32[64,128]{1,0:T(8,128)S(1)}, u32[]{:S(2)}, u32[]{:S(2)}) collective-permute-start(f32[64,128]{1,0:T(8,128)S(1)} %get-tuple-element.19), channel_id=1, source_target_pairs={{0,16},{16,32},{32,48},{48,64},{64,80},{80,96},{96,112},{112,0},{1... | collective-permute-start | bytes 98312 | tf_op jit(solution)/shard_map/ppermute | solution.py:423
  49.5 10.1 %collective-permute-start.5 = (f32[64,128]{1,0:T(8,128)S(1)}, f32[64,128]{1,0:T(8,128)S(1)}, u32[]{:S(2)}, u32[]{:S(2)}) collective-permute-start(f32[64,128]{1,0:T(8,128)S(1)} %get-tuple-element.20), channel_id=1, source_target_pairs={{0,112},{16,0},{32,16},{48,32},{64,48},{80,64},{96,80},{112,96},{1... | collective-permute-start | bytes 98312 | tf_op jit(solution)/shard_map/ppermute | solution.py:423
  59.6 5.4 %copy-start.3 = (f32[27,8,128]{2,1,0:T(8,128)S(1)}, f32[27,8,128]{2,1,0:T(8,128)}, u32[]{:S(2)}) copy-start(f32[27,8,128]{2,1,0:T(8,128)} %constant.9.clone.m_ref) | copy-start | bytes 331780
  60.3 4.7 %copy-start.2 = (f32[27,8,128]{2,1,0:T(8,128)S(1)}, f32[27,8,128]{2,1,0:T(8,128)}, u32[]{:S(2)}) copy-start(f32[27,8,128]{2,1,0:T(8,128)} %constant.10.clone.k_ref) | copy-start | bytes 331780
  61.0 3.8 %copy-start.5 = (s32[2,8,2,128]{3,2,1,0:T(2,128)S(1)}, s32[2,8,2,128]{3,2,1,0:T(2,128)}, u32[]{:S(2)}) copy-start(s32[2,8,2,128]{3,2,1,0:T(2,128)} %grid_ref.1) | copy-start | bytes 49156
  61.0 3.9 %copy-start.1 = (f32[3,2,8,2,128]{4,3,2,1,0:T(2,128)S(1)}, f32[3,2,8,2,128]{4,3,2,1,0:T(2,128)}, u32[]{:S(2)}) copy-start(f32[3,2,8,2,128]{4,3,2,1,0:T(2,128)} %vel_ref.3) | copy-start | bytes 147460
  61.0 50.4 %all-to-all-start.1 = ((f32[4,16,4]{0,2,1:T(4,128)}), f32[4,16,4]{0,2,1:T(4,128)S(1)}, u32[]{:S(2)}, u32[]{:S(2)}) async-start(f32[4,16,4]{0,2,1:T(4,128)} %copy.63), calls=%async_computation.1 | async-start | bytes 65536 | tf_op jit(solution)/shard_map/all_to_all | solution.py:441
